TPU v7x, 512 devices: a whole 4x8x8 slice. The times are simulated.
512 devices in a mesh: bus: 8 (over y), line: 8 (over x, core), scen: 8 (over z).
Axes of the slice: x: 4, y: 8, z: 8, core: 2. Of those that a mesh axis runs over, the one named last changes fastest.
Arguments:
- shift_factors: bfloat16 [12288, 8192], P('line', 'bus'), may hold values from -0.0625 to 0.0625
- net_load: bfloat16 [512, 8, 8192], P('scen', None, 'bus'), may hold values from -6 to 6
- dispatch_level: float32 [512, 8], P('scen'), may hold values from 0.3 to 1.5
- scenario_weight: float32 [512], P('scen'), may hold values from 0.5 to 2
- cluster_id: int32 [512, 1], P('scen'), may hold values from 0 to 63
- commitment: int32 [8, 4096], P(None, 'bus'), may hold values 0 or 1
- unit_capacity: float32 [4096], P('bus'), may hold values from 0.5 to 4
- unit_bus: int32 [4096], P('bus'), may hold values from 0 to 8191
- line_limit: float32 [12288], P('line'), may hold values from 0.3 to 1.5
- multipliers: float32 [64, 12288], P('scen', 'line'), may hold values from 0 to 1
- penalty_target: float32 [64], P('scen'), may hold values from 1 to 16
Outputs:
- new_multipliers: float32 [64, 12288], P('scen', 'line')
- cut_slopes: float32 [64, 8, 8192], P(('line', 'scen'), None, 'bus')
All inputs are finite; a program needn't handle non-finite values. No bound on the sum of `commitment` on one device may be relied on, other than what follows from the above.
Results may differ from a plain program's by a relative error of at most 0.0011.
Values may be sent and summed in bfloat16 or wider, within the bound.
No kernel may reach another device: no remote copies, remote signals or barrier semaphores. Data moves between devices by JAX's collectives and lax.ppermute only.
A program may use at most 64 MiB of HBM per device.

v0:
```python
import jax
import jax.numpy as jnp
from jax import lax
from jax.sharding import PartitionSpec as P

BUSES = 8192
CLUSTERS = 64


step_size = 0.1


def cut_along(shard, dim, devices):
    lengths = shard.shape
    tiles = shard.reshape(*lengths[:dim], devices, lengths[dim] // devices, *lengths[dim + 1 :])
    return jnp.moveaxis(tiles, dim, 0)


def sum_at_owner(shard, axis, dim):
    devices = lax.axis_size(axis)
    tiles = lax.all_to_all(cut_along(shard, dim, devices), axis, 0, 0, tiled=True)
    return jnp.sum(tiles, axis=0)


def joined_along(tiles, dim):
    tiles = jnp.moveaxis(tiles, 0, dim)
    lengths = tiles.shape
    return tiles.reshape(*lengths[:dim], lengths[dim] * lengths[dim + 1], *lengths[dim + 2 :])


def sent_to_all(shard, axis):
    devices = lax.axis_size(axis)
    return lax.all_to_all(
        jnp.broadcast_to(shard[None], (devices, *shard.shape)), axis, 0, 0, tiled=True
    )


def gathered_copies(shard, axis, dim):
    return joined_along(sent_to_all(shard, axis), dim)


def per_device(
    shift_factors,
    net_load,
    dispatch_level,
    scenario_weight,
    cluster_id,
    commitment,
    unit_capacity,
    unit_bus,
    line_limit,
    multipliers,
    penalty_target,
):
    highest = lax.Precision.HIGHEST
    line_count, bus_count = shift_factors.shape
    scen_count, hour_count, _ = net_load.shape
    column_count = scen_count * hour_count
    values = commitment.astype(jnp.float32) * unit_capacity[None, :]
    spread = jax.ops.segment_sum(values.T, unit_bus, num_segments=BUSES).T
    capacity = sum_at_owner(spread, "bus", 1)
    injection = (
        capacity[None, :, :] * dispatch_level[:, :, None] - net_load.astype(jnp.float32)
    ).astype(jnp.bfloat16)
    injection = injection.reshape(column_count, bus_count)
    member = (cluster_id == jnp.arange(CLUSTERS, dtype=jnp.int32)[None, :]).astype(jnp.float32)
    share = line_count // lax.axis_size("bus")
    block = shift_factors
    flow = lax.psum_scatter(
        lax.dot_general(
            block, injection, (((1,), (1,)), ((), ())), preferred_element_type=jnp.float32
        ),
        "bus",
        scatter_dimension=0,
        tiled=True,
    )
    first_line = lax.axis_index("bus") * share
    bounds = lax.dynamic_slice_in_dim(line_limit, first_line, share, 0)
    flow_cube = flow.reshape(flow.shape[0], scen_count, hour_count)
    edges = bounds[:, None, None]
    excess = flow_cube - jnp.clip(flow_cube, -edges, edges)
    current = lax.dynamic_slice_in_dim(multipliers, first_line, share, 1)
    penalty = 0.5 * jnp.sum(excess * excess, axis=2) * scenario_weight[None, :]
    pooled = sum_at_owner(jnp.dot(member.T, penalty.T, precision=highest), "scen", 0)
    owned = jnp.maximum(current + step_size * (pooled - penalty_target[:, None]), 0.0)
    every_dual = gathered_copies(owned, "scen", 0)
    owned, every_dual = (owned, every_dual)
    chosen = jnp.dot(member, every_dual, precision=highest)
    factor = (chosen.T * scenario_weight[None, :])[:, :, None]
    push = (excess * factor).astype(jnp.bfloat16).reshape(excess.shape[0], column_count)
    block = shift_factors
    sensitivity = lax.dot_general(
        gathered_copies(push, "bus", 0),
        block,
        (((0,), (0,)), ((), ())),
        preferred_element_type=jnp.float32,
    )
    dual_out = gathered_copies(owned, "bus", 1)
    scaled = (
        sensitivity.reshape(scen_count, hour_count, bus_count) * dispatch_level[:, :, None]
    ).reshape(scen_count, hour_count * bus_count)
    member_rows = member.T
    owner_count = CLUSTERS // (lax.axis_size("line") * lax.axis_size("scen"))
    slopes = sum_at_owner(jnp.dot(member_rows, scaled, precision=highest), ("line", "scen"), 0)
    return (dual_out, slopes.reshape(owner_count, hour_count, bus_count))


def solution(mesh):
    placed = (
        P("line", "bus"),
        P("scen", None, "bus"),
        P("scen", None),
        P("scen"),
        P("scen", None),
        P(None, "bus"),
        P("bus"),
        P("bus"),
        P("line"),
        P("scen", "line"),
        P("scen"),
    )
    return jax.shard_map(
        per_device,
        mesh=mesh,
        in_specs=placed,
        out_specs=(P("scen", "line"), P(("line", "scen"), None, "bus")),
        check_vma=False,
    )
```

profile of v0, /device:TPU:1, one launch (start us, length us, event | category | flops | bytes accessed | tf_op | source)
XLA Modules:
  0.0 251.9 jit_solution(4947499021366355676)
XLA Ops:
  7.2 0.0 copy-start
  7.2 0.9 multiply_bitcast_fusion
  8.1 0.1 copy.24
  8.2 4.5 %scatter_custom_fusion = f32[8192,8]{1,0:T(8,128)} fusion(s32[512]{0:T(512)} %param.18, f32[512,8]{1,0:T(8,128)S(1)} %copy.24, f32[]{:T(128)} %constant.5.clone.1), kind=kCustom, calls=%fused_computation.6 | custom fusion | flops 4096 | bytes 262656 | tf_op jit(solution)/shard_map/scatter-add | solution.py:60
  12.7 0.0 copy-start.2
  12.7 3.4 %copy.25 = f32[8,8,1024]{2,0,1:T(8,128)} copy(f32[8,8,1024]{0,2,1:T(8,128)} %bitcast.51) | data formatting | bytes 524288 | tf_op jit(solution)/shard_map/reshape | solution.py:15
  16.2 7.6 %all-to-all-start = ((f32[8,8,1024]{2,1,0:T(8,128)}), f32[8,8,1024]{2,1,0:T(8,128)S(1)}, u32[]{:S(2)}, u32[]{:S(2)}) async-start(f32[8,8,1024]{2,1,0:T(8,128)} %bitcast.4), calls=%async_computation | async-start | bytes 524288 | tf_op jit(solution)/shard_map/all_to_all | solution.py:21
  23.8 0.0 reduce-scatter.4.cloned.1.call-start
  23.8 0.0 copy-done.2
  23.8 0.1 copy.28
  23.9 9.3 %all-to-all-done = f32[8,8,1024]{2,1,0:T(8,128)S(1)} async-done(((f32[8,8,1024]{2,1,0:T(8,128)}), f32[8,8,1024]{2,1,0:T(8,128)S(1)}, u32[]{:S(2)}, u32[]{:S(2)}) %all-to-all-start) | async-done | bytes 262176 | tf_op jit(solution)/shard_map/all_to_all | solution.py:21
  33.3 0.0 copy-done
  33.3 4.8 %convolution_bitcast_fusion.1 = f32[1536,512]{0,1:T(8,128)} fusion(bf16[1536,1024]{1,0:T(8,128)(2,1)S(1)} %copy-done, bf16[64,8,1024]{2,1,0:T(8,128)(2,1)} %param.12, f32[64,8]{1,0:T(8,128)S(1)} %copy.28, f32[8,1024]{1,0:T(8,128)S(1)} %reduce_sum.36), kind=kOutput, calls=%fused_computation.2 | convolution fusion | flops 1612709888 | bytes 7374848 | tf_op jit(solution)/shard_map/dot_general | solution.py:70
  38.1 3.5 %copy.33 = f32[1536,512]{1,0:T(8,128)} copy(f32[1536,512]{0,1:T(8,128)} %convolution_bitcast_fusion.1) | data formatting | bytes 6291456
  41.7 0.0 copy-start.3
  41.7 0.0 copy-start.1
  41.7 0.0 copy-start.4
  41.7 0.0 reduce-scatter.4.cloned.1.call-update
  41.7 0.8 fusion.22
  42.5 0.0 copy-done.3
  42.5 47.7 %reduce-scatter.4.cloned.1.call-done = f32[192,512]{1,0:T(8,128)} async-done(((f32[1536,512]{1,0:T(8,128)}), f32[192,512]{1,0:T(8,128)}) %reduce-scatter.4.cloned.1.call-update) | async-done | bytes 393232
  90.2 2.0 copy.34
  92.2 1.2 fusion.15
  93.4 0.0 copy-done.1
  93.4 0.3 convolution_bitcast_fusion.2
  93.7 14.1 %all_to_all.30 = f32[8,8,192]{2,1,0:T(8,128)S(1)} all-to-all(f32[8,8,192]{2,1,0:T(8,128)S(1)} %convolution_bitcast_fusion.2), channel_id=1, replica_groups=mesh['bus'=8,'line'=8,'scen'=8] {'scen'}, dimensions={0} | all-to-all | bytes 98304 | tf_op jit(solution)/shard_map/all_to_all | solution.py:21
  107.8 0.0 copy-done.4
  107.8 0.8 add_maximum_fusion
  108.6 0.6 broadcast_in_dim.10
  109.2 10.5 %all_to_all.31 = f32[8,8,192]{2,1,0:T(8,128)S(1)} all-to-all(f32[8,8,192]{2,1,0:T(8,128)} %broadcast_in_dim.10), channel_id=1, replica_groups=mesh['bus'=8,'line'=8,'scen'=8] {'scen'}, dimensions={0} | all-to-all | bytes 98304 | tf_op jit(solution)/shard_map/all_to_all | solution.py:33
  119.7 0.2 convolution_multiply_fusion
  119.9 1.1 fusion.12
  121.0 0.8 copy.30
  121.8 1.1 broadcast_in_dim.11
  122.9 38.0 %all_to_all.32 = bf16[8,192,512]{2,1,0:T(8,128)(2,1)} all-to-all(bf16[8,192,512]{2,1,0:T(8,128)(2,1)S(1)} %broadcast_in_dim.11), channel_id=1, replica_groups=mesh['bus'=8,'line'=8,'scen'=8] {'bus'}, dimensions={0} | all-to-all | bytes 3145728 | tf_op jit(solution)/shard_map/all_to_all | solution.py:33
  160.9 3.5 %all-to-all-start.2 = ((f32[8,8,192]{2,1,0:T(8,128)}), f32[8,8,192]{2,1,0:T(8,128)S(1)}, u32[]{:S(2)}, u32[]{:S(2)}) async-start(f32[8,8,192]{2,1,0:T(8,128)} %broadcast_in_dim.10), calls=%async_computation.2 | async-start | bytes 131072 | tf_op jit(solution)/shard_map/all_to_all | solution.py:33
  164.5 2.6 %copy.31 = bf16[512,1536]{1,0:T(8,128)(2,1)} copy(bf16[512,1536]{0,1:T(8,128)(2,1)} %bitcast.53) | data formatting | bytes 3145728 | tf_op jit(solution)/shard_map/dot_general | solution.py:92
  167.1 3.2 %fusion.4 = f32[64,8,1024]{2,1,0:T(8,128)S(1)} fusion(bf16[1536,1024]{1,0:T(8,128)(2,1)S(1)} %copy-done, bf16[512,1536]{1,0:T(8,128)(2,1)} %copy.31, f32[64,8]{1,0:T(8,128)S(1)} %copy.28), kind=kOutput, calls=%fused_computation.8 | convolution fusion | flops 1611137024 | bytes 6817792 | tf_op jit(solution)/shard_map/dot_general | solution.py:92
  170.3 1.3 copy.36
  171.5 1.2 convolution_bitcast_fusion
  172.7 3.5 %copy.32 = f32[64,1,8192]{2,1,0:T(1,128)} copy(f32[64,1,8192]{2,0,1:T(8,128)S(1)} %convolution_bitcast_fusion) | data formatting | bytes 4194304 | tf_op jit(solution)/shard_map/reshape | solution.py:15
  176.2 0.0 all-to-all-done.2
  176.2 13.0 %all-to-all-start.5 = ((f32[64,1,8192]{2,1,0:T(1,128)}), f32[64,1,8192]{2,1,0:T(1,128)}, u32[]{:S(2)}, u32[]{:S(2)}) async-start(f32[64,1,8192]{2,1,0:T(1,128)} %copy.32), calls=%async_computation.5 | async-start | bytes 4194304 | tf_op jit(solution)/shard_map/all_to_all | solution.py:21
  189.3 0.7 reshape.63
  190.0 51.0 %all-to-all-done.5 = f32[64,1,8192]{2,1,0:T(1,128)} async-done(((f32[64,1,8192]{2,1,0:T(1,128)}), f32[64,1,8192]{2,1,0:T(1,128)}, u32[]{:S(2)}, u32[]{:S(2)}) %all-to-all-start.5) | async-done | bytes 2097184 | tf_op jit(solution)/shard_map/all_to_all | solution.py:21
  241.0 3.4 %reduce_sum.39 = f32[8192]{0:T(1024)S(1)} reduce(f32[64,1,8192]{2,1,0:T(1,128)} %all-to-all-done.5, f32[]{:T(128)} %constant.5.clone.1), dimensions={0,1}, to_apply=%region_5.6 | reduce | flops 516096 | bytes 2129924 | tf_op jit(solution)/shard_map/reduce_sum | solution.py:22
  244.4 0.6 reshape.68
  (4 shorter events, 0.1 us)
Async XLA Ops:
  7.2 26.1 %copy-start = (bf16[1536,1024]{1,0:T(8,128)(2,1)S(1)}, bf16[1536,1024]{1,0:T(8,128)(2,1)}, u32[]{:S(2)}) copy-start(bf16[1536,1024]{1,0:T(8,128)(2,1)} %param.11) | copy-start | bytes 9437188
  12.7 11.1 %copy-start.2 = (f32[64,8]{0,1:T(8,128)S(1)}, f32[64,8]{0,1:T(8,128)}, u32[]{:S(2)}) copy-start(f32[64,8]{0,1:T(8,128)} %param.13) | copy-start | bytes 6148
  16.2 17.1 %all-to-all-start = ((f32[8,8,1024]{2,1,0:T(8,128)}), f32[8,8,1024]{2,1,0:T(8,128)S(1)}, u32[]{:S(2)}, u32[]{:S(2)}) async-start(f32[8,8,1024]{2,1,0:T(8,128)} %bitcast.4), calls=%async_computation | async-start | bytes 524288 | tf_op jit(solution)/shard_map/all_to_all | solution.py:21
  23.8 66.4 %reduce-scatter.4.cloned.1.call-start = ((), (), s32[]{:S(2)}) async-start(), calls=%async_computation.7 | async-start | bytes 3538944
  41.7 0.8 copy-start.3
  41.7 51.7 %copy-start.1 = (s32[64,1]{0,1:T(1,128)S(1)}, s32[64,1]{0,1:T(1,128)}, u32[]{:S(2)}) copy-start(s32[64,1]{0,1:T(1,128)} %param.15) | copy-start | bytes 772
  41.7 66.1 %copy-start.4 = (f32[8]{0:T(128)S(1)}, f32[8]{0:T(128)}, u32[]{:S(2)}) copy-start(f32[8]{0:T(128)} %param.21) | copy-start | bytes 100
  160.9 15.3 %all-to-all-start.2 = ((f32[8,8,192]{2,1,0:T(8,128)}), f32[8,8,192]{2,1,0:T(8,128)S(1)}, u32[]{:S(2)}, u32[]{:S(2)}) async-start(f32[8,8,192]{2,1,0:T(8,128)} %broadcast_in_dim.10), calls=%async_computation.2 | async-start | bytes 131072 | tf_op jit(solution)/shard_map/all_to_all | solution.py:33
  176.2 64.8 %all-to-all-start.5 = ((f32[64,1,8192]{2,1,0:T(1,128)}), f32[64,1,8192]{2,1,0:T(1,128)}, u32[]{:S(2)}, u32[]{:S(2)}) async-start(f32[64,1,8192]{2,1,0:T(1,128)} %copy.32), calls=%async_computation.5 | async-start | bytes 4194304 | tf_op jit(solution)/shard_map/all_to_all | solution.py:21
Sparse Core Ops, SparseCore 0:
  41.8 48.3 reduce-scatter.3
where the time goes:
time: 253 us; the launch traced here: 252 us
  waiting for transfers between devices  108 us (43%)
  blocking collectives  62.5 us (25%)
  starting transfers between devices  24.3 us (10%)
  local copies, waits for them, and re-layouts  20.4 us (8%)
  between operations  14.2 us (6%)
  other arithmetic  12.7 us (5%)
  matrix products  9.74 us (4%)
    all_to_all x2, waiting for transfers between devices, sum_at_owner(): lax.all_to_all(cut_along(shard, dim, devices), axis, 0, 0, tiled=True)  60.3 us
    all_to_all x2, blocking collectives, sent_to_all(): lax.all_to_all(jnp.broadcast_to(shard[None], (devices, *shard.shape)), ax...  48.5 us
    unnamed x2, waiting for transfers between devices  47.7 us
    all_to_all x2, starting transfers between devices, sum_at_owner(): lax.all_to_all(cut_along(shard, dim, devices), axis, 0, 0, tiled=True)  20.7 us
    all_to_all x1, blocking collectives, sum_at_owner(): lax.all_to_all(cut_along(shard, dim, devices), axis, 0, 0, tiled=True)  14.1 us
    reshape x2, local copies, waits for them, and re-layouts, cut_along(): shard.reshape(*lengths[:dim], devices, lengths[dim] // devices, *lengths[...  6.97 us
    unnamed x14, local copies, waits for them, and re-layouts  6.9 us
  transfers between devices with their start and end apart: 4, of which 3 were waited for; matrix products, arithmetic and copies ran while one was open for 5% of the time, Pallas kernels for 0%

commit v1 on v0

v1 whole, which is shorter than its diff:
```python
import jax
import jax.numpy as jnp
from jax import lax
from jax.experimental import pallas as pl
from jax.experimental.pallas import tpu as pltpu
from jax.sharding import PartitionSpec as P


BUS_AXIS = 8
LINE_AXIS = 8
SCEN_AXIS = 8
LINES = 1536
SHARE = LINES // BUS_AXIS
BUSES = 1024
SCEN = 64
HOURS = 8
COLS = SCEN * HOURS
UNITS = 4096
OWNED = 8
ROWS = OWNED * HOURS
STEP = 0.1
CODE = 32000.0
VMEM = 56 * 1024 * 1024

F32 = jnp.float32
BF16 = jnp.bfloat16


def dot_nt(a, b):
    return lax.dot_general(a, b, (((1,), (1,)), ((), ())), preferred_element_type=F32)


def dot_nn(a, b):
    return lax.dot_general(a, b, (((1,), (0,)), ((), ())), preferred_element_type=F32)


def split2(x):
    high = x.astype(BF16)
    return high, (x - high.astype(F32)).astype(BF16)


def split3(x):
    high = x.astype(BF16)
    rest = x - high.astype(F32)
    mid = rest.astype(BF16)
    return high, mid, (rest - mid.astype(F32)).astype(BF16)


def net_flow_kernel(factors, load, net):
    net[...] = dot_nt(factors[...], load[...])


def net_flow(factors, load):
    return pl.pallas_call(
        net_flow_kernel,
        grid=(4,),
        in_specs=[
            pl.BlockSpec((LINES // 4, BUSES), lambda j: (j, 0)),
            pl.BlockSpec((COLS, BUSES), lambda j: (0, 0)),
        ],
        out_specs=pl.BlockSpec((LINES // 4, COLS), lambda j: (j, 0)),
        out_shape=jax.ShapeDtypeStruct((LINES, COLS), F32),
        compiler_params=pltpu.CompilerParams(vmem_limit_bytes=VMEM),
        name="net_flow",
    )(factors, load)


def hour_places():
    column = lax.broadcasted_iota(jnp.int32, (HOURS, COLS), 1)
    row = lax.broadcasted_iota(jnp.int32, (HOURS, COLS), 0)
    return (jnp.bitwise_and(column, HOURS - 1) == row).astype(F32).astype(BF16)


def flow_kernel(first, units, factors, net, level, coded, work, capacity):
    @pl.when(pl.program_id(0) == 0)
    def _():
        local = units[:, 8, :] - first[0].astype(F32)
        high = jnp.floor(local * (1.0 / 128.0))
        low = local - high * 128.0
        for src in range(BUS_AXIS):
            values = units[src, 0:8, :]
            row_high = high[src : src + 1, :]
            for block in range(8):
                work[block * 8 : block * 8 + 8, src * 512 : src * 512 + 512] = jnp.where(
                    row_high == float(block), values, 0.0
                )
        lows = lax.broadcasted_iota(jnp.int32, (128, 512), 0).astype(F32)
        total = jnp.zeros((192, 128), F32)
        for src in range(BUS_AXIS):
            match = jnp.where(lows == low[src : src + 1, :], 1.0, 0.0).astype(BF16)
            pieces = jnp.concatenate(split3(work[:, src * 512 : src * 512 + 512]), axis=0)
            total = total + dot_nt(pieces, match)
        total = total[0:64] + total[64:128] + total[128:192]
        for block in range(8):
            parts = split3(total[8 * block : 8 * block + 8])
            for index in range(3):
                capacity[8 * index : 8 * index + 8, 128 * block : 128 * block + 128] = parts[index].astype(F32)

    block = factors[...]
    given = dot_nt(block, capacity[...].astype(BF16))
    place = hour_places()
    place = jnp.concatenate([place, place, place], axis=0)
    g0, g1, g2 = split3(given)
    fixed = dot_nn(g0, place) + dot_nn(g1, place) + dot_nn(g2, place)
    part = fixed * level[0:1, :] - net[...]
    top = jnp.maximum(jnp.max(jnp.abs(part), axis=1, keepdims=True), 1e-30)
    power = jnp.ceil(jnp.log2(top) * 8.0)
    unit = jnp.exp2(power * -0.125) * CODE
    coded[0, 0:SHARE, :] = jnp.round(part * unit).astype(jnp.int32).astype(jnp.int16)
    across = jnp.transpose(jnp.broadcast_to(power, (SHARE, 128)))[0:8]
    across = jnp.concatenate([across, jnp.zeros((8, COLS - SHARE), F32)], axis=1)
    coded[0, SHARE : SHARE + 8, :] = across.astype(jnp.int32).astype(jnp.int16)


def coded_flow(first, units, factors, net, level):
    return pl.pallas_call(
        flow_kernel,
        grid=(BUS_AXIS,),
        in_specs=[
            pl.BlockSpec(memory_space=pltpu.SMEM),
            pl.BlockSpec(memory_space=pltpu.VMEM),
            pl.BlockSpec((SHARE, BUSES), lambda j: (j, 0)),
            pl.BlockSpec((SHARE, COLS), lambda j: (j, 0)),
            pl.BlockSpec((3, COLS), lambda j: (0, 0)),
        ],
        out_specs=pl.BlockSpec((1, SHARE + 8, COLS), lambda j: (j, 0, 0)),
        out_shape=jax.ShapeDtypeStruct((BUS_AXIS, SHARE + 8, COLS), jnp.int16),
        scratch_shapes=[pltpu.VMEM((64, UNITS), F32), pltpu.VMEM((24, BUSES), F32)],
        compiler_params=pltpu.CompilerParams(vmem_limit_bytes=VMEM),
        name="coded_flow",
    )(first, near(units), factors, net, level)


def excess_kernel(coded, limit, rows, out):
    level = rows[0:1, :]
    weight = rows[1:2, :]
    cluster = rows[2:3, :]
    column = lax.broadcasted_iota(jnp.int32, (1, COLS), 1)
    hour = jnp.bitwise_and(column, HOURS - 1)
    power = [coded[src, SHARE : SHARE + 8, 0:SHARE].astype(jnp.int32).astype(F32)[0:1] for src in range(BUS_AXIS)]
    unit = jnp.exp2(jnp.transpose(jnp.concatenate(power, axis=0)) * 0.125) * (1.0 / CODE)
    flow = coded[0, 0:SHARE, :].astype(jnp.int32).astype(F32) * unit[:, 0:1]
    for src in range(1, BUS_AXIS):
        flow = flow + coded[src, 0:SHARE, :].astype(jnp.int32).astype(F32) * unit[:, src : src + 1]
    edge = limit[:, 0:1]
    excess = flow - jnp.clip(flow, -edge, edge)
    p0, p1 = split2(excess * (level * weight))
    e0, e1 = split2(excess * excess * (0.5 * weight))
    key = cluster * float(HOURS) + hour.astype(F32)
    for dest in range(SCEN_AXIS):
        row = lax.broadcasted_iota(jnp.int32, (ROWS, COLS), 0)
        mine = ((row // HOURS) * SCEN_AXIS + dest) * HOURS + jnp.bitwise_and(row, HOURS - 1)
        pick = jnp.where(mine.astype(F32) == key, 1.0, 0.0).astype(BF16)
        pushed = dot_nt(pick, p0) + dot_nt(pick, p1)
        row = lax.broadcasted_iota(jnp.int32, (16, COLS), 0)
        mine = jnp.where(row < 8, row * SCEN_AXIS + dest, dest * OWNED + row - 8)
        pick = jnp.where(mine.astype(F32) == cluster, 1.0, 0.0).astype(BF16)
        pooled = dot_nt(pick, e0) + dot_nt(pick, e1)
        both = jnp.concatenate([pushed, pooled], axis=0)
        out[dest, 0:80, :] = both[:, 0:128]
        out[dest, 80:120, :] = jnp.concatenate([both[0:40, 128:192], both[40:80, 128:192]], axis=1)


def excess_sums(coded, limit, rows):
    return pl.pallas_call(
        excess_kernel,
        in_specs=[pl.BlockSpec(memory_space=pltpu.VMEM)] * 3,
        out_specs=pl.BlockSpec(memory_space=pltpu.VMEM),
        out_shape=jax.ShapeDtypeStruct((SCEN_AXIS, 120, 128), F32),
        compiler_params=pltpu.CompilerParams(vmem_limit_bytes=VMEM),
        name="excess_sums",
    )(near(coded), near(limit), near(rows))


def update_kernel(mine, sums, gathered, current, target, out):
    total = sums[0]
    for src in range(1, SCEN_AXIS):
        total = total + sums[src]
    spread = jnp.concatenate(
        [gathered[pl.ds(8 * i + mine[0], 1), :] for i in range(OWNED)], axis=0
    )
    tail = jnp.concatenate([total[80:120, 0:64], total[80:120, 64:128]], axis=0)
    for part, lo, hi in ((total[0:80], 0, 128), (tail, 128, 192)):
        chosen = jnp.maximum(
            spread[:, lo:hi] + STEP * (part[64:72] - spread[:, SHARE : SHARE + 1]), 0.0
        )
        owned = jnp.maximum(current[:, lo:hi] + STEP * (part[72:80] - target[:, 0:1]), 0.0)
        wide = jnp.concatenate(
            [part[8 * i : 8 * i + 8] * chosen[i : i + 1] for i in range(OWNED)] + [owned], axis=0
        )
        if lo == 0:
            for dest in range(BUS_AXIS):
                out[dest, 0:72, :] = wide
        else:
            folded = jnp.concatenate([wide[0:40], jnp.concatenate([wide[40:72], wide[64:72]], axis=0)], axis=1)
            for dest in range(BUS_AXIS):
                out[dest, 72:112, :] = folded


def updated(mine, sums, gathered, current, target):
    return pl.pallas_call(
        update_kernel,
        in_specs=[pl.BlockSpec(memory_space=pltpu.SMEM)] + [pl.BlockSpec(memory_space=pltpu.VMEM)] * 4,
        out_specs=pl.BlockSpec(memory_space=pltpu.VMEM),
        out_shape=jax.ShapeDtypeStruct((BUS_AXIS, 112, 128), F32),
        compiler_params=pltpu.CompilerParams(vmem_limit_bytes=VMEM),
        name="update",
    )(mine, near(sums), near(gathered), near(current), near(target))


def slopes_kernel(packed, factors, slopes, duals):
    step = pl.program_id(0)
    head = packed[0, 0:72, :]
    tail = packed[0, 72:112, :]
    tail = jnp.concatenate([tail[:, 0:64], tail[0:32, 64:128]], axis=0)
    wide = jnp.concatenate([head, tail], axis=1)
    duals[0] = wide[64:72]
    high, low = split2(wide[0:64])
    both = dot_nn(jnp.concatenate([high, low], axis=0), factors[...])
    part = both[0:64] + both[64:128]

    @pl.when(step == 0)
    def _():
        slopes[...] = part

    @pl.when(step > 0)
    def _():
        slopes[...] = slopes[...] + part


def slopes_of(packed, factors):
    return pl.pallas_call(
        slopes_kernel,
        grid=(BUS_AXIS,),
        in_specs=[
            pl.BlockSpec((1, 112, 128), lambda j: (j, 0, 0)),
            pl.BlockSpec((SHARE, BUSES), lambda j: (j, 0)),
        ],
        out_specs=[
            pl.BlockSpec((ROWS, BUSES), lambda j: (0, 0)),
            pl.BlockSpec((1, 8, SHARE), lambda j: (j, 0, 0)),
        ],
        out_shape=[
            jax.ShapeDtypeStruct((ROWS, BUSES), F32),
            jax.ShapeDtypeStruct((BUS_AXIS, 8, SHARE), F32),
        ],
        compiler_params=pltpu.CompilerParams(vmem_limit_bytes=VMEM),
        name="slopes",
    )(packed, factors)


def exchange(tiles, axis):
    return lax.all_to_all(tiles, axis, 0, 0, tiled=True)


def near(x):
    return pltpu.with_memory_space_constraint(x, pltpu.VMEM)


def per_device(
    shift_factors,
    net_load,
    dispatch_level,
    scenario_weight,
    cluster_id,
    commitment,
    unit_capacity,
    unit_bus,
    line_limit,
    multipliers,
    penalty_target,
):
    place = lax.axis_index("bus")
    values = commitment.astype(F32) * unit_capacity[None, :]
    units = jnp.concatenate([values, unit_bus.astype(F32)[None, :]], axis=0)
    units = exchange(jnp.broadcast_to(units[None], (BUS_AXIS, 9, 512)), "bus")

    net = net_flow(shift_factors, net_load.reshape(COLS, BUSES))
    rows = jnp.stack(
        [
            dispatch_level.reshape(COLS),
            jnp.repeat(scenario_weight, HOURS),
            jnp.repeat(cluster_id[:, 0].astype(F32), HOURS),
        ],
        axis=0,
    )
    coded = coded_flow((place * BUSES).reshape(1), units, shift_factors, net, rows)
    received = exchange(coded, "bus")

    limit = lax.dynamic_slice_in_dim(line_limit, place * SHARE, SHARE, 0).reshape(SHARE, 1)
    current = lax.dynamic_slice_in_dim(multipliers, place * SHARE, SHARE, 1)
    target = penalty_target.reshape(OWNED, 1)
    gathered = jnp.concatenate([current, jnp.broadcast_to(target, (OWNED, 64))], axis=1)
    gathered = lax.all_gather(gathered, "scen", axis=0, tiled=True)

    sums = exchange(excess_sums(received, limit, rows), "scen")
    mine = lax.axis_index("scen").reshape(1)
    packed = exchange(updated(mine, sums, gathered, current, target), "bus")
    slopes, duals = slopes_of(packed, shift_factors)
    slopes = exchange(slopes.reshape(LINE_AXIS, HOURS, BUSES), "line")
    dual_out = jnp.moveaxis(duals, 0, 1).reshape(OWNED, LINES)
    return dual_out, jnp.sum(slopes, axis=0, keepdims=True)


def solution(mesh):
    placed = (
        P("line", "bus"),
        P("scen", None, "bus"),
        P("scen", None),
        P("scen"),
        P("scen", None),
        P(None, "bus"),
        P("bus"),
        P("bus"),
        P("line"),
        P("scen", "line"),
        P("scen"),
    )

    return jax.shard_map(
        per_device,
        mesh=mesh,
        in_specs=placed,
        out_specs=(P("scen", "line"), P(("line", "scen"), None, "bus")),
        check_vma=False,
    )
```

time: 253 us -> 161 us (0.64)
  waiting for transfers between devices: 108 us -> 46.3 us
  Pallas kernels: 0 us -> 26.8 us
  blocking collectives: 62.5 us -> 42.4 us
  local copies, waits for them, and re-layouts: 20.4 us -> 5.28 us
  between operations: 14.2 us -> 0.68 us
  starting transfers between devices: 24.3 us -> 35.3 us
  matrix products: 9.74 us -> 0 us
  other arithmetic: 12.7 us -> 3.4 us
    unnamed x2 -> x0, waiting for transfers between devices: 47.7 us -> none
    all_to_all x3 -> x1, blocking collectives: 62.5 us -> 15.6 us  [exchange(): return lax.all_to_all(tiles, axis, 0, 0, tiled=True)]
    pallas_call x0 -> x5, Pallas kernels: none -> 26.8 us  [the longest x1 10.3 us: coded_flow(): pl.pallas_call(flow_kernel, grid=(BUS_AXIS,), in_specs=[pl.BlockSpec(memo...]
    all_gather x0 -> x1, blocking collectives: none -> 26.8 us  [per_device(): gathered = lax.all_gather(gathered, 'scen', axis=0, tiled=True)]
    all_to_all x3 -> x4, waiting for transfers between devices: 60.3 us -> 46.3 us  [exchange(): return lax.all_to_all(tiles, axis, 0, 0, tiled=True)]
    all_to_all x3 -> x4, starting transfers between devices: 24.2 us -> 35.3 us  [exchange(): return lax.all_to_all(tiles, axis, 0, 0, tiled=True)]
    dot_general x5 -> x0, matrix products: 9.74 us -> none  [the longest x1 4.85 us: per_device(): lax.dot_general(block, injection, (((1,), (1,)), ((), ())), preferred_ele...]
    reshape x4 -> x3, local copies, waits for them, and re-layouts: 8.3 us -> 0.9 us  [the longest x1 0.7 us: per_device(): dual_out = jnp.moveaxis(duals, 0, 1).reshape(OWNED, LINES)]
  transfers between devices with their start and end apart: 4 -> 4, of which waited for: 3 -> 3; matrix products, arithmetic and copies ran while one was open for 5% -> 4% of each run, Pallas kernels for 0% -> 4%
where the time goes in v1:
time: 161 us; the launch traced here: 160 us
  waiting for transfers between devices  46.3 us (29%)
  blocking collectives  42.4 us (26%)
  starting transfers between devices  35.3 us (22%)
  Pallas kernels  26.8 us (17%)
  local copies, waits for them, and re-layouts  5.28 us (3%)
  other arithmetic  3.4 us (2%)
    all_to_all x4, waiting for transfers between devices, exchange(): return lax.all_to_all(tiles, axis, 0, 0, tiled=True)  46.3 us
    all_to_all x4, starting transfers between devices, exchange(): return lax.all_to_all(tiles, axis, 0, 0, tiled=True)  35.3 us
    all_gather x1, blocking collectives, per_device(): gathered = lax.all_gather(gathered, 'scen', axis=0, tiled=True)  26.8 us
    all_to_all x1, blocking collectives, exchange(): return lax.all_to_all(tiles, axis, 0, 0, tiled=True)  15.6 us
    pallas_call x1, Pallas kernels, coded_flow(): pl.pallas_call(flow_kernel, grid=(BUS_AXIS,), in_specs=[pl.BlockSpec(memo...  10.3 us
    pallas_call x1, Pallas kernels, slopes_of(): pl.pallas_call(slopes_kernel, grid=(BUS_AXIS,), in_specs=[pl.BlockSpec((1...  6.62 us
    pallas_call x1, Pallas kernels, net_flow(): pl.pallas_call(net_flow_kernel, grid=(4,), in_specs=[pl.BlockSpec((LINES...  5.67 us
    pallas_call x1, Pallas kernels, excess_sums(): pl.pallas_call(excess_kernel, in_specs=[pl.BlockSpec(memory_space=pltpu.V...  3.34 us
  transfers between devices with their start and end apart: 4, of which 3 were waited for; matrix products, arithmetic and copies ran while one was open for 4% of the time, Pallas kernels for 4%

profile of v1, /device:TPU:1, one launch (start us, length us, event | category | flops | bytes accessed | tf_op | source)
XLA Modules:
  0.0 160.2 jit_solution(4111160867913278564)
XLA Ops:
  0.6 0.0 copy-start
  0.6 0.7 convert_element_type.13
  1.3 0.7 convert_multiply_fusion
  2.1 0.7 broadcast_in_dim.25
  2.8 7.6 %all-to-all-start = ((f32[8,9,512]{2,1,0:T(8,128)}), f32[8,9,512]{2,1,0:T(8,128)S(1)}, u32[]{:S(2)}, u32[]{:S(2)}) async-start(f32[8,9,512]{2,1,0:T(8,128)} %broadcast_in_dim.25), calls=%async_computation | async-start | bytes 524288 | tf_op jit(solution)/shard_map/all_to_all | solution.py:253
  10.4 0.7 convert_bitcast_fusion
  11.1 0.1 broadcast_in_dim.27
  11.2 0.1 stack_reshape.11
  11.3 0.7 broadcast_in_dim.26
  12.0 0.1 stack_reshape.10
  12.1 0.8 copy.15
  12.9 0.1 stack_reshape.9
  13.0 5.7 %net_flow.1.net = f32[1536,512]{1,0:T(8,128)} custom-call(bf16[1536,1024]{1,0:T(8,128)(2,1)} %factors.5, bf16[512,1024]{1,0:T(8,128)(2,1)} %bitcast.11), custom_call_target="tpu_custom_call" | custom-call | tf_op jit(solution)/shard_map/net_flow/pallas_call | solution.py:54
  18.6 0.6 pad_maximum_fusion.1.level.rows
  19.2 0.6 all-to-all-done.units
  19.9 10.3 %coded_flow.1 = s16[8,200,512]{2,1,0:T(8,128)(2,1)} custom-call(s32[1]{0:T(128)} %bitcast.1.first, f32[8,9,512]{2,1,0:T(8,128)S(1)} %all-to-all-done.units, bf16[1536,1024]{1,0:T(8,128)(2,1)} %factors.5, f32[1536,512]{1,0:T(8,128)} %net_flow.1.net, f32[3,512]{1,0:T(4,128)} %pad_maximum_fusion.1.level.rows), custom_call_target="tpu_custom_call" | custom-call | tf_op jit(solution)/shard_map/coded_flow/pallas_call | solution.py:116
  30.2 0.0 copy-start.1
  30.2 0.0 copy-start.2
  30.2 6.1 %all-to-all-start.1 = ((s16[8,200,512]{2,1,0:T(8,128)(2,1)}), s16[8,200,512]{2,1,0:T(8,128)(2,1)S(1)}, u32[]{:S(2)}, u32[]{:S(2)}) async-start(s16[8,200,512]{2,1,0:T(8,128)(2,1)} %coded_flow.1), calls=%async_computation.1 | async-start | bytes 3276800 | tf_op jit(solution)/shard_map/all_to_all | solution.py:253
  36.3 0.8 dynamic_slice.6
  37.1 0.1 copy.16.limit
  37.2 40.8 %all-to-all-done.1.coded = s16[8,200,512]{2,1,0:T(8,128)(2,1)S(1)} async-done(((s16[8,200,512]{2,1,0:T(8,128)(2,1)}), s16[8,200,512]{2,1,0:T(8,128)(2,1)S(1)}, u32[]{:S(2)}, u32[]{:S(2)}) %all-to-all-start.1) | async-done | bytes 1638432 | tf_op jit(solution)/shard_map/all_to_all | solution.py:253
  78.0 0.0 copy-done.1
  78.0 3.3 %excess_sums.1 = f32[8,120,128]{2,1,0:T(8,128)} custom-call(s16[8,200,512]{2,1,0:T(8,128)(2,1)S(1)} %all-to-all-done.1.coded, f32[192,1]{1,0:T(8,128)S(1)} %copy.16.limit, f32[3,512]{1,0:T(4,128)S(1)} %copy-done.1), custom_call_target="tpu_custom_call" | custom-call | tf_op jit(solution)/shard_map/excess_sums/pallas_call | solution.py:165
  81.3 10.2 %all-to-all-start.2 = ((f32[8,120,128]{2,1,0:T(8,128)}), f32[8,120,128]{2,1,0:T(8,128)S(1)}, u32[]{:S(2)}, u32[]{:S(2)}) async-start(f32[8,120,128]{2,1,0:T(8,128)} %excess_sums.1), calls=%async_computation.2 | async-start | bytes 983040 | tf_op jit(solution)/shard_map/all_to_all | solution.py:253
  91.5 0.0 copy-done.2
  91.5 0.1 copy.17.target
  91.6 0.0 copy-done
  91.6 0.1 constant_dynamic-slice_fusion.current
  91.7 0.1 broadcast_in_dim.28
  91.8 0.1 pad_maximum_fusion.2
  91.8 26.8 %all_gather.3.gathered = f32[64,256]{1,0:T(8,128)S(1)} all-gather(f32[8,256]{1,0:T(8,128)S(1)} %pad_maximum_fusion.2), channel_id=1, replica_groups=mesh['bus'=8,'line'=8,'scen'=8] {'scen'}, dimensions={0}, use_global_device_ids=true | all-gather | bytes 73728 | tf_op jit(solution)/shard_map/all_gather | solution.py:294
  118.6 0.0 all-to-all-done.2.sums
  118.6 0.9 update.1
  119.6 15.6 %all_to_all.25.packed = f32[8,112,128]{2,1,0:T(8,128)} all-to-all(f32[8,112,128]{2,1,0:T(8,128)} %update.1), channel_id=1, replica_groups=mesh['bus'=8,'line'=8,'scen'=8] {'bus'}, dimensions={0} | all-to-all | bytes 917504 | tf_op jit(solution)/shard_map/all_to_all | solution.py:253
  135.2 6.6 %slopes.1 = (f32[64,1024]{1,0:T(8,128)}, f32[8,8,192]{2,1,0:T(8,128)}) custom-call(f32[8,112,128]{2,1,0:T(8,128)} %all_to_all.25.packed, bf16[1536,1024]{1,0:T(8,128)(2,1)} %factors.5), custom_call_target="tpu_custom_call" | custom-call | tf_op jit(solution)/shard_map/slopes/pallas_call | solution.py:232
  141.8 11.3 %all-to-all-start.4 = ((f32[8,8,1024]{2,1,0:T(8,128)}), f32[8,8,1024]{2,1,0:T(8,128)S(1)}, u32[]{:S(2)}, u32[]{:S(2)}) async-start(f32[8,8,1024]{2,1,0:T(8,128)} %bitcast.12), calls=%async_computation.4 | async-start | bytes 524288 | tf_op jit(solution)/shard_map/all_to_all | solution.py:253
  153.1 0.9 copy.18
  154.0 0.7 reshape.34
  154.7 4.9 %all-to-all-done.4 = f32[8,8,1024]{2,1,0:T(8,128)S(1)} async-done(((f32[8,8,1024]{2,1,0:T(8,128)}), f32[8,8,1024]{2,1,0:T(8,128)S(1)}, u32[]{:S(2)}, u32[]{:S(2)}) %all-to-all-start.4) | async-done | bytes 262176 | tf_op jit(solution)/shard_map/all_to_all | solution.py:253
  159.6 0.6 reduce_sum.9
  (1 shorter events, 0.0 us)
Async XLA Ops:
  0.6 91.0 %copy-start = (f32[8,1536]{1,0:T(8,128)S(1)}, f32[8,1536]{1,0:T(8,128)}, u32[]{:S(2)}) copy-start(f32[8,1536]{1,0:T(8,128)} %param.20) | copy-start | bytes 147460
  2.8 17.1 %all-to-all-start = ((f32[8,9,512]{2,1,0:T(8,128)}), f32[8,9,512]{2,1,0:T(8,128)S(1)}, u32[]{:S(2)}, u32[]{:S(2)}) async-start(f32[8,9,512]{2,1,0:T(8,128)} %broadcast_in_dim.25), calls=%async_computation | async-start | bytes 524288 | tf_op jit(solution)/shard_map/all_to_all | solution.py:253
  30.2 47.8 %copy-start.1 = (f32[3,512]{1,0:T(4,128)S(1)}, f32[3,512]{1,0:T(4,128)}, u32[]{:S(2)}) copy-start(f32[3,512]{1,0:T(4,128)} %pad_maximum_fusion.1.level.rows) | copy-start | bytes 18436
  30.2 61.4 %copy-start.2 = (f32[8]{0:T(128)S(1)}, f32[8]{0:T(128)}, u32[]{:S(2)}) copy-start(f32[8]{0:T(128)} %param.21) | copy-start | bytes 100
  30.2 47.8 %all-to-all-start.1 = ((s16[8,200,512]{2,1,0:T(8,128)(2,1)}), s16[8,200,512]{2,1,0:T(8,128)(2,1)S(1)}, u32[]{:S(2)}, u32[]{:S(2)}) async-start(s16[8,200,512]{2,1,0:T(8,128)(2,1)} %coded_flow.1), calls=%async_computation.1 | async-start | bytes 3276800 | tf_op jit(solution)/shard_map/all_to_all | solution.py:253
  81.3 37.3 %all-to-all-start.2 = ((f32[8,120,128]{2,1,0:T(8,128)}), f32[8,120,128]{2,1,0:T(8,128)S(1)}, u32[]{:S(2)}, u32[]{:S(2)}) async-start(f32[8,120,128]{2,1,0:T(8,128)} %excess_sums.1), calls=%async_computation.2 | async-start | bytes 983040 | tf_op jit(solution)/shard_map/all_to_all | solution.py:253
  141.8 17.8 %all-to-all-start.4 = ((f32[8,8,1024]{2,1,0:T(8,128)}), f32[8,8,1024]{2,1,0:T(8,128)S(1)}, u32[]{:S(2)}, u32[]{:S(2)}) async-start(f32[8,8,1024]{2,1,0:T(8,128)} %bitcast.12), calls=%async_computation.4 | async-start | bytes 524288 | tf_op jit(solution)/shard_map/all_to_all | solution.py:253

commit v2 on v1

v2 whole, which is shorter than its diff:
```python
import jax
import jax.numpy as jnp
from jax import lax
from jax.experimental import pallas as pl
from jax.experimental.pallas import tpu as pltpu
from jax.sharding import PartitionSpec as P


BUS_AXIS = 8
LINE_AXIS = 8
SCEN_AXIS = 8
LINES = 1536
SHARE = LINES // BUS_AXIS
BUSES = 1024
SCEN = 64
HOURS = 8
COLS = SCEN * HOURS
OWNED = 8
ROWS = OWNED * HOURS
STEP = 0.1
CODE = 32000.0
VMEM = 20 * 1024 * 1024
WIDE = 56 * 1024 * 1024

F32 = jnp.float32
BF16 = jnp.bfloat16


def dot_nt(a, b):
    return lax.dot_general(a, b, (((1,), (1,)), ((), ())), preferred_element_type=F32)


def dot_nn(a, b):
    return lax.dot_general(a, b, (((1,), (0,)), ((), ())), preferred_element_type=F32)


def split2(x):
    high = x.astype(BF16)
    return high, (x - high.astype(F32)).astype(BF16)


def split3(x):
    high = x.astype(BF16)
    rest = x - high.astype(F32)
    mid = rest.astype(BF16)
    return high, mid, (rest - mid.astype(F32)).astype(BF16)


def net_flow_kernel(factors, load, net):
    net[...] = dot_nt(factors[...], load[...])


def net_flow(factors, load):
    return pl.pallas_call(
        net_flow_kernel,
        grid=(4,),
        in_specs=[
            pl.BlockSpec((LINES // 4, BUSES), lambda j: (j, 0)),
            pl.BlockSpec((COLS, BUSES), lambda j: (0, 0)),
        ],
        out_specs=pl.BlockSpec((LINES // 4, COLS), lambda j: (j, 0)),
        out_shape=jax.ShapeDtypeStruct((LINES, COLS), F32),
        compiler_params=pltpu.CompilerParams(vmem_limit_bytes=WIDE),
        name="net_flow",
    )(factors, load)


def hour_places():
    column = lax.broadcasted_iota(jnp.int32, (HOURS, COLS), 1)
    row = lax.broadcasted_iota(jnp.int32, (HOURS, COLS), 0)
    return (jnp.bitwise_and(column, HOURS - 1) == row).astype(F32).astype(BF16)


def flow_kernel(first, units, factors, net, level, coded, store):
    @pl.when(pl.program_id(0) == 0)
    def _():
        local = units[:, 8, :] - first[0].astype(F32)
        high = jnp.floor(local * (1.0 / 128.0))
        low = local - high * 128.0
        lows = lax.broadcasted_iota(jnp.int32, (128, 512), 0).astype(F32)
        total = jnp.zeros((192, 128), F32)
        for src in range(BUS_AXIS):
            values = units[src, 0:8, :]
            row_high = high[src : src + 1, :]
            work = jnp.concatenate([jnp.where(row_high == float(block), values, 0.0) for block in range(8)], axis=0)
            match = jnp.where(lows == low[src : src + 1, :], 1.0, 0.0).astype(BF16)
            total = total + dot_nt(jnp.concatenate(split3(work), axis=0), match)
        total = total[0:64] + total[64:128] + total[128:192]
        capacity = jnp.concatenate([total[8 * block : 8 * block + 8] for block in range(8)], axis=1)
        for index, piece in enumerate(split3(capacity)):
            store[8 * index : 8 * index + 8, :] = piece.astype(F32)

    capacity = store[...].astype(BF16)
    place = hour_places()
    place = jnp.concatenate([place, place, place], axis=0)
    first_row = pl.program_id(0) * (2 * SHARE)
    for half in range(2):
        rows = pl.ds(pl.multiple_of(first_row + half * SHARE, SHARE), SHARE)
        given = dot_nt(factors[rows, :], capacity)
        g0, g1, g2 = split3(given)
        fixed = dot_nn(g0, place) + dot_nn(g1, place) + dot_nn(g2, place)
        part = fixed * level[0:1, :] - net[half * SHARE : half * SHARE + SHARE, :]
        top = jnp.maximum(jnp.max(jnp.abs(part), axis=1, keepdims=True), 1e-30)
        power = jnp.ceil(jnp.log2(top) * 8.0)
        unit = jnp.exp2(power * -0.125) * CODE
        coded[half, 0:SHARE, :] = jnp.round(part * unit).astype(jnp.int32).astype(jnp.int16)
        across = jnp.transpose(jnp.broadcast_to(power, (SHARE, 128)))[0:8]
        across = jnp.concatenate([across, jnp.zeros((8, COLS - SHARE), F32)], axis=1)
        coded[half, SHARE : SHARE + 8, :] = across.astype(jnp.int32).astype(jnp.int16)


def coded_flow(first, units, factors, net, level):
    whole = pl.BlockSpec(memory_space=pltpu.VMEM)
    return pl.pallas_call(
        flow_kernel,
        grid=(BUS_AXIS // 2,),
        in_specs=[
            pl.BlockSpec(memory_space=pltpu.SMEM),
            whole,
            whole,
            pl.BlockSpec((2 * SHARE, COLS), lambda j: (j, 0)),
            whole,
        ],
        out_specs=pl.BlockSpec((2, SHARE + 8, COLS), lambda j: (j, 0, 0)),
        out_shape=jax.ShapeDtypeStruct((BUS_AXIS, SHARE + 8, COLS), jnp.int16),
        scratch_shapes=[pltpu.VMEM((24, BUSES), F32)],
        compiler_params=pltpu.CompilerParams(vmem_limit_bytes=WIDE),
        name="coded_flow",
    )(first, near(units), factors, net, near(level))


def excess_kernel(coded, limit, rows, current, target, out):
    level = rows[0:1, :]
    weight = rows[1:2, :]
    cluster = rows[2:3, :]
    column = lax.broadcasted_iota(jnp.int32, (1, COLS), 1)
    hour = jnp.bitwise_and(column, HOURS - 1)
    power = [coded[src, SHARE : SHARE + 8, 0:SHARE].astype(jnp.int32).astype(F32)[0:1] for src in range(BUS_AXIS)]
    unit = jnp.exp2(jnp.transpose(jnp.concatenate(power, axis=0)) * 0.125) * (1.0 / CODE)
    flow = coded[0, 0:SHARE, :].astype(jnp.int32).astype(F32) * unit[:, 0:1]
    for src in range(1, BUS_AXIS):
        flow = flow + coded[src, 0:SHARE, :].astype(jnp.int32).astype(F32) * unit[:, src : src + 1]
    edge = limit[:, 0:1]
    excess = flow - jnp.clip(flow, -edge, edge)
    p0, p1 = split2(excess * (level * weight))
    e0, e1 = split2(excess * excess * (0.5 * weight))
    key = cluster * float(HOURS) + hour.astype(F32)
    row = lax.broadcasted_iota(jnp.int32, (COLS, COLS), 0)
    inner = jnp.bitwise_and(row, ROWS - 1)
    owner = jnp.right_shift(row, 6)
    mine = (jnp.right_shift(inner, 3) * SCEN_AXIS + owner) * HOURS + jnp.bitwise_and(inner, HOURS - 1)
    pick = jnp.where(mine.astype(F32) == key, 1.0, 0.0).astype(BF16)
    pushed = dot_nt(pick, p0) + dot_nt(pick, p1)
    row = lax.broadcasted_iota(jnp.int32, (128, COLS), 0)
    inner = jnp.bitwise_and(row, 15)
    owner = jnp.right_shift(row, 4)
    mine = jnp.where(inner < 8, inner * SCEN_AXIS + owner, owner * OWNED + inner - 8)
    pick = jnp.where(mine.astype(F32) == cluster, 1.0, 0.0).astype(BF16)
    pooled = dot_nt(pick, e0) + dot_nt(pick, e1)
    last = lax.broadcasted_iota(jnp.int32, (8, SHARE), 0)
    for dest in range(SCEN_AXIS):
        given = jnp.where(last == 0, current[dest : dest + 1, :], target[dest : dest + 1, 0:1])
        both = jnp.concatenate(
            [pushed[dest * ROWS : dest * ROWS + ROWS], pooled[dest * 16 : dest * 16 + 16], given], axis=0
        )
        out[dest, 0:88, :] = both[:, 0:128]
        right = jnp.concatenate([both[48:88, 128:192], both[80:88, 128:192]], axis=0)
        out[dest, 88:136, :] = jnp.concatenate([both[0:48, 128:192], right], axis=1)


def excess_sums(coded, limit, rows, current, target):
    return pl.pallas_call(
        excess_kernel,
        in_specs=[pl.BlockSpec(memory_space=pltpu.VMEM)] * 5,
        out_specs=pl.BlockSpec(memory_space=pltpu.VMEM),
        out_shape=pltpu.VMEM((SCEN_AXIS, 136, 128), F32),
        compiler_params=pltpu.CompilerParams(vmem_limit_bytes=VMEM),
        name="excess_sums",
    )(near(coded), near(limit), near(rows), near(current), near(target))


def update_kernel(sums, current, target, out):
    total = sums[0]
    for src in range(1, SCEN_AXIS):
        total = total + sums[src]
    tail = jnp.concatenate([total[88:136, 0:64], total[88:128, 64:128]], axis=0)
    spread = jnp.concatenate(
        [jnp.concatenate([sums[src, 80:81, :], sums[src, 120:121, 64:128]], axis=1) for src in range(OWNED)], axis=0
    )
    spread_target = jnp.concatenate([sums[src, 81:82, 0:1] for src in range(OWNED)], axis=0)
    for part, lo, hi in ((total[0:80], 0, 128), (tail, 128, 192)):
        chosen = jnp.maximum(
            spread[:, lo:hi] + STEP * (part[64:72] - spread_target), 0.0
        )
        owned = jnp.maximum(current[:, lo:hi] + STEP * (part[72:80] - target[:, 0:1]), 0.0)
        wide = jnp.concatenate(
            [part[8 * i : 8 * i + 8] * chosen[i : i + 1] for i in range(OWNED)] + [owned], axis=0
        )
        if lo == 0:
            for dest in range(BUS_AXIS):
                out[dest, 0:72, :] = wide
        else:
            folded = jnp.concatenate([wide[0:40], jnp.concatenate([wide[40:72], wide[64:72]], axis=0)], axis=1)
            for dest in range(BUS_AXIS):
                out[dest, 72:112, :] = folded


def updated(sums, current, target):
    return pl.pallas_call(
        update_kernel,
        in_specs=[pl.BlockSpec(memory_space=pltpu.VMEM)] * 3,
        out_specs=pl.BlockSpec(memory_space=pltpu.VMEM),
        out_shape=jax.ShapeDtypeStruct((BUS_AXIS, 112, 128), F32),
        compiler_params=pltpu.CompilerParams(vmem_limit_bytes=VMEM),
        name="update",
    )(near(sums), near(current), near(target))


def slopes_kernel(packed, factors, slopes, duals):
    total = jnp.zeros((2 * ROWS, BUSES), F32)
    for src in range(BUS_AXIS):
        tail = packed[src, 72:112, :]
        tail = jnp.concatenate([tail[:, 0:64], tail[0:32, 64:128]], axis=0)
        wide = jnp.concatenate([packed[src, 0:72, :], tail], axis=1)
        duals[src] = wide[64:72]
        pieces = jnp.concatenate(split2(wide[0:64]), axis=0)
        total = total + dot_nn(pieces, factors[src * SHARE : src * SHARE + SHARE, :])
    slopes[...] = total[0:ROWS] + total[ROWS:]


def slopes_of(packed, factors):
    return pl.pallas_call(
        slopes_kernel,
        in_specs=[pl.BlockSpec(memory_space=pltpu.VMEM)] * 2,
        out_specs=[pl.BlockSpec(memory_space=pltpu.VMEM)] * 2,
        out_shape=[
            jax.ShapeDtypeStruct((ROWS, BUSES), F32),
            jax.ShapeDtypeStruct((BUS_AXIS, 8, SHARE), F32),
        ],
        compiler_params=pltpu.CompilerParams(vmem_limit_bytes=VMEM),
        name="slopes",
    )(near(packed), factors)


def exchange(tiles, axis):
    return lax.all_to_all(tiles, axis, 0, 0, tiled=True)


def near(x):
    return pltpu.with_memory_space_constraint(x, pltpu.VMEM)


def per_device(
    shift_factors,
    net_load,
    dispatch_level,
    scenario_weight,
    cluster_id,
    commitment,
    unit_capacity,
    unit_bus,
    line_limit,
    multipliers,
    penalty_target,
):
    place = lax.axis_index("bus")
    factors = near(shift_factors)
    values = commitment.astype(F32) * unit_capacity[None, :]
    units = jnp.concatenate([values, unit_bus.astype(F32)[None, :]], axis=0)
    units = exchange(jnp.broadcast_to(units[None], (BUS_AXIS, 9, 512)), "bus")

    net = net_flow(shift_factors, net_load.reshape(COLS, BUSES))
    rows = jnp.stack(
        [
            dispatch_level.reshape(COLS),
            jnp.repeat(scenario_weight, HOURS),
            jnp.repeat(cluster_id[:, 0].astype(F32), HOURS),
        ],
        axis=0,
    )
    coded = coded_flow((place * BUSES).reshape(1), units, factors, net, rows)
    received = exchange(coded, "bus")

    limit = lax.dynamic_slice_in_dim(line_limit, place * SHARE, SHARE, 0).reshape(SHARE, 1)
    current = lax.dynamic_slice_in_dim(multipliers, place * SHARE, SHARE, 1)
    target = penalty_target.reshape(OWNED, 1)
    sums = exchange(excess_sums(received, limit, rows, current, target), "scen")
    packed = exchange(updated(sums, current, target), "bus")
    slopes, duals = slopes_of(packed, factors)
    slopes = exchange(slopes.reshape(LINE_AXIS, HOURS, BUSES), "line")
    dual_out = jnp.moveaxis(duals, 0, 1).reshape(OWNED, LINES)
    return dual_out, jnp.sum(slopes, axis=0, keepdims=True)


def solution(mesh):
    placed = (
        P("line", "bus"),
        P("scen", None, "bus"),
        P("scen", None),
        P("scen"),
        P("scen", None),
        P(None, "bus"),
        P("bus"),
        P("bus"),
        P("line"),
        P("scen", "line"),
        P("scen"),
    )

    return jax.shard_map(
        per_device,
        mesh=mesh,
        in_specs=placed,
        out_specs=(P("scen", "line"), P(("line", "scen"), None, "bus")),
        check_vma=False,
    )
```

time: 161 us -> 138 us (0.86)
  starting transfers between devices: 35.3 us -> 21.6 us
  Pallas kernels: 26.8 us -> 17.8 us
    all_gather x1 -> x0, blocking collectives: 26.8 us -> none  [per_device(): gathered = lax.all_gather(gathered, 'scen', axis=0, tiled=True)]
    all_to_all x1 -> x2, blocking collectives: 15.6 us -> 42.4 us  [exchange(): return lax.all_to_all(tiles, axis, 0, 0, tiled=True)]
    all_to_all x4 -> x3, starting transfers between devices: 35.3 us -> 21.6 us  [exchange(): return lax.all_to_all(tiles, axis, 0, 0, tiled=True)]
    pallas_call x3, Pallas kernels: 17.8 us -> 9.24 us  [the longest x1 7.63 us: coded_flow(): pl.pallas_call(flow_kernel, grid=(BUS_AXIS // 2,), in_specs=[pl.BlockSpec...]
    all_to_all x4 -> x3, waiting for transfers between devices: 46.3 us -> 47.5 us  [exchange(): return lax.all_to_all(tiles, axis, 0, 0, tiled=True)]
  transfers between devices with their start and end apart: 4 -> 3, of which waited for: 3 -> 3; matrix products, arithmetic and copies ran while one was open for 4% -> 3% of each run, Pallas kernels for 4% -> 4%
where the time goes in v2:
time: 138 us; the launch traced here: 137 us
  waiting for transfers between devices  47.5 us (34%)
  blocking collectives  42.4 us (31%)
  starting transfers between devices  21.6 us (16%)
  Pallas kernels  17.8 us (13%)
  local copies, waits for them, and re-layouts  4.37 us (3%)
  other arithmetic  2.73 us (2%)
    all_to_all x3, waiting for transfers between devices, exchange(): return lax.all_to_all(tiles, axis, 0, 0, tiled=True)  47.5 us
    all_to_all x2, blocking collectives, exchange(): return lax.all_to_all(tiles, axis, 0, 0, tiled=True)  42.4 us
    all_to_all x3, starting transfers between devices, exchange(): return lax.all_to_all(tiles, axis, 0, 0, tiled=True)  21.6 us
    pallas_call x1, Pallas kernels, coded_flow(): pl.pallas_call(flow_kernel, grid=(BUS_AXIS // 2,), in_specs=[pl.BlockSpec...  7.63 us
    pallas_call x1, Pallas kernels, net_flow(): pl.pallas_call(net_flow_kernel, grid=(4,), in_specs=[pl.BlockSpec((LINES...  5.81 us
  transfers between devices with their start and end apart: 3, of which 3 were waited for; matrix products, arithmetic and copies ran while one was open for 3% of the time, Pallas kernels for 4%

profile of v2, /device:TPU:1, one launch (start us, length us, event | category | flops | bytes accessed | tf_op | source)
XLA Modules:
  0.0 137.2 jit_solution(719522030893632492)
XLA Ops:
  0.6 0.0 copy-start
  0.6 0.7 convert_element_type.13
  1.3 0.7 convert_multiply_fusion
  2.1 0.7 broadcast_in_dim.20
  2.8 7.6 %all-to-all-start = ((f32[8,9,512]{2,1,0:T(8,128)}), f32[8,9,512]{2,1,0:T(8,128)S(1)}, u32[]{:S(2)}, u32[]{:S(2)}) async-start(f32[8,9,512]{2,1,0:T(8,128)} %broadcast_in_dim.20), calls=%async_computation | async-start | bytes 524288 | tf_op jit(solution)/shard_map/all_to_all | solution.py:246
  10.4 0.7 convert_bitcast_fusion
  11.1 0.1 broadcast_in_dim.22
  11.2 0.1 stack_reshape.11
  11.3 0.7 broadcast_in_dim.21
  12.0 0.1 stack_reshape.10
  12.1 0.8 copy.16
  12.9 0.1 stack_reshape.9
  13.0 0.0 copy-start.1
  13.0 5.8 %net_flow.1.net = f32[1536,512]{1,0:T(8,128)} custom-call(bf16[1536,1024]{1,0:T(8,128)(2,1)} %factors.5, bf16[512,1024]{1,0:T(8,128)(2,1)} %bitcast.11), custom_call_target="tpu_custom_call" | custom-call | tf_op jit(solution)/shard_map/net_flow/pallas_call | solution.py:54
  18.8 1.1 all-to-all-done.units
  19.9 0.0 copy-done.1
  19.9 7.6 %coded_flow.1 = s16[8,200,512]{2,1,0:T(8,128)(2,1)} custom-call(s32[1]{0:T(128)} %bitcast.first, f32[8,9,512]{2,1,0:T(8,128)S(1)} %all-to-all-done.units, bf16[1536,1024]{1,0:T(8,128)(2,1)S(1)} %copy-done.1, f32[1536,512]{1,0:T(8,128)} %net_flow.1.net, f32[3,512]{1,0:T(4,128)S(1)} %pad_maximum_fusion.1.level.rows), custom_call_target="tpu_custom_call" | custom-call | tf_op jit(solution)/shard_map/coded_flow/pallas_call | solution.py:114
  27.5 0.0 copy-start.2
  27.5 5.7 %all-to-all-start.1 = ((s16[8,200,512]{2,1,0:T(8,128)(2,1)}), s16[8,200,512]{2,1,0:T(8,128)(2,1)}, u32[]{:S(2)}, u32[]{:S(2)}) async-start(s16[8,200,512]{2,1,0:T(8,128)(2,1)} %coded_flow.1), calls=%async_computation.1 | async-start | bytes 3276800 | tf_op jit(solution)/shard_map/all_to_all | solution.py:246
  33.2 0.8 dynamic_slice.6
  34.0 0.1 copy.17.limit
  34.1 0.0 copy-done.2
  34.2 0.1 copy.18.target
  34.2 0.0 copy-done
  34.2 0.1 constant_dynamic-slice_fusion.current
  34.3 40.7 %all-to-all-done.1.coded = s16[8,200,512]{2,1,0:T(8,128)(2,1)} async-done(((s16[8,200,512]{2,1,0:T(8,128)(2,1)}), s16[8,200,512]{2,1,0:T(8,128)(2,1)}, u32[]{:S(2)}, u32[]{:S(2)}) %all-to-all-start.1) | async-done | bytes 1638432 | tf_op jit(solution)/shard_map/all_to_all | solution.py:246
  75.0 2.8 %excess_sums.1 = f32[8,136,128]{2,1,0:T(8,128)S(1)} custom-call(s16[8,200,512]{2,1,0:T(8,128)(2,1)} %all-to-all-done.1.coded, f32[192,1]{1,0:T(8,128)S(1)} %copy.17.limit, f32[3,512]{1,0:T(4,128)S(1)} %pad_maximum_fusion.1.level.rows, f32[8,192]{1,0:T(8,128)S(1)} %constant_dynamic-slice_fusion.current, f32[8,1]{1,0:T(8,128)S(1)} %copy.18.target), custom_call_target="tpu_custom_call" | custom-call | tf_op jit(solution)/shard_map/excess_sums/pallas_call | solution.py:172
  77.8 27.0 %all_to_all.25.sums = f32[8,136,128]{2,1,0:T(8,128)S(1)} all-to-all(f32[8,136,128]{2,1,0:T(8,128)S(1)} %excess_sums.1), channel_id=1, replica_groups=mesh['bus'=8,'line'=8,'scen'=8] {'scen'}, dimensions={0} | all-to-all | bytes 1114112 | tf_op jit(solution)/shard_map/all_to_all | solution.py:246
  104.7 0.2 update.1
  104.9 15.5 %all_to_all.26.packed = f32[8,112,128]{2,1,0:T(8,128)S(1)} all-to-all(f32[8,112,128]{2,1,0:T(8,128)S(1)} %update.1), channel_id=1, replica_groups=mesh['bus'=8,'line'=8,'scen'=8] {'bus'}, dimensions={0} | all-to-all | bytes 917504 | tf_op jit(solution)/shard_map/all_to_all | solution.py:246
  120.4 1.4 %slopes.1 = (f32[64,1024]{1,0:T(8,128)}, f32[8,8,192]{2,1,0:T(8,128)S(1)}) custom-call(f32[8,112,128]{2,1,0:T(8,128)S(1)} %all_to_all.26.packed, bf16[1536,1024]{1,0:T(8,128)(2,1)S(1)} %copy-done.1), custom_call_target="tpu_custom_call" | custom-call | tf_op jit(solution)/shard_map/slopes/pallas_call | solution.py:232
  121.8 8.3 %all-to-all-start.4 = ((f32[8,8,1024]{2,1,0:T(8,128)}), f32[8,8,1024]{2,1,0:T(8,128)S(1)}, u32[]{:S(2)}, u32[]{:S(2)}) async-start(f32[8,8,1024]{2,1,0:T(8,128)} %bitcast.7), calls=%async_computation.4 | async-start | bytes 524288 | tf_op jit(solution)/shard_map/all_to_all | solution.py:246
  130.1 0.7 reshape.29
  130.8 5.7 %all-to-all-done.4 = f32[8,8,1024]{2,1,0:T(8,128)S(1)} async-done(((f32[8,8,1024]{2,1,0:T(8,128)}), f32[8,8,1024]{2,1,0:T(8,128)S(1)}, u32[]{:S(2)}, u32[]{:S(2)}) %all-to-all-start.4) | async-done | bytes 262176 | tf_op jit(solution)/shard_map/all_to_all | solution.py:246
  136.5 0.6 reduce_sum.9
  (3 shorter events, 0.0 us)
Async XLA Ops:
  0.6 33.6 %copy-start = (f32[8,1536]{1,0:T(8,128)S(1)}, f32[8,1536]{1,0:T(8,128)}, u32[]{:S(2)}) copy-start(f32[8,1536]{1,0:T(8,128)} %param.20) | copy-start | bytes 147460
  2.8 17.1 %all-to-all-start = ((f32[8,9,512]{2,1,0:T(8,128)}), f32[8,9,512]{2,1,0:T(8,128)S(1)}, u32[]{:S(2)}, u32[]{:S(2)}) async-start(f32[8,9,512]{2,1,0:T(8,128)} %broadcast_in_dim.20), calls=%async_computation | async-start | bytes 524288 | tf_op jit(solution)/shard_map/all_to_all | solution.py:246
  13.0 6.9 %copy-start.1 = (bf16[1536,1024]{1,0:T(8,128)(2,1)S(1)}, bf16[1536,1024]{1,0:T(8,128)(2,1)}, u32[]{:S(2)}) copy-start(bf16[1536,1024]{1,0:T(8,128)(2,1)} %factors.5) | copy-start | bytes 9437188
  27.5 6.6 %copy-start.2 = (f32[8]{0:T(128)S(1)}, f32[8]{0:T(128)}, u32[]{:S(2)}) copy-start(f32[8]{0:T(128)} %param.21) | copy-start | bytes 100
  27.5 47.5 %all-to-all-start.1 = ((s16[8,200,512]{2,1,0:T(8,128)(2,1)}), s16[8,200,512]{2,1,0:T(8,128)(2,1)}, u32[]{:S(2)}, u32[]{:S(2)}) async-start(s16[8,200,512]{2,1,0:T(8,128)(2,1)} %coded_flow.1), calls=%async_computation.1 | async-start | bytes 3276800 | tf_op jit(solution)/shard_map/all_to_all | solution.py:246
  121.8 14.7 %all-to-all-start.4 = ((f32[8,8,1024]{2,1,0:T(8,128)}), f32[8,8,1024]{2,1,0:T(8,128)S(1)}, u32[]{:S(2)}, u32[]{:S(2)}) async-start(f32[8,8,1024]{2,1,0:T(8,128)} %bitcast.7), calls=%async_computation.4 | async-start | bytes 524288 | tf_op jit(solution)/shard_map/all_to_all | solution.py:246

commit v3 on v2

--- a/solution.py
+++ b/solution.py
@@ -11,6 +11,8 @@
 SCEN_AXIS = 8
 LINES = 1536
 SHARE = LINES // BUS_AXIS
+HALF = SHARE // 2
+PAIRS = BUS_AXIS // 2
 BUSES = 1024
 SCEN = 64
 HOURS = 8
@@ -46,23 +48,111 @@
     return high, mid, (rest - mid.astype(F32)).astype(BF16)
 
 
-def net_flow_kernel(factors, load, net):
-    net[...] = dot_nt(factors[...], load[...])
-
-
-def net_flow(factors, load):
+def powers_of(part):
+    top = jnp.maximum(jnp.max(jnp.abs(part), axis=1, keepdims=True), 1e-30)
+    return jnp.ceil(jnp.log2(top) * 8.0)
+
+
+def to_code(part, power):
+    return jnp.round(part * (jnp.exp2(power * -0.125) * CODE)).astype(jnp.int32).astype(jnp.int16)
+
+
+def from_code(code):
+    return code.astype(jnp.int32).astype(F32)
+
+
+def unit_of(power):
+    return jnp.exp2(power * 0.125) * (1.0 / CODE)
+
+
+def as_row(column):
+    return jnp.transpose(jnp.broadcast_to(column, (column.shape[0], 128)))[0:1]
+
+
+def as_column(row):
+    return jnp.transpose(jnp.broadcast_to(row, (128, row.shape[1])))[:, 0:1]
+
+
+def net_flow_kernel(parity, factors, load, keep, send_a, send_b, work, powers):
+    step = pl.program_id(0)
+    work[...] = dot_nt(factors[...], load[...])
+    keep[...] = work[pl.ds(pl.multiple_of(parity[0] * SHARE, SHARE), SHARE), :]
+    other = work[pl.ds(pl.multiple_of((1 - parity[0]) * SHARE, SHARE), SHARE), :]
+
+    @pl.when(step == 0)
+    def _():
+        powers[...] = jnp.zeros_like(powers)
+
+    for index, out in enumerate((send_a, send_b)):
+        part = other[index * HALF : index * HALF + HALF]
+        power = powers_of(part)
+        out[pl.ds(pl.multiple_of(step * HALF, HALF), HALF), :] = to_code(part, power)
+        wide = jnp.concatenate([jnp.broadcast_to(power, (HALF, 128)), jnp.zeros((128 - HALF, 128), F32)], axis=0)
+        mine = lax.broadcasted_iota(jnp.int32, (8, 128), 0) == step
+        powers[index, :, 0:128] = jnp.where(mine, jnp.transpose(wide)[0:8], powers[index, :, 0:128])
+
+    @pl.when(step == PAIRS - 1)
+    def _():
+        for index, out in enumerate((send_a, send_b)):
+            out[PAIRS * HALF : PAIRS * HALF + 8, :] = powers[index].astype(jnp.int32).astype(jnp.int16)
+
+
+def net_flow(parity, factors, load):
+    sent = jax.ShapeDtypeStruct((PAIRS * HALF + 8, COLS), jnp.int16)
     return pl.pallas_call(
         net_flow_kernel,
-        grid=(4,),
+        grid=(PAIRS,),
         in_specs=[
-            pl.BlockSpec((LINES // 4, BUSES), lambda j: (j, 0)),
+            pl.BlockSpec(memory_space=pltpu.SMEM),
+            pl.BlockSpec((2 * SHARE, BUSES), lambda j: (j, 0)),
             pl.BlockSpec((COLS, BUSES), lambda j: (0, 0)),
         ],
-        out_specs=pl.BlockSpec((LINES // 4, COLS), lambda j: (j, 0)),
-        out_shape=jax.ShapeDtypeStruct((LINES, COLS), F32),
+        out_specs=[
+            pl.BlockSpec((SHARE, COLS), lambda j: (j, 0)),
+            pl.BlockSpec((PAIRS * HALF + 8, COLS), lambda j: (0, 0)),
+            pl.BlockSpec((PAIRS * HALF + 8, COLS), lambda j: (0, 0)),
+        ],
+        out_shape=[jax.ShapeDtypeStruct((PAIRS * SHARE, COLS), F32), sent, sent],
+        scratch_shapes=[pltpu.VMEM((2 * SHARE, COLS), F32), pltpu.VMEM((2, 8, COLS), F32)],
         compiler_params=pltpu.CompilerParams(vmem_limit_bytes=WIDE),
         name="net_flow",
-    )(factors, load)
+    )(parity, factors, load)
+
+
+def capacity_kernel(place, units, factors, keep, send):
+    local = units[:, 8, :] - (place[0] * BUSES).astype(F32)
+    parity = jnp.bitwise_and(place[0], 1)
+    high = jnp.floor(local * (1.0 / 128.0))
+    low = local - high * 128.0
+    lows = lax.broadcasted_iota(jnp.int32, (128, 512), 0).astype(F32)
+    total = jnp.zeros((192, 128), F32)
+    for src in range(BUS_AXIS):
+        values = units[src, 0:8, :]
+        row_high = high[src : src + 1, :]
+        work = jnp.concatenate([jnp.where(row_high == float(block), values, 0.0) for block in range(8)], axis=0)
+        match = jnp.where(lows == low[src : src + 1, :], 1.0, 0.0).astype(BF16)
+        total = total + dot_nt(jnp.concatenate(split3(work), axis=0), match)
+    total = total[0:64] + total[64:128] + total[128:192]
+    capacity = jnp.concatenate([total[8 * block : 8 * block + 8] for block in range(8)], axis=1)
+    capacity = jnp.concatenate(split3(capacity), axis=0)
+    for pair in range(PAIRS):
+        for out, side in ((keep, parity), (send, 1 - parity)):
+            first = pl.multiple_of((2 * pair + side) * SHARE, SHARE)
+            given = jnp.transpose(dot_nt(factors[pl.ds(first, SHARE), :], capacity))
+            out[pair] = given[0:8] + given[8:16] + given[16:24]
+
+
+def capacity_flow(place, units, factors):
+    whole = pl.BlockSpec(memory_space=pltpu.VMEM)
+    share = jax.ShapeDtypeStruct((PAIRS, HOURS, SHARE), F32)
+    return pl.pallas_call(
+        capacity_kernel,
+        in_specs=[pl.BlockSpec(memory_space=pltpu.SMEM), whole, whole],
+        out_specs=[whole, whole],
+        out_shape=[share, share],
+        compiler_params=pltpu.CompilerParams(vmem_limit_bytes=VMEM),
+        name="capacity_flow",
+    )(place, near(units), factors)
 
 
 def hour_places():
@@ -71,62 +161,50 @@
     return (jnp.bitwise_and(column, HOURS - 1) == row).astype(F32).astype(BF16)
 
 
-def flow_kernel(first, units, factors, net, level, coded, store):
-    @pl.when(pl.program_id(0) == 0)
-    def _():
-        local = units[:, 8, :] - first[0].astype(F32)
-        high = jnp.floor(local * (1.0 / 128.0))
-        low = local - high * 128.0
-        lows = lax.broadcasted_iota(jnp.int32, (128, 512), 0).astype(F32)
-        total = jnp.zeros((192, 128), F32)
-        for src in range(BUS_AXIS):
-            values = units[src, 0:8, :]
-            row_high = high[src : src + 1, :]
-            work = jnp.concatenate([jnp.where(row_high == float(block), values, 0.0) for block in range(8)], axis=0)
-            match = jnp.where(lows == low[src : src + 1, :], 1.0, 0.0).astype(BF16)
-            total = total + dot_nt(jnp.concatenate(split3(work), axis=0), match)
-        total = total[0:64] + total[64:128] + total[128:192]
-        capacity = jnp.concatenate([total[8 * block : 8 * block + 8] for block in range(8)], axis=1)
-        for index, piece in enumerate(split3(capacity)):
-            store[8 * index : 8 * index + 8, :] = piece.astype(F32)
-
-    capacity = store[...].astype(BF16)
+def pair_kernel(net, code_a, code_b, power_a, power_b, given, given_a, given_b, level, coded):
+    step = pl.program_id(0)
     place = hour_places()
-    place = jnp.concatenate([place, place, place], axis=0)
-    first_row = pl.program_id(0) * (2 * SHARE)
-    for half in range(2):
-        rows = pl.ds(pl.multiple_of(first_row + half * SHARE, SHARE), SHARE)
-        given = dot_nt(factors[rows, :], capacity)
-        g0, g1, g2 = split3(given)
-        fixed = dot_nn(g0, place) + dot_nn(g1, place) + dot_nn(g2, place)
-        part = fixed * level[0:1, :] - net[half * SHARE : half * SHARE + SHARE, :]
-        top = jnp.maximum(jnp.max(jnp.abs(part), axis=1, keepdims=True), 1e-30)
-        power = jnp.ceil(jnp.log2(top) * 8.0)
-        unit = jnp.exp2(power * -0.125) * CODE
-        coded[half, 0:SHARE, :] = jnp.round(part * unit).astype(jnp.int32).astype(jnp.int16)
-        across = jnp.transpose(jnp.broadcast_to(power, (SHARE, 128)))[0:8]
-        across = jnp.concatenate([across, jnp.zeros((8, COLS - SHARE), F32)], axis=1)
-        coded[half, SHARE : SHARE + 8, :] = across.astype(jnp.int32).astype(jnp.int16)
-
-
-def coded_flow(first, units, factors, net, level):
-    whole = pl.BlockSpec(memory_space=pltpu.VMEM)
-    return pl.pallas_call(
-        flow_kernel,
-        grid=(BUS_AXIS // 2,),
+    here = lax.broadcasted_iota(jnp.int32, (8, 128), 0) == step
+    halves = []
+    for index, (code, power) in enumerate(((code_a, power_a), (code_b, power_b))):
+        row = jnp.sum(jnp.where(here, from_code(power[:, 0:128]), 0.0), axis=0, keepdims=True)
+        unit = unit_of(as_column(row))[0:HALF]
+        halves.append(net[index * HALF : index * HALF + HALF, :] + from_code(code[...]) * unit)
+    lane = lax.broadcasted_iota(jnp.int32, (HOURS, SHARE), 1)
+    total = given[0] + jnp.where(lane < HALF, given_a[0], given_b[0])
+    g0, g1, g2 = split3(jnp.transpose(total))
+    fixed = dot_nn(g0, place) + dot_nn(g1, place) + dot_nn(g2, place)
+    part = fixed * level[0:1, :] - jnp.concatenate(halves, axis=0)
+    power = powers_of(part)
+    coded[0, 0:SHARE, :] = to_code(part, power)
+    across = jnp.broadcast_to(as_row(power), (8, SHARE))
+    across = jnp.concatenate([across, jnp.zeros((8, COLS - SHARE), F32)], axis=1)
+    coded[0, SHARE : SHARE + 8, :] = across.astype(jnp.int32).astype(jnp.int16)
+
+
+def pair_flow(net, code_a, code_b, given, given_a, given_b, level):
+    lines = pl.BlockSpec((HALF, COLS), lambda j: (j, 0))
+    tail = pl.BlockSpec((8, COLS), lambda j: (PAIRS * HALF // 8, 0))
+    hours = pl.BlockSpec((1, HOURS, SHARE), lambda j: (j, 0, 0))
+    return pl.pallas_call(
+        pair_kernel,
+        grid=(PAIRS,),
         in_specs=[
-            pl.BlockSpec(memory_space=pltpu.SMEM),
-            whole,
-            whole,
-            pl.BlockSpec((2 * SHARE, COLS), lambda j: (j, 0)),
-            whole,
+            pl.BlockSpec((SHARE, COLS), lambda j: (j, 0)),
+            lines,
+            lines,
+            tail,
+            tail,
+            hours,
+            hours,
+            hours,
+            pl.BlockSpec((3, COLS), lambda j: (0, 0)),
         ],
-        out_specs=pl.BlockSpec((2, SHARE + 8, COLS), lambda j: (j, 0, 0)),
-        out_shape=jax.ShapeDtypeStruct((BUS_AXIS, SHARE + 8, COLS), jnp.int16),
-        scratch_shapes=[pltpu.VMEM((24, BUSES), F32)],
+        out_specs=pl.BlockSpec((1, SHARE + 8, COLS), lambda j: (j, 0, 0)),
+        out_shape=jax.ShapeDtypeStruct((PAIRS, SHARE + 8, COLS), jnp.int16),
         compiler_params=pltpu.CompilerParams(vmem_limit_bytes=WIDE),
-        name="coded_flow",
-    )(first, near(units), factors, net, near(level))
+        name="pair_flow",
+    )(net, code_a, code_b, code_a, code_b, given, given_a, given_b, level)
 
 
 def excess_kernel(coded, limit, rows, current, target, out):
@@ -135,11 +213,11 @@
     cluster = rows[2:3, :]
     column = lax.broadcasted_iota(jnp.int32, (1, COLS), 1)
     hour = jnp.bitwise_and(column, HOURS - 1)
-    power = [coded[src, SHARE : SHARE + 8, 0:SHARE].astype(jnp.int32).astype(F32)[0:1] for src in range(BUS_AXIS)]
-    unit = jnp.exp2(jnp.transpose(jnp.concatenate(power, axis=0)) * 0.125) * (1.0 / CODE)
-    flow = coded[0, 0:SHARE, :].astype(jnp.int32).astype(F32) * unit[:, 0:1]
-    for src in range(1, BUS_AXIS):
-        flow = flow + coded[src, 0:SHARE, :].astype(jnp.int32).astype(F32) * unit[:, src : src + 1]
+    power = jnp.concatenate([from_code(coded[src, SHARE : SHARE + 8, 0:SHARE])[0:1] for src in range(PAIRS)] * 2, axis=0)
+    unit = unit_of(jnp.transpose(power))
+    flow = from_code(coded[0, 0:SHARE, :]) * unit[:, 0:1]
+    for src in range(1, PAIRS):
+        flow = flow + from_code(coded[src, 0:SHARE, :]) * unit[:, src : src + 1]
     edge = limit[:, 0:1]
     excess = flow - jnp.clip(flow, -edge, edge)
     p0, p1 = split2(excess * (level * weight))
@@ -242,6 +320,11 @@
     )(near(packed), factors)
 
 
+NEAR_A = [(i, i ^ 1) for i in range(BUS_AXIS)]
+NEAR_B = [(i, (i + 1 if i % 2 else i - 1) % BUS_AXIS) for i in range(BUS_AXIS)]
+SAME_PARITY = [list(range(0, BUS_AXIS, 2)), list(range(1, BUS_AXIS, 2))]
+
+
 def exchange(tiles, axis):
     return lax.all_to_all(tiles, axis, 0, 0, tiled=True)
 
@@ -269,7 +352,13 @@
     units = jnp.concatenate([values, unit_bus.astype(F32)[None, :]], axis=0)
     units = exchange(jnp.broadcast_to(units[None], (BUS_AXIS, 9, 512)), "bus")
 
-    net = net_flow(shift_factors, net_load.reshape(COLS, BUSES))
+    parity = jnp.bitwise_and(place, 1)
+    keep, send_a, send_b = net_flow(parity.reshape(1), shift_factors, net_load.reshape(COLS, BUSES))
+    code_a = lax.ppermute(send_a, "bus", NEAR_A)
+    code_b = lax.ppermute(send_b, "bus", NEAR_B)
+    keep, dispatch_level, scenario_weight, cluster_id = lax.optimization_barrier(
+        (keep, dispatch_level, scenario_weight, cluster_id)
+    )
     rows = jnp.stack(
         [
             dispatch_level.reshape(COLS),
@@ -278,8 +367,11 @@
         ],
         axis=0,
     )
-    coded = coded_flow((place * BUSES).reshape(1), units, factors, net, rows)
-    received = exchange(coded, "bus")
+    given, send = capacity_flow(place.reshape(1), units, factors)
+    given_a = lax.ppermute(send, "bus", NEAR_A)
+    given_b = lax.ppermute(send, "bus", NEAR_B)
+    coded = pair_flow(keep, code_a, code_b, given, given_a, given_b, rows)
+    received = lax.all_to_all(coded, "bus", 0, 0, axis_index_groups=SAME_PARITY, tiled=True)
 
     limit = lax.dynamic_slice_in_dim(line_limit, place * SHARE, SHARE, 0).reshape(SHARE, 1)
     current = lax.dynamic_slice_in_dim(multipliers, place * SHARE, SHARE, 1)

time: 138 us -> 138 us (level)
  waiting for transfers between devices: 47.5 us -> 33.8 us
  starting transfers between devices: 21.6 us -> 34.8 us
  blocking collectives: 42.4 us -> 44.8 us
  other arithmetic: 2.73 us -> 1.26 us
    all_to_all x3 -> x2, waiting for transfers between devices: 47.5 us -> 13.4 us  [exchange(): return lax.all_to_all(tiles, axis, 0, 0, tiled=True)]
    all_to_all x0 -> x1, waiting for transfers between devices: none -> 19.7 us  [per_device(): lax.all_to_all(coded, 'bus', 0, 0, axis_index_groups=SAME_PARITY, tiled=T...]
    ppermute x0 -> x4, starting transfers between devices: none -> 17.5 us  [the longest x1 4.87 us: per_device(): code_b = lax.ppermute(send_b, 'bus', NEAR_B)]
    all_to_all x3 -> x2, starting transfers between devices: 21.6 us -> 11.8 us  [exchange(): return lax.all_to_all(tiles, axis, 0, 0, tiled=True)]
    all_to_all x0 -> x1, starting transfers between devices: none -> 5.52 us  [per_device(): lax.all_to_all(coded, 'bus', 0, 0, axis_index_groups=SAME_PARITY, tiled=T...]
    all_to_all x2, blocking collectives: 42.4 us -> 44.8 us  [exchange(): return lax.all_to_all(tiles, axis, 0, 0, tiled=True)]
    pallas_call x2 -> x3, Pallas kernels: 13.4 us -> 13.4 us  [the longest x1 6.45 us: net_flow(): pl.pallas_call(net_flow_kernel, grid=(PAIRS,), in_specs=[pl.BlockSpec(mem...]
  transfers between devices with their start and end apart: 3 -> 7, of which waited for: 3 -> 4; matrix products, arithmetic and copies ran while one was open for 3% -> 3% of each run, Pallas kernels for 4% -> 2%
where the time goes in v3:
time: 138 us; the launch traced here: 137 us
  blocking collectives  44.8 us (32%)
  starting transfers between devices  34.8 us (25%)
  waiting for transfers between devices  33.8 us (24%)
  Pallas kernels  17.3 us (13%)
  local copies, waits for them, and re-layouts  4.29 us (3%)
    all_to_all x2, blocking collectives, exchange(): return lax.all_to_all(tiles, axis, 0, 0, tiled=True)  44.8 us
    all_to_all x1, waiting for transfers between devices, per_device(): lax.all_to_all(coded, 'bus', 0, 0, axis_index_groups=SAME_PARITY, tiled=T...  19.7 us
    all_to_all x2, waiting for transfers between devices, exchange(): return lax.all_to_all(tiles, axis, 0, 0, tiled=True)  13.4 us
    all_to_all x2, starting transfers between devices, exchange(): return lax.all_to_all(tiles, axis, 0, 0, tiled=True)  11.8 us
    pallas_call x1, Pallas kernels, net_flow(): pl.pallas_call(net_flow_kernel, grid=(PAIRS,), in_specs=[pl.BlockSpec(mem...  6.45 us
    all_to_all x1, starting transfers between devices, per_device(): lax.all_to_all(coded, 'bus', 0, 0, axis_index_groups=SAME_PARITY, tiled=T...  5.52 us
    ppermute x1, starting transfers between devices, per_device(): code_b = lax.ppermute(send_b, 'bus', NEAR_B)  4.87 us
    ppermute x1, starting transfers between devices, per_device(): given_b = lax.ppermute(send, 'bus', NEAR_B)  4.6 us
  transfers between devices with their start and end apart: 7, of which 4 were waited for; matrix products, arithmetic and copies ran while one was open for 3% of the time, Pallas kernels for 2%

profile of v3, /device:TPU:1, one launch (start us, length us, event | category | flops | bytes accessed | tf_op | source)
XLA Modules:
  0.0 137.2 jit_solution(9319054073817236960)
XLA Ops:
  0.6 0.0 copy-start
  0.6 0.0 copy-start.1
  0.7 0.0 copy-start.9
  0.7 0.0 copy-start.6
  0.7 0.0 copy-start.8
  0.7 0.0 copy-start.7
  0.7 0.0 copy-start.10
  0.7 0.0 copy-start.12
  0.7 6.4 %net_flow.1 = (f32[768,512]{1,0:T(8,128)}, s16[392,512]{1,0:T(8,128)(2,1)}, s16[392,512]{1,0:T(8,128)(2,1)}) custom-call(s32[1]{0:T(128)} %bitcast.parity, bf16[1536,1024]{1,0:T(8,128)(2,1)} %factors.5, bf16[512,1024]{1,0:T(8,128)(2,1)} %bitcast.12), custom_call_target="tpu_custom_call" | custom-call | tf_op jit(solution)/shard_map/net_flow/pallas_call | solution.py:102
  7.2 4.0 %collective-permute-start = (s16[392,512]{1,0:T(8,128)(2,1)}, s16[392,512]{1,0:T(8,128)(2,1)}, u32[]{:S(2)}, u32[]{:S(2)}) collective-permute-start(s16[392,512]{1,0:T(8,128)(2,1)} %get-tuple-element.15), channel_id=1, source_target_pairs={{0,64},{64,0},{128,192},{192,128},{256,320},{320,256},{384,448},{4... | collective-permute-start | bytes 1204232 | tf_op jit(solution)/shard_map/ppermute | solution.py:357
  11.2 4.9 %collective-permute-start.1 = (s16[392,512]{1,0:T(8,128)(2,1)}, s16[392,512]{1,0:T(8,128)(2,1)}, u32[]{:S(2)}, u32[]{:S(2)}) collective-permute-start(s16[392,512]{1,0:T(8,128)(2,1)} %get-tuple-element.16), channel_id=1, source_target_pairs={{0,448},{64,128},{128,64},{192,256},{256,192},{320,384},{384,320},... | collective-permute-start | bytes 1204232 | tf_op jit(solution)/shard_map/ppermute | solution.py:358
  16.1 0.0 copy-done.9
  16.1 0.0 copy-done.6
  16.1 0.0 copy-done.8
  16.1 0.7 broadcast_in_dim.20
  16.9 3.4 %all-to-all-start = ((f32[8,9,512]{2,1,0:T(8,128)}), f32[8,9,512]{2,1,0:T(8,128)S(1)}, u32[]{:S(2)}, u32[]{:S(2)}) async-start(f32[8,9,512]{2,1,0:T(8,128)} %broadcast_in_dim.20), calls=%async_computation | async-start | bytes 524288 | tf_op jit(solution)/shard_map/all_to_all | solution.py:329
  20.3 0.0 copy-done.12
  20.3 0.1 broadcast_in_dim.22
  20.4 0.1 stack_reshape.11
  20.5 0.0 copy-done.10
  20.5 0.1 broadcast_in_dim.21
  20.6 0.1 stack_reshape.10
  20.7 0.0 copy-done.7
  20.7 0.1 copy.16
  20.8 0.1 stack_reshape.9
  20.9 7.7 %all-to-all-done.units = f32[8,9,512]{2,1,0:T(8,128)S(1)} async-done(((f32[8,9,512]{2,1,0:T(8,128)}), f32[8,9,512]{2,1,0:T(8,128)S(1)}, u32[]{:S(2)}, u32[]{:S(2)}) %all-to-all-start) | async-done | bytes 147488 | tf_op jit(solution)/shard_map/all_to_all | solution.py:329
  28.5 0.0 copy-done.1
  28.5 2.4 %capacity_flow.1 = (f32[4,8,192]{2,1,0:T(8,128)S(1)}, f32[4,8,192]{2,1,0:T(8,128)S(1)}) custom-call(s32[1]{0:T(128)} %bitcast.2.place, f32[8,9,512]{2,1,0:T(8,128)S(1)} %all-to-all-done.units, bf16[1536,1024]{1,0:T(8,128)(2,1)S(1)} %copy-done.1), custom_call_target="tpu_custom_call" | custom-call | tf_op jit(solution)/shard_map/capacity_flow/pallas_call | solution.py:148
  30.9 0.0 copy-start.3
  30.9 0.6 copy-done.3
  31.5 0.0 copy-start.11
  31.5 4.0 %collective-permute-start.2 = (f32[4,8,192]{2,1,0:T(8,128)S(1)}, f32[4,8,192]{2,1,0:T(8,128)S(1)}, u32[]{:S(2)}, u32[]{:S(2)}) collective-permute-start(f32[4,8,192]{2,1,0:T(8,128)S(1)} %get-tuple-element.18), channel_id=1, source_target_pairs={{0,64},{64,0},{128,192},{192,128},{256,320},{320,256},{384,448},{4... | collective-permute-start | bytes 73736 | tf_op jit(solution)/shard_map/ppermute | solution.py:371
  35.5 4.6 %collective-permute-start.3 = (f32[4,8,192]{2,1,0:T(8,128)S(1)}, f32[4,8,192]{2,1,0:T(8,128)S(1)}, u32[]{:S(2)}, u32[]{:S(2)}) collective-permute-start(f32[4,8,192]{2,1,0:T(8,128)S(1)} %get-tuple-element.18), channel_id=1, source_target_pairs={{0,448},{64,128},{128,64},{192,256},{256,192},{320,384},{384,320},... | collective-permute-start | bytes 73736 | tf_op jit(solution)/shard_map/ppermute | solution.py:372
  40.2 0.6 pad_maximum_fusion.1.level.rows
  40.8 0.0 copy-start.2
  40.8 0.0 collective-permute-done.2.given_a
  40.8 0.0 copy-start.4
  40.8 0.7 collective-permute-done.3.given_b
  41.4 0.0 copy-start.5
  41.4 0.0 collective-permute-done.code_a.power_a
  41.4 0.0 collective-permute-done.1.code_b.power_b
  41.5 0.0 copy-done.4
  41.5 0.6 copy-done.5
  42.0 4.6 %pair_flow.1 = s16[4,200,512]{2,1,0:T(8,128)(2,1)} custom-call(f32[768,512]{1,0:T(8,128)} %get-tuple-element.14.net, s16[392,512]{1,0:T(8,128)(2,1)} %collective-permute-done.code_a.power_a, s16[392,512]{1,0:T(8,128)(2,1)} %collective-permute-done.1.code_b.power_b, s16[392,512]{1,0:T(8,128)(2,1)} %collective-permute-done.code_a.power_a, ...), custom_call_target="tpu_custom_call" | custom-call | tf_op jit(solution)/shard_map/pair_flow/pallas_call | solution.py:189
  46.6 5.5 %all-to-all-start.1 = ((s16[4,200,512]{2,1,0:T(8,128)(2,1)}), s16[4,200,512]{2,1,0:T(8,128)(2,1)}, u32[]{:S(2)}, u32[]{:S(2)}) async-start(s16[4,200,512]{2,1,0:T(8,128)(2,1)} %pair_flow.1), calls=%async_computation.1 | async-start | bytes 1638400 | tf_op jit(solution)/shard_map/all_to_all | solution.py:374
  52.2 0.8 dynamic_slice.6
  52.9 0.1 copy.17.limit
  53.0 0.0 copy-done.11
  53.1 0.1 copy.18.target
  53.1 0.0 copy-done
  53.1 0.1 constant_dynamic-slice_fusion.current
  53.2 19.7 %all-to-all-done.1.coded = s16[4,200,512]{2,1,0:T(8,128)(2,1)} async-done(((s16[4,200,512]{2,1,0:T(8,128)(2,1)}), s16[4,200,512]{2,1,0:T(8,128)(2,1)}, u32[]{:S(2)}, u32[]{:S(2)}) %all-to-all-start.1) | async-done | bytes 819232 | tf_op jit(solution)/shard_map/all_to_all | solution.py:374
  73.0 0.0 copy-done.2
  73.0 2.3 %excess_sums.1 = f32[8,136,128]{2,1,0:T(8,128)S(1)} custom-call(s16[4,200,512]{2,1,0:T(8,128)(2,1)} %all-to-all-done.1.coded, f32[192,1]{1,0:T(8,128)S(1)} %copy.17.limit, f32[3,512]{1,0:T(4,128)S(1)} %copy-done.2, f32[8,192]{1,0:T(8,128)S(1)} %constant_dynamic-slice_fusion.current, f32[8,1]{1,0:T(8,128)S(1)} %copy.18.target), custom_call_target="tpu_custom_call" | custom-call | tf_op jit(solution)/shard_map/excess_sums/pallas_call | solution.py:250
  75.2 27.0 %all_to_all.25.sums = f32[8,136,128]{2,1,0:T(8,128)S(1)} all-to-all(f32[8,136,128]{2,1,0:T(8,128)S(1)} %excess_sums.1), channel_id=1, replica_groups=mesh['bus'=8,'line'=8,'scen'=8] {'scen'}, dimensions={0} | all-to-all | bytes 1114112 | tf_op jit(solution)/shard_map/all_to_all | solution.py:329
  102.2 0.2 update.1
  102.4 17.8 %all_to_all.26.packed = f32[8,112,128]{2,1,0:T(8,128)S(1)} all-to-all(f32[8,112,128]{2,1,0:T(8,128)S(1)} %update.1), channel_id=1, replica_groups=mesh['bus'=8,'line'=8,'scen'=8] {'bus'}, dimensions={0} | all-to-all | bytes 917504 | tf_op jit(solution)/shard_map/all_to_all | solution.py:329
  120.2 1.4 %slopes.1 = (f32[64,1024]{1,0:T(8,128)}, f32[8,8,192]{2,1,0:T(8,128)S(1)}) custom-call(f32[8,112,128]{2,1,0:T(8,128)S(1)} %all_to_all.26.packed, bf16[1536,1024]{1,0:T(8,128)(2,1)S(1)} %copy-done.1), custom_call_target="tpu_custom_call" | custom-call | tf_op jit(solution)/shard_map/slopes/pallas_call | solution.py:310
  121.7 8.4 %all-to-all-start.4 = ((f32[8,8,1024]{2,1,0:T(8,128)}), f32[8,8,1024]{2,1,0:T(8,128)S(1)}, u32[]{:S(2)}, u32[]{:S(2)}) async-start(f32[8,8,1024]{2,1,0:T(8,128)} %bitcast.8), calls=%async_computation.4 | async-start | bytes 524288 | tf_op jit(solution)/shard_map/all_to_all | solution.py:329
  130.1 0.7 reshape.33
  130.8 5.7 %all-to-all-done.4 = f32[8,8,1024]{2,1,0:T(8,128)S(1)} async-done(((f32[8,8,1024]{2,1,0:T(8,128)}), f32[8,8,1024]{2,1,0:T(8,128)S(1)}, u32[]{:S(2)}, u32[]{:S(2)}) %all-to-all-start.4) | async-done | bytes 262176 | tf_op jit(solution)/shard_map/all_to_all | solution.py:329
  136.5 0.6 reduce_sum.9
  (5 shorter events, 0.0 us)
Async XLA Ops:
  0.6 52.5 %copy-start = (f32[8,1536]{1,0:T(8,128)S(1)}, f32[8,1536]{1,0:T(8,128)}, u32[]{:S(2)}) copy-start(f32[8,1536]{1,0:T(8,128)} %param.20) | copy-start | bytes 147460
  0.6 27.9 %copy-start.1 = (bf16[1536,1024]{1,0:T(8,128)(2,1)S(1)}, bf16[1536,1024]{1,0:T(8,128)(2,1)}, u32[]{:S(2)}) copy-start(bf16[1536,1024]{1,0:T(8,128)(2,1)} %factors.5) | copy-start | bytes 9437188
  0.7 15.4 %copy-start.9 = (s32[512]{0:T(512)S(1)}, s32[512]{0:T(512)}, u32[]{:S(2)}) copy-start(s32[512]{0:T(512)} %param.18) | copy-start | bytes 6148
  0.7 15.4 %copy-start.6 = (s32[8,512]{1,0:T(8,128)S(1)}, s32[8,512]{1,0:T(8,128)}, u32[]{:S(2)}) copy-start(s32[8,512]{1,0:T(8,128)} %param.16) | copy-start | bytes 49156
  0.7 15.4 %copy-start.8 = (f32[512]{0:T(512)S(1)}, f32[512]{0:T(512)}, u32[]{:S(2)}) copy-start(f32[512]{0:T(512)} %param.17) | copy-start | bytes 6148
  0.7 20.0 %copy-start.7 = (f32[64,8]{0,1:T(8,128)S(1)}, f32[64,8]{0,1:T(8,128)}, u32[]{:S(2)}) copy-start(f32[64,8]{0,1:T(8,128)} %param.13) | copy-start | bytes 6148
  0.7 19.8 %copy-start.10 = (f32[64]{0:T(128)S(1)}, f32[64]{0:T(128)}, u32[]{:S(2)}) copy-start(f32[64]{0:T(128)} %param.14) | copy-start | bytes 772
  0.7 19.6 %copy-start.12 = (s32[64,1]{0,1:T(1,128)S(1)}, s32[64,1]{0,1:T(1,128)}, u32[]{:S(2)}) copy-start(s32[64,1]{0,1:T(1,128)} %param.15) | copy-start | bytes 772
  7.2 34.3 %collective-permute-start = (s16[392,512]{1,0:T(8,128)(2,1)}, s16[392,512]{1,0:T(8,128)(2,1)}, u32[]{:S(2)}, u32[]{:S(2)}) collective-permute-start(s16[392,512]{1,0:T(8,128)(2,1)} %get-tuple-element.15), channel_id=1, source_target_pairs={{0,64},{64,0},{128,192},{192,128},{256,320},{320,256},{384,448},{4... | collective-permute-start | bytes 1204232 | tf_op jit(solution)/shard_map/ppermute | solution.py:357
  11.2 30.3 %collective-permute-start.1 = (s16[392,512]{1,0:T(8,128)(2,1)}, s16[392,512]{1,0:T(8,128)(2,1)}, u32[]{:S(2)}, u32[]{:S(2)}) collective-permute-start(s16[392,512]{1,0:T(8,128)(2,1)} %get-tuple-element.16), channel_id=1, source_target_pairs={{0,448},{64,128},{128,64},{192,256},{256,192},{320,384},{384,320},... | collective-permute-start | bytes 1204232 | tf_op jit(solution)/shard_map/ppermute | solution.py:358
  16.9 11.6 %all-to-all-start = ((f32[8,9,512]{2,1,0:T(8,128)}), f32[8,9,512]{2,1,0:T(8,128)S(1)}, u32[]{:S(2)}, u32[]{:S(2)}) async-start(f32[8,9,512]{2,1,0:T(8,128)} %broadcast_in_dim.20), calls=%async_computation | async-start | bytes 524288 | tf_op jit(solution)/shard_map/all_to_all | solution.py:329
  30.9 0.6 copy-start.3
  31.5 21.5 %copy-start.11 = (f32[8]{0:T(128)S(1)}, f32[8]{0:T(128)}, u32[]{:S(2)}) copy-start(f32[8]{0:T(128)} %param.21) | copy-start | bytes 100
  31.5 9.2 %collective-permute-start.2 = (f32[4,8,192]{2,1,0:T(8,128)S(1)}, f32[4,8,192]{2,1,0:T(8,128)S(1)}, u32[]{:S(2)}, u32[]{:S(2)}) collective-permute-start(f32[4,8,192]{2,1,0:T(8,128)S(1)} %get-tuple-element.18), channel_id=1, source_target_pairs={{0,64},{64,0},{128,192},{192,128},{256,320},{320,256},{384,448},{4... | collective-permute-start | bytes 73736 | tf_op jit(solution)/shard_map/ppermute | solution.py:371
  35.5 5.9 %collective-permute-start.3 = (f32[4,8,192]{2,1,0:T(8,128)S(1)}, f32[4,8,192]{2,1,0:T(8,128)S(1)}, u32[]{:S(2)}, u32[]{:S(2)}) collective-permute-start(f32[4,8,192]{2,1,0:T(8,128)S(1)} %get-tuple-element.18), channel_id=1, source_target_pairs={{0,448},{64,128},{128,64},{192,256},{256,192},{320,384},{384,320},... | collective-permute-start | bytes 73736 | tf_op jit(solution)/shard_map/ppermute | solution.py:372
  40.8 32.2 %copy-start.2 = (f32[3,512]{1,0:T(4,128)S(1)}, f32[3,512]{1,0:T(4,128)}, u32[]{:S(2)}) copy-start(f32[3,512]{1,0:T(4,128)} %pad_maximum_fusion.1.level.rows) | copy-start | bytes 18436
  40.8 0.7 copy-start.4
  41.4 0.6 copy-start.5
  46.6 26.3 %all-to-all-start.1 = ((s16[4,200,512]{2,1,0:T(8,128)(2,1)}), s16[4,200,512]{2,1,0:T(8,128)(2,1)}, u32[]{:S(2)}, u32[]{:S(2)}) async-start(s16[4,200,512]{2,1,0:T(8,128)(2,1)} %pair_flow.1), calls=%async_computation.1 | async-start | bytes 1638400 | tf_op jit(solution)/shard_map/all_to_all | solution.py:374
  121.7 14.9 %all-to-all-start.4 = ((f32[8,8,1024]{2,1,0:T(8,128)}), f32[8,8,1024]{2,1,0:T(8,128)S(1)}, u32[]{:S(2)}, u32[]{:S(2)}) async-start(f32[8,8,1024]{2,1,0:T(8,128)} %bitcast.8), calls=%async_computation.4 | async-start | bytes 524288 | tf_op jit(solution)/shard_map/all_to_all | solution.py:329

commit v4 on v3

--- a/solution.py
+++ b/solution.py
@@ -73,32 +73,36 @@
     return jnp.transpose(jnp.broadcast_to(row, (128, row.shape[1])))[:, 0:1]
 
 
-def net_flow_kernel(parity, factors, load, keep, send_a, send_b, work, powers):
-    step = pl.program_id(0)
+def units_kernel(commitment, capacity, bus, out):
+    values = commitment[...].astype(F32) * capacity[...]
+    where = bus[...].astype(F32)
+    blank = jnp.zeros((8, 128), F32)
+    row = lax.broadcasted_iota(jnp.int32, (8, 128), 0)
+    for part in range(4):
+        blank = jnp.where(row == part, where[:, 128 * part : 128 * part + 128], blank)
+    for dest in range(BUS_AXIS):
+        for part in range(4):
+            out[dest, 8 * part : 8 * part + 8, :] = values[:, 128 * part : 128 * part + 128]
+        out[dest, 32:40, :] = blank
+
+
+def packed_units(commitment, capacity, bus):
+    return pl.pallas_call(
+        units_kernel,
+        out_shape=jax.ShapeDtypeStruct((BUS_AXIS, 40, 128), F32),
+        compiler_params=pltpu.CompilerParams(vmem_limit_bytes=WIDE),
+        name="units",
+    )(commitment, capacity.reshape(1, 512), bus.reshape(1, 512))
+
+
+def net_flow_kernel(parity, factors, load, keep, other, work):
     work[...] = dot_nt(factors[...], load[...])
     keep[...] = work[pl.ds(pl.multiple_of(parity[0] * SHARE, SHARE), SHARE), :]
-    other = work[pl.ds(pl.multiple_of((1 - parity[0]) * SHARE, SHARE), SHARE), :]
-
-    @pl.when(step == 0)
-    def _():
-        powers[...] = jnp.zeros_like(powers)
-
-    for index, out in enumerate((send_a, send_b)):
-        part = other[index * HALF : index * HALF + HALF]
-        power = powers_of(part)
-        out[pl.ds(pl.multiple_of(step * HALF, HALF), HALF), :] = to_code(part, power)
-        wide = jnp.concatenate([jnp.broadcast_to(power, (HALF, 128)), jnp.zeros((128 - HALF, 128), F32)], axis=0)
-        mine = lax.broadcasted_iota(jnp.int32, (8, 128), 0) == step
-        powers[index, :, 0:128] = jnp.where(mine, jnp.transpose(wide)[0:8], powers[index, :, 0:128])
-
-    @pl.when(step == PAIRS - 1)
-    def _():
-        for index, out in enumerate((send_a, send_b)):
-            out[PAIRS * HALF : PAIRS * HALF + 8, :] = powers[index].astype(jnp.int32).astype(jnp.int16)
+    other[...] = work[pl.ds(pl.multiple_of((1 - parity[0]) * SHARE, SHARE), SHARE), :]
 
 
 def net_flow(parity, factors, load):
-    sent = jax.ShapeDtypeStruct((PAIRS * HALF + 8, COLS), jnp.int16)
+    half = jax.ShapeDtypeStruct((PAIRS * SHARE, COLS), F32)
     return pl.pallas_call(
         net_flow_kernel,
         grid=(PAIRS,),
@@ -107,74 +111,97 @@
             pl.BlockSpec((2 * SHARE, BUSES), lambda j: (j, 0)),
             pl.BlockSpec((COLS, BUSES), lambda j: (0, 0)),
         ],
-        out_specs=[
-            pl.BlockSpec((SHARE, COLS), lambda j: (j, 0)),
-            pl.BlockSpec((PAIRS * HALF + 8, COLS), lambda j: (0, 0)),
-            pl.BlockSpec((PAIRS * HALF + 8, COLS), lambda j: (0, 0)),
-        ],
-        out_shape=[jax.ShapeDtypeStruct((PAIRS * SHARE, COLS), F32), sent, sent],
-        scratch_shapes=[pltpu.VMEM((2 * SHARE, COLS), F32), pltpu.VMEM((2, 8, COLS), F32)],
+        out_specs=[pl.BlockSpec((SHARE, COLS), lambda j: (j, 0))] * 2,
+        out_shape=[half, half],
+        scratch_shapes=[pltpu.VMEM((2 * SHARE, COLS), F32)],
         compiler_params=pltpu.CompilerParams(vmem_limit_bytes=WIDE),
         name="net_flow",
     )(parity, factors, load)
 
 
-def capacity_kernel(place, units, factors, keep, send):
-    local = units[:, 8, :] - (place[0] * BUSES).astype(F32)
+def hour_places():
+    column = lax.broadcasted_iota(jnp.int32, (3 * HOURS, COLS), 1)
+    row = lax.broadcasted_iota(jnp.int32, (3 * HOURS, COLS), 0)
+    return (jnp.bitwise_and(column, HOURS - 1) == jnp.bitwise_and(row, HOURS - 1)).astype(F32).astype(BF16)
+
+
+def over_columns(given, place):
+    pieces = jnp.concatenate([piece.astype(F32) for piece in split3(given)], axis=0)
+    return dot_nn(jnp.transpose(pieces).astype(BF16), place)
+
+
+def send_kernel(place, units, factors, level, other, given, send_a, send_b, stage, powers, semaphore):
+    load = pltpu.make_async_copy(other, stage, semaphore)
+    load.start()
     parity = jnp.bitwise_and(place[0], 1)
-    high = jnp.floor(local * (1.0 / 128.0))
-    low = local - high * 128.0
+    first = (place[0] * BUSES).astype(F32)
     lows = lax.broadcasted_iota(jnp.int32, (128, 512), 0).astype(F32)
     total = jnp.zeros((192, 128), F32)
     for src in range(BUS_AXIS):
-        values = units[src, 0:8, :]
-        row_high = high[src : src + 1, :]
-        work = jnp.concatenate([jnp.where(row_high == float(block), values, 0.0) for block in range(8)], axis=0)
-        match = jnp.where(lows == low[src : src + 1, :], 1.0, 0.0).astype(BF16)
+        values = jnp.concatenate([units[src, 8 * part : 8 * part + 8, :] for part in range(4)], axis=1)
+        local = jnp.concatenate([units[src, 32 + part : 33 + part, :] for part in range(4)], axis=1) - first
+        high = jnp.floor(local * (1.0 / 128.0))
+        low = local - high * 128.0
+        work = jnp.concatenate([jnp.where(high == float(block), values, 0.0) for block in range(8)], axis=0)
+        match = jnp.where(lows == low, 1.0, 0.0).astype(BF16)
         total = total + dot_nt(jnp.concatenate(split3(work), axis=0), match)
     total = total[0:64] + total[64:128] + total[128:192]
     capacity = jnp.concatenate([total[8 * block : 8 * block + 8] for block in range(8)], axis=1)
     capacity = jnp.concatenate(split3(capacity), axis=0)
+    spread = hour_places()
+    powers[...] = jnp.zeros_like(powers)
+    load.wait()
     for pair in range(PAIRS):
-        for out, side in ((keep, parity), (send, 1 - parity)):
-            first = pl.multiple_of((2 * pair + side) * SHARE, SHARE)
-            given = jnp.transpose(dot_nt(factors[pl.ds(first, SHARE), :], capacity))
-            out[pair] = given[0:8] + given[8:16] + given[16:24]
-
-
-def capacity_flow(place, units, factors):
+        halves = []
+        for side in (parity, 1 - parity):
+            row = pl.multiple_of((2 * pair + side) * SHARE, SHARE)
+            part = jnp.transpose(dot_nt(factors[pl.ds(row, SHARE), :], capacity))
+            halves.append(part[0:8] + part[8:16] + part[16:24])
+        given[pair] = halves[0]
+        part = over_columns(halves[1], spread) * level[0:1, :] - stage[pair * SHARE : pair * SHARE + SHARE, :]
+        power = powers_of(part)
+        code = to_code(part, power)
+        across = as_row(power)
+        for index, out in enumerate((send_a, send_b)):
+            out[pair * HALF : pair * HALF + HALF, :] = code[index * HALF : index * HALF + HALF]
+        powers[pair : pair + 1, 0:SHARE] = across
+    for out in (send_a, send_b):
+        out[PAIRS * HALF : PAIRS * HALF + 8, :] = powers[...].astype(jnp.int32).astype(jnp.int16)
+
+
+def sent_flow(place, units, factors, level, other):
     whole = pl.BlockSpec(memory_space=pltpu.VMEM)
-    share = jax.ShapeDtypeStruct((PAIRS, HOURS, SHARE), F32)
-    return pl.pallas_call(
-        capacity_kernel,
-        in_specs=[pl.BlockSpec(memory_space=pltpu.SMEM), whole, whole],
-        out_specs=[whole, whole],
-        out_shape=[share, share],
-        compiler_params=pltpu.CompilerParams(vmem_limit_bytes=VMEM),
-        name="capacity_flow",
-    )(place, near(units), factors)
-
-
-def hour_places():
-    column = lax.broadcasted_iota(jnp.int32, (HOURS, COLS), 1)
-    row = lax.broadcasted_iota(jnp.int32, (HOURS, COLS), 0)
-    return (jnp.bitwise_and(column, HOURS - 1) == row).astype(F32).astype(BF16)
-
-
-def pair_kernel(net, code_a, code_b, power_a, power_b, given, given_a, given_b, level, coded):
-    step = pl.program_id(0)
-    place = hour_places()
-    here = lax.broadcasted_iota(jnp.int32, (8, 128), 0) == step
-    halves = []
-    for index, (code, power) in enumerate(((code_a, power_a), (code_b, power_b))):
-        row = jnp.sum(jnp.where(here, from_code(power[:, 0:128]), 0.0), axis=0, keepdims=True)
-        unit = unit_of(as_column(row))[0:HALF]
-        halves.append(net[index * HALF : index * HALF + HALF, :] + from_code(code[...]) * unit)
-    lane = lax.broadcasted_iota(jnp.int32, (HOURS, SHARE), 1)
-    total = given[0] + jnp.where(lane < HALF, given_a[0], given_b[0])
-    g0, g1, g2 = split3(jnp.transpose(total))
-    fixed = dot_nn(g0, place) + dot_nn(g1, place) + dot_nn(g2, place)
-    part = fixed * level[0:1, :] - jnp.concatenate(halves, axis=0)
+    sent = jax.ShapeDtypeStruct((PAIRS * HALF + 8, COLS), jnp.int16)
+    return pl.pallas_call(
+        send_kernel,
+        in_specs=[
+            pl.BlockSpec(memory_space=pltpu.SMEM),
+            whole,
+            whole,
+            whole,
+            pl.BlockSpec(memory_space=pl.ANY),
+        ],
+        out_specs=[whole, whole, whole],
+        out_shape=[jax.ShapeDtypeStruct((PAIRS, HOURS, SHARE), F32), sent, sent],
+        scratch_shapes=[
+            pltpu.VMEM((PAIRS * SHARE, COLS), F32),
+            pltpu.VMEM((8, COLS), F32),
+            pltpu.SemaphoreType.DMA(()),
+        ],
+        compiler_params=pltpu.CompilerParams(vmem_limit_bytes=WIDE),
+        name="sent_flow",
+    )(place, near(units), factors, near(level), other)
+
+
+def pair_kernel(net, code_a, code_b, power_a, power_b, given, level, coded):
+    here = lax.broadcasted_iota(jnp.int32, (8, 256), 0) == pl.program_id(0)
+    lane = lax.broadcasted_iota(jnp.int32, (1, 256), 1)
+    rows = [
+        jnp.sum(jnp.where(here, from_code(power[:, 0:256]), 0.0), axis=0, keepdims=True) for power in (power_a, power_b)
+    ]
+    unit = unit_of(as_column(jnp.where(lane < HALF, rows[0], rows[1])))[0:SHARE]
+    code = jnp.concatenate([from_code(code_a[...]), from_code(code_b[...])], axis=0)
+    part = over_columns(given[0], hour_places()) * level[0:1, :] - net[...] + code * unit
     power = powers_of(part)
     coded[0, 0:SHARE, :] = to_code(part, power)
     across = jnp.broadcast_to(as_row(power), (8, SHARE))
@@ -182,10 +209,9 @@
     coded[0, SHARE : SHARE + 8, :] = across.astype(jnp.int32).astype(jnp.int16)
 
 
-def pair_flow(net, code_a, code_b, given, given_a, given_b, level):
+def pair_flow(net, code_a, code_b, given, level):
     lines = pl.BlockSpec((HALF, COLS), lambda j: (j, 0))
     tail = pl.BlockSpec((8, COLS), lambda j: (PAIRS * HALF // 8, 0))
-    hours = pl.BlockSpec((1, HOURS, SHARE), lambda j: (j, 0, 0))
     return pl.pallas_call(
         pair_kernel,
         grid=(PAIRS,),
@@ -195,16 +221,14 @@
             lines,
             tail,
             tail,
-            hours,
-            hours,
-            hours,
+            pl.BlockSpec((1, HOURS, SHARE), lambda j: (j, 0, 0)),
             pl.BlockSpec((3, COLS), lambda j: (0, 0)),
         ],
         out_specs=pl.BlockSpec((1, SHARE + 8, COLS), lambda j: (j, 0, 0)),
-        out_shape=jax.ShapeDtypeStruct((PAIRS, SHARE + 8, COLS), jnp.int16),
-        compiler_params=pltpu.CompilerParams(vmem_limit_bytes=WIDE),
+        out_shape=pltpu.HBM((PAIRS, SHARE + 8, COLS), jnp.int16),
+        compiler_params=pltpu.CompilerParams(vmem_limit_bytes=VMEM),
         name="pair_flow",
-    )(net, code_a, code_b, code_a, code_b, given, given_a, given_b, level)
+    )(net, code_a, code_b, code_a, code_b, given, level)
 
 
 def excess_kernel(coded, limit, rows, current, target, out):
@@ -348,14 +372,9 @@
 ):
     place = lax.axis_index("bus")
     factors = near(shift_factors)
-    values = commitment.astype(F32) * unit_capacity[None, :]
-    units = jnp.concatenate([values, unit_bus.astype(F32)[None, :]], axis=0)
-    units = exchange(jnp.broadcast_to(units[None], (BUS_AXIS, 9, 512)), "bus")
-
+    units = exchange(packed_units(commitment, unit_capacity, unit_bus), "bus")
     parity = jnp.bitwise_and(place, 1)
-    keep, send_a, send_b = net_flow(parity.reshape(1), shift_factors, net_load.reshape(COLS, BUSES))
-    code_a = lax.ppermute(send_a, "bus", NEAR_A)
-    code_b = lax.ppermute(send_b, "bus", NEAR_B)
+    keep, other = net_flow(parity.reshape(1), shift_factors, net_load.reshape(COLS, BUSES))
     keep, dispatch_level, scenario_weight, cluster_id = lax.optimization_barrier(
         (keep, dispatch_level, scenario_weight, cluster_id)
     )
@@ -367,10 +386,10 @@
         ],
         axis=0,
     )
-    given, send = capacity_flow(place.reshape(1), units, factors)
-    given_a = lax.ppermute(send, "bus", NEAR_A)
-    given_b = lax.ppermute(send, "bus", NEAR_B)
-    coded = pair_flow(keep, code_a, code_b, given, given_a, given_b, rows)
+    given, send_a, send_b = sent_flow(place.reshape(1), units, factors, rows, other)
+    code_a = lax.ppermute(send_a, "bus", NEAR_A)
+    code_b = lax.ppermute(send_b, "bus", NEAR_B)
+    coded = pair_flow(keep, code_a, code_b, given, rows)
     received = lax.all_to_all(coded, "bus", 0, 0, axis_index_groups=SAME_PARITY, tiled=True)
 
     limit = lax.dynamic_slice_in_dim(line_limit, place * SHARE, SHARE, 0).reshape(SHARE, 1)

time: 138 us -> 133 us (0.964)
  starting transfers between devices: 34.8 us -> 28 us
  Pallas kernels: 17.3 us -> 20 us
    ppermute x2 -> x0, starting transfers between devices: 8.6 us -> none  [the longest x1 4.6 us: per_device(): given_b = lax.ppermute(send, 'bus', NEAR_B)]
    all_to_all x2, waiting for transfers between devices: 13.4 us -> 7.57 us  [exchange(): return lax.all_to_all(tiles, axis, 0, 0, tiled=True)]
    pallas_call x1 -> x2, Pallas kernels: 2.38 us -> 7.57 us  [the longest x1 6.14 us: sent_flow(): pl.pallas_call(send_kernel, in_specs=[pl.BlockSpec(memory_space=pltpu.SME...]
    all_to_all x2, starting transfers between devices: 11.8 us -> 16 us  [exchange(): return lax.all_to_all(tiles, axis, 0, 0, tiled=True)]
    ppermute x1, waiting for transfers between devices: 0.01 us -> 3.54 us  [per_device(): code_a = lax.ppermute(send_a, 'bus', NEAR_A)]
    ppermute x1, waiting for transfers between devices: 0.01 us -> 2.72 us  [per_device(): code_b = lax.ppermute(send_b, 'bus', NEAR_B)]
    pallas_call x1, Pallas kernels: 4.59 us -> 2.66 us  [pair_flow(): pl.pallas_call(pair_kernel, grid=(PAIRS,), in_specs=[pl.BlockSpec((SHARE,...]
    ppermute x1, starting transfers between devices: 4.01 us -> 2.09 us  [per_device(): code_a = lax.ppermute(send_a, 'bus', NEAR_A)]
  transfers between devices with their start and end apart: 7 -> 5, of which waited for: 4 -> 5; matrix products, arithmetic and copies ran while one was open for 3% -> 2% of each run, Pallas kernels for 2% -> 5%
where the time goes in v4:
time: 133 us; the launch traced here: 132 us
  blocking collectives  45.5 us (34%)
  waiting for transfers between devices  33.8 us (25%)
  starting transfers between devices  28 us (21%)
  Pallas kernels  20 us (15%)
  local copies, waits for them, and re-layouts  3.07 us (2%)
    all_to_all x2, blocking collectives, exchange(): return lax.all_to_all(tiles, axis, 0, 0, tiled=True)  45.5 us
    all_to_all x1, waiting for transfers between devices, per_device(): lax.all_to_all(coded, 'bus', 0, 0, axis_index_groups=SAME_PARITY, tiled=T...  20 us
    all_to_all x2, starting transfers between devices, exchange(): return lax.all_to_all(tiles, axis, 0, 0, tiled=True)  16 us
    all_to_all x2, waiting for transfers between devices, exchange(): return lax.all_to_all(tiles, axis, 0, 0, tiled=True)  7.57 us
    pallas_call x1, Pallas kernels, sent_flow(): pl.pallas_call(send_kernel, in_specs=[pl.BlockSpec(memory_space=pltpu.SME...  6.14 us
    all_to_all x1, starting transfers between devices, per_device(): lax.all_to_all(coded, 'bus', 0, 0, axis_index_groups=SAME_PARITY, tiled=T...  6.12 us
    pallas_call x1, Pallas kernels, net_flow(): pl.pallas_call(net_flow_kernel, grid=(PAIRS,), in_specs=[pl.BlockSpec(mem...  5.95 us
    ppermute x1, starting transfers between devices, per_device(): code_b = lax.ppermute(send_b, 'bus', NEAR_B)  3.76 us
  transfers between devices with their start and end apart: 5, of which 5 were waited for; matrix products, arithmetic and copies ran while one was open for 2% of the time, Pallas kernels for 5%

profile of v4, /device:TPU:1, one launch (start us, length us, event | category | flops | bytes accessed | tf_op | source)
XLA Modules:
  0.0 131.8 jit_solution(13818009475495540583)
XLA Ops:
  0.6 0.0 copy-start
  0.6 1.4 %units.1 = f32[8,40,128]{2,1,0:T(8,128)} custom-call(s32[8,512]{1,0:T(8,128)} %commitment.1, f32[1,512]{1,0:T(1,128)} %bitcast.16, s32[1,512]{1,0:T(1,128)} %bitcast.17), custom_call_target="tpu_custom_call" | custom-call | tf_op jit(solution)/shard_map/units/pallas_call | solution.py:90
  2.1 7.6 %all-to-all-start = ((f32[8,40,128]{2,1,0:T(8,128)}), f32[8,40,128]{2,1,0:T(8,128)S(1)}, u32[]{:S(2)}, u32[]{:S(2)}) async-start(f32[8,40,128]{2,1,0:T(8,128)} %units.1), calls=%async_computation | async-start | bytes 327680 | tf_op jit(solution)/shard_map/all_to_all | solution.py:353
  9.7 0.0 copy-start.7
  9.7 0.0 copy-start.5
  9.7 0.0 copy-start.4
  9.7 0.0 copy-start.1
  9.8 5.9 %net_flow.1 = (f32[768,512]{1,0:T(8,128)}, f32[768,512]{1,0:T(8,128)}) custom-call(s32[1]{0:T(128)} %bitcast.parity, bf16[1536,1024]{1,0:T(8,128)(2,1)} %factors.5, bf16[512,1024]{1,0:T(8,128)(2,1)} %bitcast.13), custom_call_target="tpu_custom_call" | custom-call | tf_op jit(solution)/shard_map/net_flow/pallas_call | solution.py:106
  15.7 0.0 copy-done.7
  15.7 0.1 broadcast_in_dim.10
  15.8 0.1 stack_reshape.11
  15.9 0.0 copy-done.5
  15.9 0.1 broadcast_in_dim.9
  16.0 0.1 stack_reshape.10
  16.1 0.0 copy-done.4
  16.1 0.1 copy.16
  16.2 0.1 stack_reshape.9
  16.3 1.8 %all-to-all-done.units = f32[8,40,128]{2,1,0:T(8,128)S(1)} async-done(((f32[8,40,128]{2,1,0:T(8,128)}), f32[8,40,128]{2,1,0:T(8,128)S(1)}, u32[]{:S(2)}, u32[]{:S(2)}) %all-to-all-start) | async-done | bytes 163872 | tf_op jit(solution)/shard_map/all_to_all | solution.py:353
  18.1 0.0 copy-done.1
  18.1 0.0 copy-start.2
  18.1 6.1 %sent_flow.1 = (f32[4,8,192]{2,1,0:T(8,128)}, s16[392,512]{1,0:T(8,128)(2,1)}, s16[392,512]{1,0:T(8,128)(2,1)}) custom-call(s32[1]{0:T(128)} %bitcast.2.place, f32[8,40,128]{2,1,0:T(8,128)S(1)} %all-to-all-done.units, bf16[1536,1024]{1,0:T(8,128)(2,1)S(1)} %copy-done.1, f32[3,512]{1,0:T(4,128)S(1)} %pad_maximum_fusion.level.rows, ...), custom_call_target="tpu_custom_call" | custom-call | tf_op jit(solution)/shard_map/sent_flow/pallas_call | solution.py:175
  24.3 2.1 %collective-permute-start = (s16[392,512]{1,0:T(8,128)(2,1)}, s16[392,512]{1,0:T(8,128)(2,1)S(1)}, u32[]{:S(2)}, u32[]{:S(2)}) collective-permute-start(s16[392,512]{1,0:T(8,128)(2,1)} %get-tuple-element.19), channel_id=1, source_target_pairs={{0,64},{64,0},{128,192},{192,128},{256,320},{320,256},{384,448},{4... | collective-permute-start | bytes 1204232 | tf_op jit(solution)/shard_map/ppermute | solution.py:390
  26.4 3.8 %collective-permute-start.1 = (s16[392,512]{1,0:T(8,128)(2,1)}, s16[392,512]{1,0:T(8,128)(2,1)S(1)}, u32[]{:S(2)}, u32[]{:S(2)}) collective-permute-start(s16[392,512]{1,0:T(8,128)(2,1)} %get-tuple-element.20), channel_id=1, source_target_pairs={{0,448},{64,128},{128,64},{192,256},{256,192},{320,384},{384,320},... | collective-permute-start | bytes 1204232 | tf_op jit(solution)/shard_map/ppermute | solution.py:391
  30.1 3.5 %collective-permute-done.code_a.power_a = s16[392,512]{1,0:T(8,128)(2,1)S(1)} collective-permute-done((s16[392,512]{1,0:T(8,128)(2,1)}, s16[392,512]{1,0:T(8,128)(2,1)S(1)}, u32[]{:S(2)}, u32[]{:S(2)}) %collective-permute-start) | collective-permute-done | bytes 401440 | tf_op jit(solution)/shard_map/ppermute | solution.py:390
  33.7 2.7 %collective-permute-done.1.code_b.power_b = s16[392,512]{1,0:T(8,128)(2,1)S(1)} collective-permute-done((s16[392,512]{1,0:T(8,128)(2,1)}, s16[392,512]{1,0:T(8,128)(2,1)S(1)}, u32[]{:S(2)}, u32[]{:S(2)}) %collective-permute-start.1) | collective-permute-done | bytes 401440 | tf_op jit(solution)/shard_map/ppermute | solution.py:391
  36.4 0.0 copy-done.2
  36.4 0.0 copy-start.3
  36.4 0.8 copy-done.3
  37.1 2.7 %pair_flow.1 = s16[4,200,512]{2,1,0:T(8,128)(2,1)} custom-call(f32[768,512]{1,0:T(8,128)S(1)} %copy-done.2, s16[392,512]{1,0:T(8,128)(2,1)S(1)} %collective-permute-done.code_a.power_a, s16[392,512]{1,0:T(8,128)(2,1)S(1)} %collective-permute-done.1.code_b.power_b, s16[392,512]{1,0:T(8,128)(2,1)S(1)} %collective-permute-done.code_a.power_a, ...), custom_call_target="tpu_custom_call" | custom-call | tf_op jit(solution)/shard_map/pair_flow/pallas_call | solution.py:215
  39.8 0.0 copy-start.6
  39.8 6.1 %all-to-all-start.1 = ((s16[4,200,512]{2,1,0:T(8,128)(2,1)}), s16[4,200,512]{2,1,0:T(8,128)(2,1)}, u32[]{:S(2)}, u32[]{:S(2)}) async-start(s16[4,200,512]{2,1,0:T(8,128)(2,1)} %pair_flow.1), calls=%async_computation.1 | async-start | bytes 1638400 | tf_op jit(solution)/shard_map/all_to_all | solution.py:393
  45.9 0.8 dynamic_slice.6
  46.7 0.1 copy.17.limit
  46.8 0.0 copy-done.6
  46.8 0.1 copy.18.target
  46.9 0.0 copy-done
  46.9 0.1 constant_dynamic-slice_fusion.current
  47.0 20.0 %all-to-all-done.1.coded = s16[4,200,512]{2,1,0:T(8,128)(2,1)} async-done(((s16[4,200,512]{2,1,0:T(8,128)(2,1)}), s16[4,200,512]{2,1,0:T(8,128)(2,1)}, u32[]{:S(2)}, u32[]{:S(2)}) %all-to-all-start.1) | async-done | bytes 819232 | tf_op jit(solution)/shard_map/all_to_all | solution.py:393
  67.0 2.3 %excess_sums.1 = f32[8,136,128]{2,1,0:T(8,128)S(1)} custom-call(s16[4,200,512]{2,1,0:T(8,128)(2,1)} %all-to-all-done.1.coded, f32[192,1]{1,0:T(8,128)S(1)} %copy.17.limit, f32[3,512]{1,0:T(4,128)S(1)} %pad_maximum_fusion.level.rows, f32[8,192]{1,0:T(8,128)S(1)} %constant_dynamic-slice_fusion.current, f32[8,1]{1,0:T(8,128)S(1)} %copy.18.target), custom_call_target="tpu_custom_call" | custom-call | tf_op jit(solution)/shard_map/excess_sums/pallas_call | solution.py:274
  69.2 27.8 %all_to_all.25.sums = f32[8,136,128]{2,1,0:T(8,128)S(1)} all-to-all(f32[8,136,128]{2,1,0:T(8,128)S(1)} %excess_sums.1), channel_id=1, replica_groups=mesh['bus'=8,'line'=8,'scen'=8] {'scen'}, dimensions={0} | all-to-all | bytes 1114112 | tf_op jit(solution)/shard_map/all_to_all | solution.py:353
  97.0 0.2 update.1
  97.2 17.7 %all_to_all.26.packed = f32[8,112,128]{2,1,0:T(8,128)S(1)} all-to-all(f32[8,112,128]{2,1,0:T(8,128)S(1)} %update.1), channel_id=1, replica_groups=mesh['bus'=8,'line'=8,'scen'=8] {'bus'}, dimensions={0} | all-to-all | bytes 917504 | tf_op jit(solution)/shard_map/all_to_all | solution.py:353
  114.9 1.4 %slopes.1 = (f32[64,1024]{1,0:T(8,128)}, f32[8,8,192]{2,1,0:T(8,128)S(1)}) custom-call(f32[8,112,128]{2,1,0:T(8,128)S(1)} %all_to_all.26.packed, bf16[1536,1024]{1,0:T(8,128)(2,1)S(1)} %copy-done.1), custom_call_target="tpu_custom_call" | custom-call | tf_op jit(solution)/shard_map/slopes/pallas_call | solution.py:334
  116.4 8.4 %all-to-all-start.4 = ((f32[8,8,1024]{2,1,0:T(8,128)}), f32[8,8,1024]{2,1,0:T(8,128)S(1)}, u32[]{:S(2)}, u32[]{:S(2)}) async-start(f32[8,8,1024]{2,1,0:T(8,128)} %bitcast.9), calls=%async_computation.4 | async-start | bytes 524288 | tf_op jit(solution)/shard_map/all_to_all | solution.py:353
  124.7 0.7 reshape.39
  125.4 5.7 %all-to-all-done.4 = f32[8,8,1024]{2,1,0:T(8,128)S(1)} async-done(((f32[8,8,1024]{2,1,0:T(8,128)}), f32[8,8,1024]{2,1,0:T(8,128)S(1)}, u32[]{:S(2)}, u32[]{:S(2)}) %all-to-all-start.4) | async-done | bytes 262176 | tf_op jit(solution)/shard_map/all_to_all | solution.py:353
  131.2 0.6 reduce_sum.9
  (3 shorter events, 0.0 us)
Async XLA Ops:
  0.6 46.3 %copy-start = (f32[8,1536]{1,0:T(8,128)S(1)}, f32[8,1536]{1,0:T(8,128)}, u32[]{:S(2)}) copy-start(f32[8,1536]{1,0:T(8,128)} %param.20) | copy-start | bytes 147460
  2.1 16.0 %all-to-all-start = ((f32[8,40,128]{2,1,0:T(8,128)}), f32[8,40,128]{2,1,0:T(8,128)S(1)}, u32[]{:S(2)}, u32[]{:S(2)}) async-start(f32[8,40,128]{2,1,0:T(8,128)} %units.1), calls=%async_computation | async-start | bytes 327680 | tf_op jit(solution)/shard_map/all_to_all | solution.py:353
  9.7 6.0 %copy-start.7 = (s32[64,1]{0,1:T(1,128)S(1)}, s32[64,1]{0,1:T(1,128)}, u32[]{:S(2)}) copy-start(s32[64,1]{0,1:T(1,128)} %param.15) | copy-start | bytes 772
  9.7 6.2 %copy-start.5 = (f32[64]{0:T(128)S(1)}, f32[64]{0:T(128)}, u32[]{:S(2)}) copy-start(f32[64]{0:T(128)} %param.14) | copy-start | bytes 772
  9.7 6.3 %copy-start.4 = (f32[64,8]{0,1:T(8,128)S(1)}, f32[64,8]{0,1:T(8,128)}, u32[]{:S(2)}) copy-start(f32[64,8]{0,1:T(8,128)} %param.13) | copy-start | bytes 6148
  9.7 8.4 %copy-start.1 = (bf16[1536,1024]{1,0:T(8,128)(2,1)S(1)}, bf16[1536,1024]{1,0:T(8,128)(2,1)}, u32[]{:S(2)}) copy-start(bf16[1536,1024]{1,0:T(8,128)(2,1)} %factors.5) | copy-start | bytes 9437188
  18.1 18.3 %copy-start.2 = (f32[768,512]{1,0:T(8,128)S(1)}, f32[768,512]{1,0:T(8,128)}, u32[]{:S(2)}) copy-start(f32[768,512]{1,0:T(8,128)} %get-tuple-element.14.net) | copy-start | bytes 4718596
  24.3 9.4 %collective-permute-start = (s16[392,512]{1,0:T(8,128)(2,1)}, s16[392,512]{1,0:T(8,128)(2,1)S(1)}, u32[]{:S(2)}, u32[]{:S(2)}) collective-permute-start(s16[392,512]{1,0:T(8,128)(2,1)} %get-tuple-element.19), channel_id=1, source_target_pairs={{0,64},{64,0},{128,192},{192,128},{256,320},{320,256},{384,448},{4... | collective-permute-start | bytes 1204232 | tf_op jit(solution)/shard_map/ppermute | solution.py:390
  26.4 10.0 %collective-permute-start.1 = (s16[392,512]{1,0:T(8,128)(2,1)}, s16[392,512]{1,0:T(8,128)(2,1)S(1)}, u32[]{:S(2)}, u32[]{:S(2)}) collective-permute-start(s16[392,512]{1,0:T(8,128)(2,1)} %get-tuple-element.20), channel_id=1, source_target_pairs={{0,448},{64,128},{128,64},{192,256},{256,192},{320,384},{384,320},... | collective-permute-start | bytes 1204232 | tf_op jit(solution)/shard_map/ppermute | solution.py:391
  36.4 0.8 copy-start.3
  39.8 7.0 %copy-start.6 = (f32[8]{0:T(128)S(1)}, f32[8]{0:T(128)}, u32[]{:S(2)}) copy-start(f32[8]{0:T(128)} %param.21) | copy-start | bytes 100
  39.8 27.1 %all-to-all-start.1 = ((s16[4,200,512]{2,1,0:T(8,128)(2,1)}), s16[4,200,512]{2,1,0:T(8,128)(2,1)}, u32[]{:S(2)}, u32[]{:S(2)}) async-start(s16[4,200,512]{2,1,0:T(8,128)(2,1)} %pair_flow.1), calls=%async_computation.1 | async-start | bytes 1638400 | tf_op jit(solution)/shard_map/all_to_all | solution.py:393
  116.4 14.8 %all-to-all-start.4 = ((f32[8,8,1024]{2,1,0:T(8,128)}), f32[8,8,1024]{2,1,0:T(8,128)S(1)}, u32[]{:S(2)}, u32[]{:S(2)}) async-start(f32[8,8,1024]{2,1,0:T(8,128)} %bitcast.9), calls=%async_computation.4 | async-start | bytes 524288 | tf_op jit(solution)/shard_map/all_to_all | solution.py:353

commit v5 on v4

--- a/solution.py
+++ b/solution.py
@@ -21,6 +21,9 @@
 ROWS = OWNED * HOURS
 STEP = 0.1
 CODE = 32000.0
+FINE = 60000.0
+POOLED = 176
+UPDATED = 128
 VMEM = 20 * 1024 * 1024
 WIDE = 56 * 1024 * 1024
 
@@ -53,8 +56,12 @@
     return jnp.ceil(jnp.log2(top) * 8.0)
 
 
+def rounded(x):
+    return jnp.floor(x + 0.5)
+
+
 def to_code(part, power):
-    return jnp.round(part * (jnp.exp2(power * -0.125) * CODE)).astype(jnp.int32).astype(jnp.int16)
+    return rounded(part * (jnp.exp2(power * -0.125) * CODE)).astype(jnp.int32).astype(jnp.int16)
 
 
 def from_code(code):
@@ -63,6 +70,28 @@
 
 def unit_of(power):
     return jnp.exp2(power * 0.125) * (1.0 / CODE)
+
+
+def coded_rows(rough, fine):
+    rough_power = powers_of(rough)
+    fine_power = powers_of(fine)
+    rough = rounded(rough * (jnp.exp2(rough_power * -0.125) * CODE))
+    fine = fine * (jnp.exp2(fine_power * -0.125) * CODE)
+    high = rounded(fine)
+    both = jnp.concatenate([rough, high, rounded((fine - high) * FINE)], axis=0)
+    half = both.shape[0] // 2
+    tail = jnp.concatenate([both[0:half, 128:SHARE], both[half:, 128:SHARE]], axis=1)
+    blank = jnp.zeros((128 - rough_power.shape[0] - fine_power.shape[0], 1), F32)
+    return jnp.concatenate([both[:, 0:128], tail], axis=0), jnp.concatenate([rough_power, fine_power, blank], axis=0)
+
+
+def decoded_rows(block, unit, count):
+    rows = ROWS + 2 * count
+    tail = block[rows : rows + rows // 2]
+    tail = jnp.concatenate([tail[:, 0:64], tail[:, 64:128]], axis=0)
+    both = jnp.concatenate([block[0:rows], tail], axis=1)
+    fine = both[ROWS : ROWS + count] + both[ROWS + count : rows] * (1.0 / FINE)
+    return both[0:ROWS] * unit[0:ROWS], fine * unit[ROWS : ROWS + count]
 
 
 def as_row(column):
@@ -259,15 +288,22 @@
     mine = jnp.where(inner < 8, inner * SCEN_AXIS + owner, owner * OWNED + inner - 8)
     pick = jnp.where(mine.astype(F32) == cluster, 1.0, 0.0).astype(BF16)
     pooled = dot_nt(pick, e0) + dot_nt(pick, e1)
+    lane = lax.broadcasted_iota(jnp.int32, (128, 128), 1)
     last = lax.broadcasted_iota(jnp.int32, (8, SHARE), 0)
+    table = jnp.zeros((128, 128), F32)
+    blocks = []
     for dest in range(SCEN_AXIS):
-        given = jnp.where(last == 0, current[dest : dest + 1, :], target[dest : dest + 1, 0:1])
-        both = jnp.concatenate(
-            [pushed[dest * ROWS : dest * ROWS + ROWS], pooled[dest * 16 : dest * 16 + 16], given], axis=0
+        given = jnp.where(last == 0, current[dest : dest + 1, :], jnp.where(last == 1, target[dest : dest + 1, 0:1], 0.0))
+        block, power = coded_rows(
+            pushed[dest * ROWS : dest * ROWS + ROWS],
+            jnp.concatenate([pooled[dest * 16 : dest * 16 + 16], given], axis=0),
         )
-        out[dest, 0:88, :] = both[:, 0:128]
-        right = jnp.concatenate([both[48:88, 128:192], both[80:88, 128:192]], axis=0)
-        out[dest, 88:136, :] = jnp.concatenate([both[0:48, 128:192], right], axis=1)
+        table = jnp.where(lane == dest, power, table)
+        blocks.append(block)
+    table = jnp.transpose(table)
+    for dest in range(SCEN_AXIS):
+        tail = jnp.broadcast_to(table[dest : dest + 1], (8, 128))
+        out[dest] = jnp.concatenate([blocks[dest], tail], axis=0).astype(jnp.int32).astype(jnp.int16)
 
 
 def excess_sums(coded, limit, rows, current, target):
@@ -275,36 +311,33 @@
         excess_kernel,
         in_specs=[pl.BlockSpec(memory_space=pltpu.VMEM)] * 5,
         out_specs=pl.BlockSpec(memory_space=pltpu.VMEM),
-        out_shape=pltpu.VMEM((SCEN_AXIS, 136, 128), F32),
+        out_shape=pltpu.VMEM((SCEN_AXIS, POOLED, 128), jnp.int16),
         compiler_params=pltpu.CompilerParams(vmem_limit_bytes=VMEM),
         name="excess_sums",
     )(near(coded), near(limit), near(rows), near(current), near(target))
 
 
 def update_kernel(sums, current, target, out):
-    total = sums[0]
-    for src in range(1, SCEN_AXIS):
-        total = total + sums[src]
-    tail = jnp.concatenate([total[88:136, 0:64], total[88:128, 64:128]], axis=0)
-    spread = jnp.concatenate(
-        [jnp.concatenate([sums[src, 80:81, :], sums[src, 120:121, 64:128]], axis=1) for src in range(OWNED)], axis=0
-    )
-    spread_target = jnp.concatenate([sums[src, 81:82, 0:1] for src in range(OWNED)], axis=0)
-    for part, lo, hi in ((total[0:80], 0, 128), (tail, 128, 192)):
-        chosen = jnp.maximum(
-            spread[:, lo:hi] + STEP * (part[64:72] - spread_target), 0.0
-        )
-        owned = jnp.maximum(current[:, lo:hi] + STEP * (part[72:80] - target[:, 0:1]), 0.0)
-        wide = jnp.concatenate(
-            [part[8 * i : 8 * i + 8] * chosen[i : i + 1] for i in range(OWNED)] + [owned], axis=0
-        )
-        if lo == 0:
-            for dest in range(BUS_AXIS):
-                out[dest, 0:72, :] = wide
-        else:
-            folded = jnp.concatenate([wide[0:40], jnp.concatenate([wide[40:72], wide[64:72]], axis=0)], axis=1)
-            for dest in range(BUS_AXIS):
-                out[dest, 72:112, :] = folded
+    tables = jnp.concatenate([from_code(sums[src, POOLED - 16 : POOLED, :])[15:16] for src in range(SCEN_AXIS)], axis=0)
+    units = unit_of(jnp.transpose(tables))
+    pushed = jnp.zeros((ROWS, SHARE), F32)
+    pooled = jnp.zeros((16, SHARE), F32)
+    given = []
+    for src in range(SCEN_AXIS):
+        rough, fine = decoded_rows(from_code(sums[src]), units[:, src : src + 1], 24)
+        pushed = pushed + rough
+        pooled = pooled + fine[0:16]
+        given.append(fine[16:24])
+    spread = jnp.concatenate([part[0:1] for part in given], axis=0)
+    spread_target = jnp.concatenate([part[1:2, 0:1] for part in given], axis=0)
+    chosen = jnp.maximum(spread + STEP * (pooled[0:8] - spread_target), 0.0)
+    owned = jnp.maximum(current[...] + STEP * (pooled[8:16] - target[:, 0:1]), 0.0)
+    wide = jnp.concatenate([pushed[8 * i : 8 * i + 8] * chosen[i : i + 1] for i in range(OWNED)], axis=0)
+    block, power = coded_rows(wide, owned)
+    tail = jnp.broadcast_to(as_row(power), (8, 128))
+    block = jnp.concatenate([block, tail], axis=0).astype(jnp.int32).astype(jnp.int16)
+    for dest in range(BUS_AXIS):
+        out[dest] = block
 
 
 def updated(sums, current, target):
@@ -312,20 +345,19 @@
         update_kernel,
         in_specs=[pl.BlockSpec(memory_space=pltpu.VMEM)] * 3,
         out_specs=pl.BlockSpec(memory_space=pltpu.VMEM),
-        out_shape=jax.ShapeDtypeStruct((BUS_AXIS, 112, 128), F32),
+        out_shape=jax.ShapeDtypeStruct((BUS_AXIS, UPDATED, 128), jnp.int16),
         compiler_params=pltpu.CompilerParams(vmem_limit_bytes=VMEM),
         name="update",
     )(near(sums), near(current), near(target))
 
 
 def slopes_kernel(packed, factors, slopes, duals):
+    tables = jnp.concatenate([from_code(packed[src, UPDATED - 16 : UPDATED, :])[15:16] for src in range(BUS_AXIS)], axis=0)
+    units = unit_of(jnp.transpose(tables))
     total = jnp.zeros((2 * ROWS, BUSES), F32)
     for src in range(BUS_AXIS):
-        tail = packed[src, 72:112, :]
-        tail = jnp.concatenate([tail[:, 0:64], tail[0:32, 64:128]], axis=0)
-        wide = jnp.concatenate([packed[src, 0:72, :], tail], axis=1)
-        duals[src] = wide[64:72]
-        pieces = jnp.concatenate(split2(wide[0:64]), axis=0)
+        wide, duals[src] = decoded_rows(from_code(packed[src]), units[:, src : src + 1], 8)
+        pieces = jnp.concatenate(split2(wide), axis=0)
         total = total + dot_nn(pieces, factors[src * SHARE : src * SHARE + SHARE, :])
     slopes[...] = total[0:ROWS] + total[ROWS:]
 

time: 133 us -> 126 us (0.947)
  blocking collectives: 45.5 us -> 37.9 us
  Pallas kernels: 20 us -> 21.7 us
    all_to_all x2, blocking collectives: 45.5 us -> 37.9 us  [exchange(): return lax.all_to_all(tiles, axis, 0, 0, tiled=True)]
where the time goes in v5:
time: 126 us; the launch traced here: 125 us
  blocking collectives  37.9 us (30%)
  waiting for transfers between devices  33.8 us (27%)
  starting transfers between devices  27.6 us (22%)
  Pallas kernels  21.7 us (17%)
  local copies, waits for them, and re-layouts  3.07 us (2%)
    all_to_all x2, blocking collectives, exchange(): return lax.all_to_all(tiles, axis, 0, 0, tiled=True)  37.9 us
    all_to_all x1, waiting for transfers between devices, per_device(): lax.all_to_all(coded, 'bus', 0, 0, axis_index_groups=SAME_PARITY, tiled=T...  20 us
    all_to_all x2, starting transfers between devices, exchange(): return lax.all_to_all(tiles, axis, 0, 0, tiled=True)  15.6 us
    all_to_all x2, waiting for transfers between devices, exchange(): return lax.all_to_all(tiles, axis, 0, 0, tiled=True)  7.57 us
    pallas_call x1, Pallas kernels, sent_flow(): pl.pallas_call(send_kernel, in_specs=[pl.BlockSpec(memory_space=pltpu.SME...  6.19 us
    all_to_all x1, starting transfers between devices, per_device(): lax.all_to_all(coded, 'bus', 0, 0, axis_index_groups=SAME_PARITY, tiled=T...  6.11 us
    pallas_call x1, Pallas kernels, net_flow(): pl.pallas_call(net_flow_kernel, grid=(PAIRS,), in_specs=[pl.BlockSpec(mem...  5.95 us
    ppermute x1, starting transfers between devices, per_device(): code_b = lax.ppermute(send_b, 'bus', NEAR_B)  3.76 us
  transfers between devices with their start and end apart: 5, of which 5 were waited for; matrix products, arithmetic and copies ran while one was open for 2% of the time, Pallas kernels for 5%

profile of v5, /device:TPU:1, one launch (start us, length us, event | category | flops | bytes accessed | tf_op | source)
XLA Modules:
  0.0 125.4 jit_solution(7423122405453897068)
XLA Ops:
  0.6 0.0 copy-start
  0.6 1.4 %units.1 = f32[8,40,128]{2,1,0:T(8,128)} custom-call(s32[8,512]{1,0:T(8,128)} %commitment.1, f32[1,512]{1,0:T(1,128)} %bitcast.16, s32[1,512]{1,0:T(1,128)} %bitcast.17), custom_call_target="tpu_custom_call" | custom-call | tf_op jit(solution)/shard_map/units/pallas_call | solution.py:119
  2.1 7.6 %all-to-all-start = ((f32[8,40,128]{2,1,0:T(8,128)}), f32[8,40,128]{2,1,0:T(8,128)S(1)}, u32[]{:S(2)}, u32[]{:S(2)}) async-start(f32[8,40,128]{2,1,0:T(8,128)} %units.1), calls=%async_computation | async-start | bytes 327680 | tf_op jit(solution)/shard_map/all_to_all | solution.py:385
  9.7 0.0 copy-start.7
  9.7 0.0 copy-start.5
  9.7 0.0 copy-start.4
  9.7 0.0 copy-start.1
  9.8 5.9 %net_flow.1 = (f32[768,512]{1,0:T(8,128)}, f32[768,512]{1,0:T(8,128)}) custom-call(s32[1]{0:T(128)} %bitcast.parity, bf16[1536,1024]{1,0:T(8,128)(2,1)} %factors.5, bf16[512,1024]{1,0:T(8,128)(2,1)} %bitcast.13), custom_call_target="tpu_custom_call" | custom-call | tf_op jit(solution)/shard_map/net_flow/pallas_call | solution.py:135
  15.7 0.0 copy-done.7
  15.7 0.1 broadcast_in_dim.10
  15.8 0.1 stack_reshape.11
  15.9 0.0 copy-done.5
  15.9 0.1 broadcast_in_dim.9
  16.0 0.1 stack_reshape.10
  16.1 0.0 copy-done.4
  16.1 0.1 copy.16
  16.2 0.1 stack_reshape.9
  16.3 1.8 %all-to-all-done.units = f32[8,40,128]{2,1,0:T(8,128)S(1)} async-done(((f32[8,40,128]{2,1,0:T(8,128)}), f32[8,40,128]{2,1,0:T(8,128)S(1)}, u32[]{:S(2)}, u32[]{:S(2)}) %all-to-all-start) | async-done | bytes 163872 | tf_op jit(solution)/shard_map/all_to_all | solution.py:385
  18.1 0.0 copy-done.1
  18.1 0.0 copy-start.2
  18.1 6.2 %sent_flow.1 = (f32[4,8,192]{2,1,0:T(8,128)}, s16[392,512]{1,0:T(8,128)(2,1)}, s16[392,512]{1,0:T(8,128)(2,1)}) custom-call(s32[1]{0:T(128)} %bitcast.2.place, f32[8,40,128]{2,1,0:T(8,128)S(1)} %all-to-all-done.units, bf16[1536,1024]{1,0:T(8,128)(2,1)S(1)} %copy-done.1, f32[3,512]{1,0:T(4,128)S(1)} %pad_maximum_fusion.level.rows, ...), custom_call_target="tpu_custom_call" | custom-call | tf_op jit(solution)/shard_map/sent_flow/pallas_call | solution.py:204
  24.3 2.1 %collective-permute-start = (s16[392,512]{1,0:T(8,128)(2,1)}, s16[392,512]{1,0:T(8,128)(2,1)S(1)}, u32[]{:S(2)}, u32[]{:S(2)}) collective-permute-start(s16[392,512]{1,0:T(8,128)(2,1)} %get-tuple-element.19), channel_id=1, source_target_pairs={{0,64},{64,0},{128,192},{192,128},{256,320},{320,256},{384,448},{4... | collective-permute-start | bytes 1204232 | tf_op jit(solution)/shard_map/ppermute | solution.py:422
  26.4 3.8 %collective-permute-start.1 = (s16[392,512]{1,0:T(8,128)(2,1)}, s16[392,512]{1,0:T(8,128)(2,1)S(1)}, u32[]{:S(2)}, u32[]{:S(2)}) collective-permute-start(s16[392,512]{1,0:T(8,128)(2,1)} %get-tuple-element.20), channel_id=1, source_target_pairs={{0,448},{64,128},{128,64},{192,256},{256,192},{320,384},{384,320},... | collective-permute-start | bytes 1204232 | tf_op jit(solution)/shard_map/ppermute | solution.py:423
  30.2 3.5 %collective-permute-done.code_a.power_a = s16[392,512]{1,0:T(8,128)(2,1)S(1)} collective-permute-done((s16[392,512]{1,0:T(8,128)(2,1)}, s16[392,512]{1,0:T(8,128)(2,1)S(1)}, u32[]{:S(2)}, u32[]{:S(2)}) %collective-permute-start) | collective-permute-done | bytes 401440 | tf_op jit(solution)/shard_map/ppermute | solution.py:422
  33.7 2.7 %collective-permute-done.1.code_b.power_b = s16[392,512]{1,0:T(8,128)(2,1)S(1)} collective-permute-done((s16[392,512]{1,0:T(8,128)(2,1)}, s16[392,512]{1,0:T(8,128)(2,1)S(1)}, u32[]{:S(2)}, u32[]{:S(2)}) %collective-permute-start.1) | collective-permute-done | bytes 401440 | tf_op jit(solution)/shard_map/ppermute | solution.py:423
  36.4 0.0 copy-done.2
  36.4 0.0 copy-start.3
  36.4 0.8 copy-done.3
  37.2 2.7 %pair_flow.1 = s16[4,200,512]{2,1,0:T(8,128)(2,1)} custom-call(f32[768,512]{1,0:T(8,128)S(1)} %copy-done.2, s16[392,512]{1,0:T(8,128)(2,1)S(1)} %collective-permute-done.code_a.power_a, s16[392,512]{1,0:T(8,128)(2,1)S(1)} %collective-permute-done.1.code_b.power_b, s16[392,512]{1,0:T(8,128)(2,1)S(1)} %collective-permute-done.code_a.power_a, ...), custom_call_target="tpu_custom_call" | custom-call | tf_op jit(solution)/shard_map/pair_flow/pallas_call | solution.py:244
  39.9 0.0 copy-start.6
  39.9 6.1 %all-to-all-start.1 = ((s16[4,200,512]{2,1,0:T(8,128)(2,1)}), s16[4,200,512]{2,1,0:T(8,128)(2,1)}, u32[]{:S(2)}, u32[]{:S(2)}) async-start(s16[4,200,512]{2,1,0:T(8,128)(2,1)} %pair_flow.1), calls=%async_computation.1 | async-start | bytes 1638400 | tf_op jit(solution)/shard_map/all_to_all | solution.py:425
  46.0 0.8 dynamic_slice.6
  46.8 0.1 copy.17.limit
  46.9 0.0 copy-done.6
  46.9 0.1 copy.18.target
  47.0 0.0 copy-done
  47.0 0.1 constant_dynamic-slice_fusion.current
  47.1 20.0 %all-to-all-done.1.coded = s16[4,200,512]{2,1,0:T(8,128)(2,1)} async-done(((s16[4,200,512]{2,1,0:T(8,128)(2,1)}), s16[4,200,512]{2,1,0:T(8,128)(2,1)}, u32[]{:S(2)}, u32[]{:S(2)}) %all-to-all-start.1) | async-done | bytes 819232 | tf_op jit(solution)/shard_map/all_to_all | solution.py:425
  67.1 3.2 %excess_sums.1 = s16[8,176,128]{2,1,0:T(8,128)(2,1)S(1)} custom-call(s16[4,200,512]{2,1,0:T(8,128)(2,1)} %all-to-all-done.1.coded, f32[192,1]{1,0:T(8,128)S(1)} %copy.17.limit, f32[3,512]{1,0:T(4,128)S(1)} %pad_maximum_fusion.level.rows, f32[8,192]{1,0:T(8,128)S(1)} %constant_dynamic-slice_fusion.current, f32[8,1]{1,0:T(8,128)S(1)} %copy.18.target), custom_call_target="tpu_custom_call" | custom-call | tf_op jit(solution)/shard_map/excess_sums/pallas_call | solution.py:310
  70.3 24.4 %all_to_all.25.sums = s16[8,176,128]{2,1,0:T(8,128)(2,1)S(1)} all-to-all(s16[8,176,128]{2,1,0:T(8,128)(2,1)S(1)} %excess_sums.1), channel_id=1, replica_groups=mesh['bus'=8,'line'=8,'scen'=8] {'scen'}, dimensions={0} | all-to-all | bytes 720896 | tf_op jit(solution)/shard_map/all_to_all | solution.py:385
  94.7 0.6 update.1
  95.2 13.5 %all_to_all.26.packed = s16[8,128,128]{2,1,0:T(8,128)(2,1)S(1)} all-to-all(s16[8,128,128]{2,1,0:T(8,128)(2,1)S(1)} %update.1), channel_id=1, replica_groups=mesh['bus'=8,'line'=8,'scen'=8] {'bus'}, dimensions={0} | all-to-all | bytes 524288 | tf_op jit(solution)/shard_map/all_to_all | solution.py:385
  108.8 1.5 %slopes.1 = (f32[64,1024]{1,0:T(8,128)}, f32[8,8,192]{2,1,0:T(8,128)S(1)}) custom-call(s16[8,128,128]{2,1,0:T(8,128)(2,1)S(1)} %all_to_all.26.packed, bf16[1536,1024]{1,0:T(8,128)(2,1)S(1)} %copy-done.1), custom_call_target="tpu_custom_call" | custom-call | tf_op jit(solution)/shard_map/slopes/pallas_call | solution.py:366
  110.3 8.0 %all-to-all-start.4 = ((f32[8,8,1024]{2,1,0:T(8,128)}), f32[8,8,1024]{2,1,0:T(8,128)S(1)}, u32[]{:S(2)}, u32[]{:S(2)}) async-start(f32[8,8,1024]{2,1,0:T(8,128)} %bitcast.9), calls=%async_computation.4 | async-start | bytes 524288 | tf_op jit(solution)/shard_map/all_to_all | solution.py:385
  118.3 0.7 reshape.39
  119.0 5.7 %all-to-all-done.4 = f32[8,8,1024]{2,1,0:T(8,128)S(1)} async-done(((f32[8,8,1024]{2,1,0:T(8,128)}), f32[8,8,1024]{2,1,0:T(8,128)S(1)}, u32[]{:S(2)}, u32[]{:S(2)}) %all-to-all-start.4) | async-done | bytes 262176 | tf_op jit(solution)/shard_map/all_to_all | solution.py:385
  124.8 0.6 reduce_sum.9
  (3 shorter events, 0.0 us)
Async XLA Ops:
  0.6 46.4 %copy-start = (f32[8,1536]{1,0:T(8,128)S(1)}, f32[8,1536]{1,0:T(8,128)}, u32[]{:S(2)}) copy-start(f32[8,1536]{1,0:T(8,128)} %param.20) | copy-start | bytes 147460
  2.1 16.0 %all-to-all-start = ((f32[8,40,128]{2,1,0:T(8,128)}), f32[8,40,128]{2,1,0:T(8,128)S(1)}, u32[]{:S(2)}, u32[]{:S(2)}) async-start(f32[8,40,128]{2,1,0:T(8,128)} %units.1), calls=%async_computation | async-start | bytes 327680 | tf_op jit(solution)/shard_map/all_to_all | solution.py:385
  9.7 6.0 %copy-start.7 = (s32[64,1]{0,1:T(1,128)S(1)}, s32[64,1]{0,1:T(1,128)}, u32[]{:S(2)}) copy-start(s32[64,1]{0,1:T(1,128)} %param.15) | copy-start | bytes 772
  9.7 6.2 %copy-start.5 = (f32[64]{0:T(128)S(1)}, f32[64]{0:T(128)}, u32[]{:S(2)}) copy-start(f32[64]{0:T(128)} %param.14) | copy-start | bytes 772
  9.7 6.3 %copy-start.4 = (f32[64,8]{0,1:T(8,128)S(1)}, f32[64,8]{0,1:T(8,128)}, u32[]{:S(2)}) copy-start(f32[64,8]{0,1:T(8,128)} %param.13) | copy-start | bytes 6148
  9.7 8.4 %copy-start.1 = (bf16[1536,1024]{1,0:T(8,128)(2,1)S(1)}, bf16[1536,1024]{1,0:T(8,128)(2,1)}, u32[]{:S(2)}) copy-start(bf16[1536,1024]{1,0:T(8,128)(2,1)} %factors.5) | copy-start | bytes 9437188
  18.1 18.3 %copy-start.2 = (f32[768,512]{1,0:T(8,128)S(1)}, f32[768,512]{1,0:T(8,128)}, u32[]{:S(2)}) copy-start(f32[768,512]{1,0:T(8,128)} %get-tuple-element.14.net) | copy-start | bytes 4718596
  24.3 9.4 %collective-permute-start = (s16[392,512]{1,0:T(8,128)(2,1)}, s16[392,512]{1,0:T(8,128)(2,1)S(1)}, u32[]{:S(2)}, u32[]{:S(2)}) collective-permute-start(s16[392,512]{1,0:T(8,128)(2,1)} %get-tuple-element.19), channel_id=1, source_target_pairs={{0,64},{64,0},{128,192},{192,128},{256,320},{320,256},{384,448},{4... | collective-permute-start | bytes 1204232 | tf_op jit(solution)/shard_map/ppermute | solution.py:422
  26.4 10.0 %collective-permute-start.1 = (s16[392,512]{1,0:T(8,128)(2,1)}, s16[392,512]{1,0:T(8,128)(2,1)S(1)}, u32[]{:S(2)}, u32[]{:S(2)}) collective-permute-start(s16[392,512]{1,0:T(8,128)(2,1)} %get-tuple-element.20), channel_id=1, source_target_pairs={{0,448},{64,128},{128,64},{192,256},{256,192},{320,384},{384,320},... | collective-permute-start | bytes 1204232 | tf_op jit(solution)/shard_map/ppermute | solution.py:423
  36.4 0.8 copy-start.3
  39.9 7.0 %copy-start.6 = (f32[8]{0:T(128)S(1)}, f32[8]{0:T(128)}, u32[]{:S(2)}) copy-start(f32[8]{0:T(128)} %param.21) | copy-start | bytes 100
  39.9 27.1 %all-to-all-start.1 = ((s16[4,200,512]{2,1,0:T(8,128)(2,1)}), s16[4,200,512]{2,1,0:T(8,128)(2,1)}, u32[]{:S(2)}, u32[]{:S(2)}) async-start(s16[4,200,512]{2,1,0:T(8,128)(2,1)} %pair_flow.1), calls=%async_computation.1 | async-start | bytes 1638400 | tf_op jit(solution)/shard_map/all_to_all | solution.py:425
  110.3 14.4 %all-to-all-start.4 = ((f32[8,8,1024]{2,1,0:T(8,128)}), f32[8,8,1024]{2,1,0:T(8,128)S(1)}, u32[]{:S(2)}, u32[]{:S(2)}) async-start(f32[8,8,1024]{2,1,0:T(8,128)} %bitcast.9), calls=%async_computation.4 | async-start | bytes 524288 | tf_op jit(solution)/shard_map/all_to_all | solution.py:385

commit v6 on v5

--- a/solution.py
+++ b/solution.py
@@ -51,9 +51,12 @@
     return high, mid, (rest - mid.astype(F32)).astype(BF16)
 
 
+def power_of(top):
+    return jnp.ceil(jnp.log2(jnp.maximum(top, 1e-30)) * 8.0)
+
+
 def powers_of(part):
-    top = jnp.maximum(jnp.max(jnp.abs(part), axis=1, keepdims=True), 1e-30)
-    return jnp.ceil(jnp.log2(top) * 8.0)
+    return power_of(jnp.max(jnp.abs(part), axis=1, keepdims=True))
 
 
 def rounded(x):
@@ -124,10 +127,12 @@
     )(commitment, capacity.reshape(1, 512), bus.reshape(1, 512))
 
 
-def net_flow_kernel(parity, factors, load, keep, other, work):
+def net_flow_kernel(parity, factors, load, keep, other, top, work):
     work[...] = dot_nt(factors[...], load[...])
     keep[...] = work[pl.ds(pl.multiple_of(parity[0] * SHARE, SHARE), SHARE), :]
-    other[...] = work[pl.ds(pl.multiple_of((1 - parity[0]) * SHARE, SHARE), SHARE), :]
+    part = work[pl.ds(pl.multiple_of((1 - parity[0]) * SHARE, SHARE), SHARE), :]
+    other[...] = part
+    top[...] = jnp.broadcast_to(jnp.max(jnp.abs(part), axis=1, keepdims=True), (SHARE, 128))
 
 
 def net_flow(parity, factors, load):
@@ -140,8 +145,8 @@
             pl.BlockSpec((2 * SHARE, BUSES), lambda j: (j, 0)),
             pl.BlockSpec((COLS, BUSES), lambda j: (0, 0)),
         ],
-        out_specs=[pl.BlockSpec((SHARE, COLS), lambda j: (j, 0))] * 2,
-        out_shape=[half, half],
+        out_specs=[pl.BlockSpec((SHARE, COLS), lambda j: (j, 0))] * 2 + [pl.BlockSpec((SHARE, 128), lambda j: (j, 0))],
+        out_shape=[half, half, jax.ShapeDtypeStruct((PAIRS * SHARE, 128), F32)],
         scratch_shapes=[pltpu.VMEM((2 * SHARE, COLS), F32)],
         compiler_params=pltpu.CompilerParams(vmem_limit_bytes=WIDE),
         name="net_flow",
@@ -154,14 +159,22 @@
     return (jnp.bitwise_and(column, HOURS - 1) == jnp.bitwise_and(row, HOURS - 1)).astype(F32).astype(BF16)
 
 
-def over_columns(given, place):
-    pieces = jnp.concatenate([piece.astype(F32) for piece in split3(given)], axis=0)
-    return dot_nn(jnp.transpose(pieces).astype(BF16), place)
-
-
-def send_kernel(place, units, factors, level, other, given, send_a, send_b, stage, powers, semaphore):
-    load = pltpu.make_async_copy(other, stage, semaphore)
-    load.start()
+def capacity_part(factors, capacity, place):
+    given = jnp.transpose(dot_nt(factors, capacity))
+    given = given[0:8] + given[8:16] + given[16:24]
+    largest = jnp.broadcast_to(jnp.max(jnp.abs(given), axis=0, keepdims=True), (8, SHARE))
+    pieces = jnp.concatenate([piece.astype(F32) for piece in split3(given)] + [largest], axis=0)
+    pieces = jnp.transpose(pieces)
+    return dot_nn(pieces[:, 0:24].astype(BF16), place), pieces[:, 24:25]
+
+
+def send_kernel(place, units, factors, level, other, top, capacity_out, send_a, send_b, stage, tops, powers, semaphores):
+    loads = (
+        pltpu.make_async_copy(other, stage, semaphores.at[0]),
+        pltpu.make_async_copy(top, tops, semaphores.at[1]),
+    )
+    for load in loads:
+        load.start()
     parity = jnp.bitwise_and(place[0], 1)
     first = (place[0] * BUSES).astype(F32)
     lows = lax.broadcasted_iota(jnp.int32, (128, 512), 0).astype(F32)
@@ -171,74 +184,99 @@
         local = jnp.concatenate([units[src, 32 + part : 33 + part, :] for part in range(4)], axis=1) - first
         high = jnp.floor(local * (1.0 / 128.0))
         low = local - high * 128.0
-        work = jnp.concatenate([jnp.where(high == float(block), values, 0.0) for block in range(8)], axis=0)
+        pieces = [piece.astype(F32) for piece in split3(values)]
+        work = [jnp.where(high == float(block), piece, 0.0) for piece in pieces for block in range(8)]
         match = jnp.where(lows == low, 1.0, 0.0).astype(BF16)
-        total = total + dot_nt(jnp.concatenate(split3(work), axis=0), match)
+        total = total + dot_nt(jnp.concatenate(work, axis=0).astype(BF16), match)
     total = total[0:64] + total[64:128] + total[128:192]
     capacity = jnp.concatenate([total[8 * block : 8 * block + 8] for block in range(8)], axis=1)
     capacity = jnp.concatenate(split3(capacity), axis=0)
+    capacity_out[...] = capacity.astype(F32)
     spread = hour_places()
+    most = jnp.max(jnp.abs(level[0:1, :]), axis=1, keepdims=True)
     powers[...] = jnp.zeros_like(powers)
-    load.wait()
+    for load in loads:
+        load.wait()
     for pair in range(PAIRS):
-        halves = []
-        for side in (parity, 1 - parity):
-            row = pl.multiple_of((2 * pair + side) * SHARE, SHARE)
-            part = jnp.transpose(dot_nt(factors[pl.ds(row, SHARE), :], capacity))
-            halves.append(part[0:8] + part[8:16] + part[16:24])
-        given[pair] = halves[0]
-        part = over_columns(halves[1], spread) * level[0:1, :] - stage[pair * SHARE : pair * SHARE + SHARE, :]
-        power = powers_of(part)
-        code = to_code(part, power)
-        across = as_row(power)
+        row = pl.multiple_of((2 * pair + 1 - parity) * SHARE, SHARE)
+        fixed, largest = capacity_part(factors[pl.ds(row, SHARE), :], capacity, spread)
+        rows = slice(pair * SHARE, pair * SHARE + SHARE)
+        power = power_of(tops[rows, 0:1] + largest * most)
+        code = to_code(fixed * level[0:1, :] - stage[rows, :], power)
         for index, out in enumerate((send_a, send_b)):
             out[pair * HALF : pair * HALF + HALF, :] = code[index * HALF : index * HALF + HALF]
-        powers[pair : pair + 1, 0:SHARE] = across
+        powers[pair : pair + 1, 0:SHARE] = as_row(power)
     for out in (send_a, send_b):
         out[PAIRS * HALF : PAIRS * HALF + 8, :] = powers[...].astype(jnp.int32).astype(jnp.int16)
 
 
-def sent_flow(place, units, factors, level, other):
+def sent_flow(place, units, factors, level, other, top):
     whole = pl.BlockSpec(memory_space=pltpu.VMEM)
+    anywhere = pl.BlockSpec(memory_space=pl.ANY)
     sent = jax.ShapeDtypeStruct((PAIRS * HALF + 8, COLS), jnp.int16)
     return pl.pallas_call(
         send_kernel,
+        in_specs=[pl.BlockSpec(memory_space=pltpu.SMEM), whole, whole, whole, anywhere, anywhere],
+        out_specs=[whole, whole, whole],
+        out_shape=[pltpu.VMEM((3 * HOURS, BUSES), F32), sent, sent],
+        scratch_shapes=[
+            pltpu.VMEM((PAIRS * SHARE, COLS), F32),
+            pltpu.VMEM((PAIRS * SHARE, 128), F32),
+            pltpu.VMEM((8, COLS), F32),
+            pltpu.SemaphoreType.DMA((2,)),
+        ],
+        compiler_params=pltpu.CompilerParams(vmem_limit_bytes=WIDE),
+        name="sent_flow",
+    )(place, near(units), factors, near(level), other, top)
+
+
+def kept_kernel(place, capacity, factors, net, level, out, top):
+    side = 2 * pl.program_id(0) + jnp.bitwise_and(place[0], 1)
+    rows = pl.ds(pl.multiple_of(side * SHARE, SHARE), SHARE)
+    fixed, _ = capacity_part(factors[rows, :], capacity[...].astype(BF16), hour_places())
+    part = fixed * level[0:1, :] - net[...]
+    out[...] = part
+    top[...] = jnp.broadcast_to(jnp.max(jnp.abs(part), axis=1, keepdims=True), (SHARE, 128))
+
+
+def kept_flow(place, capacity, factors, net, level):
+    whole = pl.BlockSpec(memory_space=pltpu.VMEM)
+    return pl.pallas_call(
+        kept_kernel,
+        grid=(PAIRS,),
         in_specs=[
             pl.BlockSpec(memory_space=pltpu.SMEM),
             whole,
             whole,
+            pl.BlockSpec((SHARE, COLS), lambda j: (j, 0)),
             whole,
-            pl.BlockSpec(memory_space=pl.ANY),
-        ],
-        out_specs=[whole, whole, whole],
-        out_shape=[jax.ShapeDtypeStruct((PAIRS, HOURS, SHARE), F32), sent, sent],
-        scratch_shapes=[
+        ],
+        out_specs=[pl.BlockSpec((SHARE, COLS), lambda j: (j, 0)), pl.BlockSpec((SHARE, 128), lambda j: (j, 0))],
+        out_shape=[
             pltpu.VMEM((PAIRS * SHARE, COLS), F32),
-            pltpu.VMEM((8, COLS), F32),
-            pltpu.SemaphoreType.DMA(()),
-        ],
-        compiler_params=pltpu.CompilerParams(vmem_limit_bytes=WIDE),
-        name="sent_flow",
-    )(place, near(units), factors, near(level), other)
-
-
-def pair_kernel(net, code_a, code_b, power_a, power_b, given, level, coded):
+            pltpu.VMEM((PAIRS * SHARE, 128), F32),
+        ],
+        compiler_params=pltpu.CompilerParams(vmem_limit_bytes=VMEM),
+        name="kept_flow",
+    )(place, near(capacity), factors, net, near(level))
+
+
+def pair_kernel(part, top, code_a, code_b, power_a, power_b, coded):
     here = lax.broadcasted_iota(jnp.int32, (8, 256), 0) == pl.program_id(0)
     lane = lax.broadcasted_iota(jnp.int32, (1, 256), 1)
     rows = [
         jnp.sum(jnp.where(here, from_code(power[:, 0:256]), 0.0), axis=0, keepdims=True) for power in (power_a, power_b)
     ]
     unit = unit_of(as_column(jnp.where(lane < HALF, rows[0], rows[1])))[0:SHARE]
+    power = power_of(top[:, 0:1] + unit * CODE)
     code = jnp.concatenate([from_code(code_a[...]), from_code(code_b[...])], axis=0)
-    part = over_columns(given[0], hour_places()) * level[0:1, :] - net[...] + code * unit
-    power = powers_of(part)
-    coded[0, 0:SHARE, :] = to_code(part, power)
+    coded[0, 0:SHARE, :] = to_code(part[...] + code * unit, power)
     across = jnp.broadcast_to(as_row(power), (8, SHARE))
     across = jnp.concatenate([across, jnp.zeros((8, COLS - SHARE), F32)], axis=1)
     coded[0, SHARE : SHARE + 8, :] = across.astype(jnp.int32).astype(jnp.int16)
 
 
-def pair_flow(net, code_a, code_b, given, level):
+def pair_flow(part, top, code_a, code_b):
     lines = pl.BlockSpec((HALF, COLS), lambda j: (j, 0))
     tail = pl.BlockSpec((8, COLS), lambda j: (PAIRS * HALF // 8, 0))
     return pl.pallas_call(
@@ -246,18 +284,17 @@
         grid=(PAIRS,),
         in_specs=[
             pl.BlockSpec((SHARE, COLS), lambda j: (j, 0)),
+            pl.BlockSpec((SHARE, 128), lambda j: (j, 0)),
             lines,
             lines,
             tail,
             tail,
-            pl.BlockSpec((1, HOURS, SHARE), lambda j: (j, 0, 0)),
-            pl.BlockSpec((3, COLS), lambda j: (0, 0)),
         ],
         out_specs=pl.BlockSpec((1, SHARE + 8, COLS), lambda j: (j, 0, 0)),
         out_shape=pltpu.HBM((PAIRS, SHARE + 8, COLS), jnp.int16),
         compiler_params=pltpu.CompilerParams(vmem_limit_bytes=VMEM),
         name="pair_flow",
-    )(net, code_a, code_b, code_a, code_b, given, level)
+    )(part, top, code_a, code_b, code_a, code_b)
 
 
 def excess_kernel(coded, limit, rows, current, target, out):
@@ -406,7 +443,7 @@
     factors = near(shift_factors)
     units = exchange(packed_units(commitment, unit_capacity, unit_bus), "bus")
     parity = jnp.bitwise_and(place, 1)
-    keep, other = net_flow(parity.reshape(1), shift_factors, net_load.reshape(COLS, BUSES))
+    keep, other, top = net_flow(parity.reshape(1), shift_factors, net_load.reshape(COLS, BUSES))
     keep, dispatch_level, scenario_weight, cluster_id = lax.optimization_barrier(
         (keep, dispatch_level, scenario_weight, cluster_id)
     )
@@ -418,10 +455,11 @@
         ],
         axis=0,
     )
-    given, send_a, send_b = sent_flow(place.reshape(1), units, factors, rows, other)
+    capacity, send_a, send_b = sent_flow(place.reshape(1), units, factors, rows, other, top)
     code_a = lax.ppermute(send_a, "bus", NEAR_A)
     code_b = lax.ppermute(send_b, "bus", NEAR_B)
-    coded = pair_flow(keep, code_a, code_b, given, rows)
+    part, top = kept_flow(place.reshape(1), capacity, factors, keep, rows)
+    coded = pair_flow(part, top, code_a, code_b)
     received = lax.all_to_all(coded, "bus", 0, 0, axis_index_groups=SAME_PARITY, tiled=True)
 
     limit = lax.dynamic_slice_in_dim(line_limit, place * SHARE, SHARE, 0).reshape(SHARE, 1)

time: 126 us -> 125 us (level)
  waiting for transfers between devices: 33.8 us -> 30.3 us
  Pallas kernels: 21.7 us -> 23.9 us
    ppermute x1, waiting for transfers between devices: 3.54 us -> 0.25 us  [per_device(): code_a = lax.ppermute(send_a, 'bus', NEAR_A)]
    pallas_call x0 -> x1, Pallas kernels: none -> 3.09 us  [kept_flow(): pl.pallas_call(kept_kernel, grid=(PAIRS,), in_specs=[pl.BlockSpec(memory_...]
  transfers between devices with their start and end apart: 5 -> 5, of which waited for: 5 -> 5; matrix products, arithmetic and copies ran while one was open for 2% -> 2% of each run, Pallas kernels for 5% -> 7%
where the time goes in v6:
time: 125 us; the launch traced here: 124 us
  blocking collectives  38 us (30%)
  waiting for transfers between devices  30.3 us (24%)
  starting transfers between devices  28 us (22%)
  Pallas kernels  23.9 us (19%)
  local copies, waits for them, and re-layouts  2.31 us (2%)
    all_to_all x2, blocking collectives, exchange(): return lax.all_to_all(tiles, axis, 0, 0, tiled=True)  38 us
    all_to_all x1, waiting for transfers between devices, per_device(): lax.all_to_all(coded, 'bus', 0, 0, axis_index_groups=SAME_PARITY, tiled=T...  19.9 us
    all_to_all x2, starting transfers between devices, exchange(): return lax.all_to_all(tiles, axis, 0, 0, tiled=True)  15.6 us
    all_to_all x2, waiting for transfers between devices, exchange(): return lax.all_to_all(tiles, axis, 0, 0, tiled=True)  7.39 us
    all_to_all x1, starting transfers between devices, per_device(): lax.all_to_all(coded, 'bus', 0, 0, axis_index_groups=SAME_PARITY, tiled=T...  6.31 us
    pallas_call x1, Pallas kernels, net_flow(): pl.pallas_call(net_flow_kernel, grid=(PAIRS,), in_specs=[pl.BlockSpec(mem...  6.13 us
    pallas_call x1, Pallas kernels, sent_flow(): pl.pallas_call(send_kernel, in_specs=[pl.BlockSpec(memory_space=pltpu.SME...  5.7 us
    ppermute x1, starting transfers between devices, per_device(): code_b = lax.ppermute(send_b, 'bus', NEAR_B)  3.94 us
  transfers between devices with their start and end apart: 5, of which 5 were waited for; matrix products, arithmetic and copies ran while one was open for 2% of the time, Pallas kernels for 7%

profile of v6, /device:TPU:1, one launch (start us, length us, event | category | flops | bytes accessed | tf_op | source)
XLA Modules:
  0.0 123.9 jit_solution(4672558677802200811)
XLA Ops:
  0.6 0.0 copy-start
  0.6 1.4 %units.1 = f32[8,40,128]{2,1,0:T(8,128)} custom-call(s32[8,512]{1,0:T(8,128)} %commitment.1, f32[1,512]{1,0:T(1,128)} %bitcast.16, s32[1,512]{1,0:T(1,128)} %bitcast.17), custom_call_target="tpu_custom_call" | custom-call | tf_op jit(solution)/shard_map/units/pallas_call | solution.py:122
  2.1 7.6 %all-to-all-start = ((f32[8,40,128]{2,1,0:T(8,128)}), f32[8,40,128]{2,1,0:T(8,128)S(1)}, u32[]{:S(2)}, u32[]{:S(2)}) async-start(f32[8,40,128]{2,1,0:T(8,128)} %units.1), calls=%async_computation | async-start | bytes 327680 | tf_op jit(solution)/shard_map/all_to_all | solution.py:422
  9.7 0.0 copy-start.6
  9.7 0.0 copy-start.4
  9.7 0.0 copy-start.3
  9.7 0.0 copy-start.1
  9.8 6.1 %net_flow.1 = (f32[768,512]{1,0:T(8,128)}, f32[768,512]{1,0:T(8,128)}, f32[768,128]{1,0:T(8,128)}) custom-call(s32[1]{0:T(128)} %bitcast.3.parity, bf16[1536,1024]{1,0:T(8,128)(2,1)} %factors.7, bf16[512,1024]{1,0:T(8,128)(2,1)} %bitcast.13), custom_call_target="tpu_custom_call" | custom-call | tf_op jit(solution)/shard_map/net_flow/pallas_call | solution.py:140
  15.9 0.0 copy-done.6
  15.9 0.1 broadcast_in_dim.10
  16.0 0.1 stack_reshape.11
  16.1 0.0 copy-done.4
  16.1 0.1 broadcast_in_dim.9
  16.1 0.1 stack_reshape.10
  16.2 0.0 copy-done.3
  16.2 0.1 copy.16
  16.3 0.1 stack_reshape.9
  16.4 1.6 %all-to-all-done.units = f32[8,40,128]{2,1,0:T(8,128)S(1)} async-done(((f32[8,40,128]{2,1,0:T(8,128)}), f32[8,40,128]{2,1,0:T(8,128)S(1)}, u32[]{:S(2)}, u32[]{:S(2)}) %all-to-all-start) | async-done | bytes 163872 | tf_op jit(solution)/shard_map/all_to_all | solution.py:422
  18.1 0.0 copy-done.1
  18.1 0.0 copy-start.2
  18.1 5.7 %sent_flow.1 = (f32[24,1024]{1,0:T(8,128)S(1)}, s16[392,512]{1,0:T(8,128)(2,1)}, s16[392,512]{1,0:T(8,128)(2,1)}) custom-call(s32[1]{0:T(128)} %bitcast.place, f32[8,40,128]{2,1,0:T(8,128)S(1)} %all-to-all-done.units, bf16[1536,1024]{1,0:T(8,128)(2,1)S(1)} %copy-done.1, f32[3,512]{1,0:T(4,128)S(1)} %pad_maximum_fusion.level.rows, ...), custom_call_target="tpu_custom_call" | custom-call | tf_op jit(solution)/shard_map/sent_flow/pallas_call | solution.py:217
  23.8 2.1 %collective-permute-start = (s16[392,512]{1,0:T(8,128)(2,1)}, s16[392,512]{1,0:T(8,128)(2,1)S(1)}, u32[]{:S(2)}, u32[]{:S(2)}) collective-permute-start(s16[392,512]{1,0:T(8,128)(2,1)} %get-tuple-element.26), channel_id=1, source_target_pairs={{0,64},{64,0},{128,192},{192,128},{256,320},{320,256},{384,448},{4... | collective-permute-start | bytes 1204232 | tf_op jit(solution)/shard_map/ppermute | solution.py:459
  25.9 3.9 %collective-permute-start.1 = (s16[392,512]{1,0:T(8,128)(2,1)}, s16[392,512]{1,0:T(8,128)(2,1)S(1)}, u32[]{:S(2)}, u32[]{:S(2)}) collective-permute-start(s16[392,512]{1,0:T(8,128)(2,1)} %get-tuple-element.27), channel_id=1, source_target_pairs={{0,448},{64,128},{128,64},{192,256},{256,192},{320,384},{384,320},... | collective-permute-start | bytes 1204232 | tf_op jit(solution)/shard_map/ppermute | solution.py:460
  29.9 0.0 copy-done.2
  29.9 3.1 %kept_flow.1 = (f32[768,512]{1,0:T(8,128)S(1)}, f32[768,128]{1,0:T(8,128)S(1)}) custom-call(s32[1]{0:T(128)} %bitcast.place, f32[24,1024]{1,0:T(8,128)S(1)} %get-tuple-element.22.capacity, bf16[1536,1024]{1,0:T(8,128)(2,1)S(1)} %copy-done.1, f32[768,512]{1,0:T(8,128)S(1)} %copy-done.2, f32[3,512]{1,0:T(4,128)S(1)} %pad_maximum_fusion.level.rows), custom_call_target="tpu_custom_call" | custom-call | tf_op jit(solution)/shard_map/kept_flow/pallas_call | solution.py:244
  33.0 0.3 collective-permute-done.code_a.power_a
  33.2 2.7 %collective-permute-done.1.code_b.power_b = s16[392,512]{1,0:T(8,128)(2,1)S(1)} collective-permute-done((s16[392,512]{1,0:T(8,128)(2,1)}, s16[392,512]{1,0:T(8,128)(2,1)S(1)}, u32[]{:S(2)}, u32[]{:S(2)}) %collective-permute-start.1) | collective-permute-done | bytes 401440 | tf_op jit(solution)/shard_map/ppermute | solution.py:460
  35.9 2.2 %pair_flow.1 = s16[4,200,512]{2,1,0:T(8,128)(2,1)} custom-call(f32[768,512]{1,0:T(8,128)S(1)} %get-tuple-element.24.part, f32[768,128]{1,0:T(8,128)S(1)} %get-tuple-element.25.top, s16[392,512]{1,0:T(8,128)(2,1)S(1)} %collective-permute-done.code_a.power_a, s16[392,512]{1,0:T(8,128)(2,1)S(1)} %collective-permute-done.1.code_b.power_b, ...), custom_call_target="tpu_custom_call" | custom-call | tf_op jit(solution)/shard_map/pair_flow/pallas_call | solution.py:282
  38.1 0.0 copy-start.5
  38.1 6.3 %all-to-all-start.1 = ((s16[4,200,512]{2,1,0:T(8,128)(2,1)}), s16[4,200,512]{2,1,0:T(8,128)(2,1)}, u32[]{:S(2)}, u32[]{:S(2)}) async-start(s16[4,200,512]{2,1,0:T(8,128)(2,1)} %pair_flow.1), calls=%async_computation.1 | async-start | bytes 1638400 | tf_op jit(solution)/shard_map/all_to_all | solution.py:463
  44.4 0.8 dynamic_slice.6
  45.2 0.1 copy.17.limit
  45.3 0.0 copy-done.5
  45.4 0.1 copy.18.target
  45.4 0.0 copy-done
  45.4 0.1 constant_dynamic-slice_fusion.current
  45.5 19.9 %all-to-all-done.1.coded = s16[4,200,512]{2,1,0:T(8,128)(2,1)} async-done(((s16[4,200,512]{2,1,0:T(8,128)(2,1)}), s16[4,200,512]{2,1,0:T(8,128)(2,1)}, u32[]{:S(2)}, u32[]{:S(2)}) %all-to-all-start.1) | async-done | bytes 819232 | tf_op jit(solution)/shard_map/all_to_all | solution.py:463
  65.4 3.2 %excess_sums.1 = s16[8,176,128]{2,1,0:T(8,128)(2,1)S(1)} custom-call(s16[4,200,512]{2,1,0:T(8,128)(2,1)} %all-to-all-done.1.coded, f32[192,1]{1,0:T(8,128)S(1)} %copy.17.limit, f32[3,512]{1,0:T(4,128)S(1)} %pad_maximum_fusion.level.rows, f32[8,192]{1,0:T(8,128)S(1)} %constant_dynamic-slice_fusion.current, f32[8,1]{1,0:T(8,128)S(1)} %copy.18.target), custom_call_target="tpu_custom_call" | custom-call | tf_op jit(solution)/shard_map/excess_sums/pallas_call | solution.py:347
  68.7 24.4 %all_to_all.25.sums = s16[8,176,128]{2,1,0:T(8,128)(2,1)S(1)} all-to-all(s16[8,176,128]{2,1,0:T(8,128)(2,1)S(1)} %excess_sums.1), channel_id=1, replica_groups=mesh['bus'=8,'line'=8,'scen'=8] {'scen'}, dimensions={0} | all-to-all | bytes 720896 | tf_op jit(solution)/shard_map/all_to_all | solution.py:422
  93.1 0.6 update.1
  93.6 13.6 %all_to_all.26.packed = s16[8,128,128]{2,1,0:T(8,128)(2,1)S(1)} all-to-all(s16[8,128,128]{2,1,0:T(8,128)(2,1)S(1)} %update.1), channel_id=1, replica_groups=mesh['bus'=8,'line'=8,'scen'=8] {'bus'}, dimensions={0} | all-to-all | bytes 524288 | tf_op jit(solution)/shard_map/all_to_all | solution.py:422
  107.2 1.5 %slopes.1 = (f32[64,1024]{1,0:T(8,128)}, f32[8,8,192]{2,1,0:T(8,128)S(1)}) custom-call(s16[8,128,128]{2,1,0:T(8,128)(2,1)S(1)} %all_to_all.26.packed, bf16[1536,1024]{1,0:T(8,128)(2,1)S(1)} %copy-done.1), custom_call_target="tpu_custom_call" | custom-call | tf_op jit(solution)/shard_map/slopes/pallas_call | solution.py:403
  108.8 8.0 %all-to-all-start.4 = ((f32[8,8,1024]{2,1,0:T(8,128)}), f32[8,8,1024]{2,1,0:T(8,128)S(1)}, u32[]{:S(2)}, u32[]{:S(2)}) async-start(f32[8,8,1024]{2,1,0:T(8,128)} %bitcast.9), calls=%async_computation.4 | async-start | bytes 524288 | tf_op jit(solution)/shard_map/all_to_all | solution.py:422
  116.8 0.7 reshape.40
  117.5 5.7 %all-to-all-done.4 = f32[8,8,1024]{2,1,0:T(8,128)S(1)} async-done(((f32[8,8,1024]{2,1,0:T(8,128)}), f32[8,8,1024]{2,1,0:T(8,128)S(1)}, u32[]{:S(2)}, u32[]{:S(2)}) %all-to-all-start.4) | async-done | bytes 262176 | tf_op jit(solution)/shard_map/all_to_all | solution.py:422
  123.2 0.6 reduce_sum.9
  (3 shorter events, 0.0 us)
Async XLA Ops:
  0.6 44.8 %copy-start = (f32[8,1536]{1,0:T(8,128)S(1)}, f32[8,1536]{1,0:T(8,128)}, u32[]{:S(2)}) copy-start(f32[8,1536]{1,0:T(8,128)} %param.20) | copy-start | bytes 147460
  2.1 16.0 %all-to-all-start = ((f32[8,40,128]{2,1,0:T(8,128)}), f32[8,40,128]{2,1,0:T(8,128)S(1)}, u32[]{:S(2)}, u32[]{:S(2)}) async-start(f32[8,40,128]{2,1,0:T(8,128)} %units.1), calls=%async_computation | async-start | bytes 327680 | tf_op jit(solution)/shard_map/all_to_all | solution.py:422
  9.7 6.2 %copy-start.6 = (s32[64,1]{0,1:T(1,128)S(1)}, s32[64,1]{0,1:T(1,128)}, u32[]{:S(2)}) copy-start(s32[64,1]{0,1:T(1,128)} %param.15) | copy-start | bytes 772
  9.7 6.3 %copy-start.4 = (f32[64]{0:T(128)S(1)}, f32[64]{0:T(128)}, u32[]{:S(2)}) copy-start(f32[64]{0:T(128)} %param.14) | copy-start | bytes 772
  9.7 6.5 %copy-start.3 = (f32[64,8]{0,1:T(8,128)S(1)}, f32[64,8]{0,1:T(8,128)}, u32[]{:S(2)}) copy-start(f32[64,8]{0,1:T(8,128)} %param.13) | copy-start | bytes 6148
  9.7 8.4 %copy-start.1 = (bf16[1536,1024]{1,0:T(8,128)(2,1)S(1)}, bf16[1536,1024]{1,0:T(8,128)(2,1)}, u32[]{:S(2)}) copy-start(bf16[1536,1024]{1,0:T(8,128)(2,1)} %factors.7) | copy-start | bytes 9437188
  18.1 11.8 %copy-start.2 = (f32[768,512]{1,0:T(8,128)S(1)}, f32[768,512]{1,0:T(8,128)}, u32[]{:S(2)}) copy-start(f32[768,512]{1,0:T(8,128)} %get-tuple-element.23.net) | copy-start | bytes 4718596
  23.8 9.4 %collective-permute-start = (s16[392,512]{1,0:T(8,128)(2,1)}, s16[392,512]{1,0:T(8,128)(2,1)S(1)}, u32[]{:S(2)}, u32[]{:S(2)}) collective-permute-start(s16[392,512]{1,0:T(8,128)(2,1)} %get-tuple-element.26), channel_id=1, source_target_pairs={{0,64},{64,0},{128,192},{192,128},{256,320},{320,256},{384,448},{4... | collective-permute-start | bytes 1204232 | tf_op jit(solution)/shard_map/ppermute | solution.py:459
  25.9 10.0 %collective-permute-start.1 = (s16[392,512]{1,0:T(8,128)(2,1)}, s16[392,512]{1,0:T(8,128)(2,1)S(1)}, u32[]{:S(2)}, u32[]{:S(2)}) collective-permute-start(s16[392,512]{1,0:T(8,128)(2,1)} %get-tuple-element.27), channel_id=1, source_target_pairs={{0,448},{64,128},{128,64},{192,256},{256,192},{320,384},{384,320},... | collective-permute-start | bytes 1204232 | tf_op jit(solution)/shard_map/ppermute | solution.py:460
  38.1 7.2 %copy-start.5 = (f32[8]{0:T(128)S(1)}, f32[8]{0:T(128)}, u32[]{:S(2)}) copy-start(f32[8]{0:T(128)} %param.21) | copy-start | bytes 100
  38.1 27.3 %all-to-all-start.1 = ((s16[4,200,512]{2,1,0:T(8,128)(2,1)}), s16[4,200,512]{2,1,0:T(8,128)(2,1)}, u32[]{:S(2)}, u32[]{:S(2)}) async-start(s16[4,200,512]{2,1,0:T(8,128)(2,1)} %pair_flow.1), calls=%async_computation.1 | async-start | bytes 1638400 | tf_op jit(solution)/shard_map/all_to_all | solution.py:463
  108.8 14.5 %all-to-all-start.4 = ((f32[8,8,1024]{2,1,0:T(8,128)}), f32[8,8,1024]{2,1,0:T(8,128)S(1)}, u32[]{:S(2)}, u32[]{:S(2)}) async-start(f32[8,8,1024]{2,1,0:T(8,128)} %bitcast.9), calls=%async_computation.4 | async-start | bytes 524288 | tf_op jit(solution)/shard_map/all_to_all | solution.py:422

commit v7 on v6

--- a/solution.py
+++ b/solution.py
@@ -22,6 +22,7 @@
 STEP = 0.1
 CODE = 32000.0
 FINE = 60000.0
+OFFSET = 65536.5
 POOLED = 176
 UPDATED = 128
 VMEM = 20 * 1024 * 1024
@@ -44,13 +45,6 @@
     return high, (x - high.astype(F32)).astype(BF16)
 
 
-def split3(x):
-    high = x.astype(BF16)
-    rest = x - high.astype(F32)
-    mid = rest.astype(BF16)
-    return high, mid, (rest - mid.astype(F32)).astype(BF16)
-
-
 def power_of(top):
     return jnp.ceil(jnp.log2(jnp.maximum(top, 1e-30)) * 8.0)
 
@@ -63,8 +57,8 @@
     return jnp.floor(x + 0.5)
 
 
-def to_code(part, power):
-    return rounded(part * (jnp.exp2(power * -0.125) * CODE)).astype(jnp.int32).astype(jnp.int16)
+def wrapped(x):
+    return x.astype(jnp.int32).astype(jnp.int16)
 
 
 def from_code(code):
@@ -101,10 +95,6 @@
     return jnp.transpose(jnp.broadcast_to(column, (column.shape[0], 128)))[0:1]
 
 
-def as_column(row):
-    return jnp.transpose(jnp.broadcast_to(row, (128, row.shape[1])))[:, 0:1]
-
-
 def units_kernel(commitment, capacity, bus, out):
     values = commitment[...].astype(F32) * capacity[...]
     where = bus[...].astype(F32)
@@ -132,7 +122,7 @@
     keep[...] = work[pl.ds(pl.multiple_of(parity[0] * SHARE, SHARE), SHARE), :]
     part = work[pl.ds(pl.multiple_of((1 - parity[0]) * SHARE, SHARE), SHARE), :]
     other[...] = part
-    top[...] = jnp.broadcast_to(jnp.max(jnp.abs(part), axis=1, keepdims=True), (SHARE, 128))
+    top[0] = jnp.broadcast_to(as_row(jnp.max(jnp.abs(part), axis=1, keepdims=True)), (8, SHARE))
 
 
 def net_flow(parity, factors, load):
@@ -145,27 +135,35 @@
             pl.BlockSpec((2 * SHARE, BUSES), lambda j: (j, 0)),
             pl.BlockSpec((COLS, BUSES), lambda j: (0, 0)),
         ],
-        out_specs=[pl.BlockSpec((SHARE, COLS), lambda j: (j, 0))] * 2 + [pl.BlockSpec((SHARE, 128), lambda j: (j, 0))],
-        out_shape=[half, half, jax.ShapeDtypeStruct((PAIRS * SHARE, 128), F32)],
+        out_specs=[pl.BlockSpec((SHARE, COLS), lambda j: (j, 0))] * 2 + [pl.BlockSpec((1, 8, SHARE), lambda j: (j, 0, 0))],
+        out_shape=[half, half, jax.ShapeDtypeStruct((PAIRS, 8, SHARE), F32)],
         scratch_shapes=[pltpu.VMEM((2 * SHARE, COLS), F32)],
         compiler_params=pltpu.CompilerParams(vmem_limit_bytes=WIDE),
         name="net_flow",
     )(parity, factors, load)
 
 
-def hour_places():
-    column = lax.broadcasted_iota(jnp.int32, (3 * HOURS, COLS), 1)
-    row = lax.broadcasted_iota(jnp.int32, (3 * HOURS, COLS), 0)
-    return (jnp.bitwise_and(column, HOURS - 1) == jnp.bitwise_and(row, HOURS - 1)).astype(F32).astype(BF16)
-
-
-def capacity_part(factors, capacity, place):
-    given = jnp.transpose(dot_nt(factors, capacity))
-    given = given[0:8] + given[8:16] + given[16:24]
-    largest = jnp.broadcast_to(jnp.max(jnp.abs(given), axis=0, keepdims=True), (8, SHARE))
-    pieces = jnp.concatenate([piece.astype(F32) for piece in split3(given)] + [largest], axis=0)
-    pieces = jnp.transpose(pieces)
-    return dot_nn(pieces[:, 0:24].astype(BF16), place), pieces[:, 24:25]
+def hour_levels(level):
+    column = lax.broadcasted_iota(jnp.int32, (HOURS, COLS), 1)
+    row = lax.broadcasted_iota(jnp.int32, (HOURS, COLS), 0)
+    here = jnp.bitwise_and(column, HOURS - 1) == row
+    first, second = [jnp.where(here, piece.astype(F32), 0.0) for piece in split2(level)]
+    ones = jnp.where(row < 2, 1.0, 0.0)
+    return jnp.concatenate([first, second, first, ones], axis=0).astype(BF16)
+
+
+def capacity_part(factors, capacity):
+    half = BUSES // 2
+    given = jnp.transpose(dot_nt(factors[:, 0:half], capacity[:, 0:half]) + dot_nt(factors[:, half:], capacity[:, half:]))
+    return given[0:8] + given[8:16]
+
+
+def left_side(given, high, low, value):
+    first, second = [piece.astype(F32) for piece in split2(given)]
+    row = lax.broadcasted_iota(jnp.int32, (8, SHARE), 0)
+    constant = jnp.where(row == 0, high, jnp.where(row == 1, low, 0.0))
+    both = jnp.transpose(jnp.concatenate([first, first, second, constant, jnp.broadcast_to(value, (8, SHARE))], axis=0))
+    return both[:, 0:32].astype(BF16), both[:, 32:33]
 
 
 def send_kernel(place, units, factors, level, other, top, capacity_out, send_a, send_b, stage, tops, powers, semaphores):
@@ -178,34 +176,39 @@
     parity = jnp.bitwise_and(place[0], 1)
     first = (place[0] * BUSES).astype(F32)
     lows = lax.broadcasted_iota(jnp.int32, (128, 512), 0).astype(F32)
-    total = jnp.zeros((192, 128), F32)
+    totals = [jnp.zeros((128, 128), F32), jnp.zeros((128, 128), F32)]
     for src in range(BUS_AXIS):
         values = jnp.concatenate([units[src, 8 * part : 8 * part + 8, :] for part in range(4)], axis=1)
         local = jnp.concatenate([units[src, 32 + part : 33 + part, :] for part in range(4)], axis=1) - first
         high = jnp.floor(local * (1.0 / 128.0))
         low = local - high * 128.0
-        pieces = [piece.astype(F32) for piece in split3(values)]
+        pieces = [piece.astype(F32) for piece in split2(values)]
         work = [jnp.where(high == float(block), piece, 0.0) for piece in pieces for block in range(8)]
         match = jnp.where(lows == low, 1.0, 0.0).astype(BF16)
-        total = total + dot_nt(jnp.concatenate(work, axis=0).astype(BF16), match)
-    total = total[0:64] + total[64:128] + total[128:192]
+        totals[src % 2] = totals[src % 2] + dot_nt(jnp.concatenate(work, axis=0).astype(BF16), match)
+    total = totals[0] + totals[1]
+    total = total[0:64] + total[64:128]
     capacity = jnp.concatenate([total[8 * block : 8 * block + 8] for block in range(8)], axis=1)
-    capacity = jnp.concatenate(split3(capacity), axis=0)
+    capacity = jnp.concatenate(split2(capacity), axis=0)
     capacity_out[...] = capacity.astype(F32)
-    spread = hour_places()
+    right = hour_levels(level[0:1, :])
     most = jnp.max(jnp.abs(level[0:1, :]), axis=1, keepdims=True)
     powers[...] = jnp.zeros_like(powers)
     for load in loads:
         load.wait()
     for pair in range(PAIRS):
         row = pl.multiple_of((2 * pair + 1 - parity) * SHARE, SHARE)
-        fixed, largest = capacity_part(factors[pl.ds(row, SHARE), :], capacity, spread)
-        rows = slice(pair * SHARE, pair * SHARE + SHARE)
-        power = power_of(tops[rows, 0:1] + largest * most)
-        code = to_code(fixed * level[0:1, :] - stage[rows, :], power)
+        given = capacity_part(factors[pl.ds(row, SHARE), :], capacity)
+        power = power_of(tops[pair, 0:1, :] + jnp.max(jnp.abs(given), axis=0, keepdims=True) * most)
+        powers[pair : pair + 1, 0:SHARE] = power
+        unit = jnp.exp2(power * -0.125) * CODE
+        left, unit = left_side(given * unit, OFFSET - 0.5, 0.5, unit)
         for index, out in enumerate((send_a, send_b)):
-            out[pair * HALF : pair * HALF + HALF, :] = code[index * HALF : index * HALF + HALF]
-        powers[pair : pair + 1, 0:SHARE] = as_row(power)
+            for start in range(0, HALF, 32):
+                some = slice(index * HALF + start, index * HALF + start + 32)
+                rows = slice(pair * SHARE + some.start, pair * SHARE + some.stop)
+                code = wrapped(dot_nn(left[some], right) - stage[rows, :] * unit[some])
+                out[pair * HALF + start : pair * HALF + start + 32, :] = code
     for out in (send_a, send_b):
         out[PAIRS * HALF : PAIRS * HALF + 8, :] = powers[...].astype(jnp.int32).astype(jnp.int16)
 
@@ -218,10 +221,10 @@
         send_kernel,
         in_specs=[pl.BlockSpec(memory_space=pltpu.SMEM), whole, whole, whole, anywhere, anywhere],
         out_specs=[whole, whole, whole],
-        out_shape=[pltpu.VMEM((3 * HOURS, BUSES), F32), sent, sent],
+        out_shape=[pltpu.VMEM((2 * HOURS, BUSES), F32), sent, sent],
         scratch_shapes=[
             pltpu.VMEM((PAIRS * SHARE, COLS), F32),
-            pltpu.VMEM((PAIRS * SHARE, 128), F32),
+            pltpu.VMEM((PAIRS, 8, SHARE), F32),
             pltpu.VMEM((8, COLS), F32),
             pltpu.SemaphoreType.DMA((2,)),
         ],
@@ -233,10 +236,11 @@
 def kept_kernel(place, capacity, factors, net, level, out, top):
     side = 2 * pl.program_id(0) + jnp.bitwise_and(place[0], 1)
     rows = pl.ds(pl.multiple_of(side * SHARE, SHARE), SHARE)
-    fixed, _ = capacity_part(factors[rows, :], capacity[...].astype(BF16), hour_places())
-    part = fixed * level[0:1, :] - net[...]
+    given = capacity_part(factors[rows, :], capacity[...].astype(BF16))
+    left, _ = left_side(given, 0.0, 0.0, given[0:1])
+    part = dot_nn(left, hour_levels(level[0:1, :])) - net[...]
     out[...] = part
-    top[...] = jnp.broadcast_to(jnp.max(jnp.abs(part), axis=1, keepdims=True), (SHARE, 128))
+    top[0] = jnp.broadcast_to(as_row(jnp.max(jnp.abs(part), axis=1, keepdims=True)), (8, SHARE))
 
 
 def kept_flow(place, capacity, factors, net, level):
@@ -251,10 +255,10 @@
             pl.BlockSpec((SHARE, COLS), lambda j: (j, 0)),
             whole,
         ],
-        out_specs=[pl.BlockSpec((SHARE, COLS), lambda j: (j, 0)), pl.BlockSpec((SHARE, 128), lambda j: (j, 0))],
+        out_specs=[pl.BlockSpec((SHARE, COLS), lambda j: (j, 0)), pl.BlockSpec((1, 8, SHARE), lambda j: (j, 0, 0))],
         out_shape=[
             pltpu.VMEM((PAIRS * SHARE, COLS), F32),
-            pltpu.VMEM((PAIRS * SHARE, 128), F32),
+            pltpu.VMEM((PAIRS, 8, SHARE), F32),
         ],
         compiler_params=pltpu.CompilerParams(vmem_limit_bytes=VMEM),
         name="kept_flow",
@@ -267,12 +271,17 @@
     rows = [
         jnp.sum(jnp.where(here, from_code(power[:, 0:256]), 0.0), axis=0, keepdims=True) for power in (power_a, power_b)
     ]
-    unit = unit_of(as_column(jnp.where(lane < HALF, rows[0], rows[1])))[0:SHARE]
-    power = power_of(top[:, 0:1] + unit * CODE)
-    code = jnp.concatenate([from_code(code_a[...]), from_code(code_b[...])], axis=0)
-    coded[0, 0:SHARE, :] = to_code(part[...] + code * unit, power)
-    across = jnp.broadcast_to(as_row(power), (8, SHARE))
-    across = jnp.concatenate([across, jnp.zeros((8, COLS - SHARE), F32)], axis=1)
+    unit = unit_of(jnp.where(lane < HALF, rows[0], rows[1]))[:, 0:SHARE]
+    power = power_of(top[0, 0:1, :] + unit * CODE)
+    again = jnp.exp2(power * -0.125) * CODE
+    scales = [jnp.broadcast_to(scale, (8, SHARE)) for scale in (unit * again, again)]
+    scales = jnp.transpose(jnp.concatenate(scales, axis=0))
+    for index, code in enumerate((code_a, code_b)):
+        for start in range(0, HALF, 32):
+            some = slice(index * HALF + start, index * HALF + start + 32)
+            value = part[some, :] * scales[some, 8:9] + OFFSET
+            coded[0, some, :] = wrapped(value + from_code(code[start : start + 32, :]) * scales[some, 0:1])
+    across = jnp.concatenate([jnp.broadcast_to(power, (8, SHARE)), jnp.zeros((8, COLS - SHARE), F32)], axis=1)
     coded[0, SHARE : SHARE + 8, :] = across.astype(jnp.int32).astype(jnp.int16)
 
 
@@ -284,7 +293,7 @@
         grid=(PAIRS,),
         in_specs=[
             pl.BlockSpec((SHARE, COLS), lambda j: (j, 0)),
-            pl.BlockSpec((SHARE, 128), lambda j: (j, 0)),
+            pl.BlockSpec((1, 8, SHARE), lambda j: (j, 0, 0)),
             lines,
             lines,
             tail,

time: 125 us -> 124 us (level)
  transfers between devices with their start and end apart: 5 -> 5, of which waited for: 5 -> 5; matrix products, arithmetic and copies ran while one was open for 2% -> 2% of each run, Pallas kernels for 7% -> 8%
where the time goes in v7:
time: 124 us; the launch traced here: 123 us
  blocking collectives  37.9 us (31%)
  waiting for transfers between devices  30.3 us (24%)
  starting transfers between devices  27.9 us (22%)
  Pallas kernels  23.6 us (19%)
  local copies, waits for them, and re-layouts  2.31 us (2%)
    all_to_all x2, blocking collectives, exchange(): return lax.all_to_all(tiles, axis, 0, 0, tiled=True)  37.9 us
    all_to_all x1, waiting for transfers between devices, per_device(): lax.all_to_all(coded, 'bus', 0, 0, axis_index_groups=SAME_PARITY, tiled=T...  20 us
    all_to_all x2, starting transfers between devices, exchange(): return lax.all_to_all(tiles, axis, 0, 0, tiled=True)  15.6 us
    all_to_all x2, waiting for transfers between devices, exchange(): return lax.all_to_all(tiles, axis, 0, 0, tiled=True)  7.41 us
    all_to_all x1, starting transfers between devices, per_device(): lax.all_to_all(coded, 'bus', 0, 0, axis_index_groups=SAME_PARITY, tiled=T...  6.26 us
    pallas_call x1, Pallas kernels, net_flow(): pl.pallas_call(net_flow_kernel, grid=(PAIRS,), in_specs=[pl.BlockSpec(mem...  6.11 us
    pallas_call x1, Pallas kernels, sent_flow(): pl.pallas_call(send_kernel, in_specs=[pl.BlockSpec(memory_space=pltpu.SME...  5.32 us
    ppermute x1, starting transfers between devices, per_device(): code_b = lax.ppermute(send_b, 'bus', NEAR_B)  3.9 us
  transfers between devices with their start and end apart: 5, of which 5 were waited for; matrix products, arithmetic and copies ran while one was open for 2% of the time, Pallas kernels for 8%

profile of v7, /device:TPU:1, one launch (start us, length us, event | category | flops | bytes accessed | tf_op | source)
XLA Modules:
  0.0 123.4 jit_solution(16862329404428017076)
XLA Ops:
  0.6 0.0 copy-start
  0.6 1.4 %units.1 = f32[8,40,128]{2,1,0:T(8,128)} custom-call(s32[8,512]{1,0:T(8,128)} %commitment.1, f32[1,512]{1,0:T(1,128)} %bitcast.16, s32[1,512]{1,0:T(1,128)} %bitcast.17), custom_call_target="tpu_custom_call" | custom-call | tf_op jit(solution)/shard_map/units/pallas_call | solution.py:112
  2.1 7.6 %all-to-all-start = ((f32[8,40,128]{2,1,0:T(8,128)}), f32[8,40,128]{2,1,0:T(8,128)S(1)}, u32[]{:S(2)}, u32[]{:S(2)}) async-start(f32[8,40,128]{2,1,0:T(8,128)} %units.1), calls=%async_computation | async-start | bytes 327680 | tf_op jit(solution)/shard_map/all_to_all | solution.py:431
  9.7 0.0 copy-start.6
  9.7 0.0 copy-start.4
  9.7 0.0 copy-start.3
  9.7 0.0 copy-start.1
  9.8 6.1 %net_flow.1 = (f32[768,512]{1,0:T(8,128)}, f32[768,512]{1,0:T(8,128)}, f32[4,8,192]{2,1,0:T(8,128)}) custom-call(s32[1]{0:T(128)} %bitcast.3.parity, bf16[1536,1024]{1,0:T(8,128)(2,1)} %factors.7, bf16[512,1024]{1,0:T(8,128)(2,1)} %bitcast.13), custom_call_target="tpu_custom_call" | custom-call | tf_op jit(solution)/shard_map/net_flow/pallas_call | solution.py:130
  15.9 0.0 copy-done.6
  15.9 0.1 broadcast_in_dim.10
  15.9 0.1 stack_reshape.11
  16.0 0.0 copy-done.4
  16.1 0.1 broadcast_in_dim.9
  16.1 0.1 stack_reshape.10
  16.2 0.0 copy-done.3
  16.2 0.1 copy.16
  16.3 0.1 stack_reshape.9
  16.4 1.7 %all-to-all-done.units = f32[8,40,128]{2,1,0:T(8,128)S(1)} async-done(((f32[8,40,128]{2,1,0:T(8,128)}), f32[8,40,128]{2,1,0:T(8,128)S(1)}, u32[]{:S(2)}, u32[]{:S(2)}) %all-to-all-start) | async-done | bytes 163872 | tf_op jit(solution)/shard_map/all_to_all | solution.py:431
  18.1 0.0 copy-done.1
  18.1 0.0 copy-start.2
  18.1 5.3 %sent_flow.1 = (f32[16,1024]{1,0:T(8,128)S(1)}, s16[392,512]{1,0:T(8,128)(2,1)}, s16[392,512]{1,0:T(8,128)(2,1)}) custom-call(s32[1]{0:T(128)} %bitcast.place, f32[8,40,128]{2,1,0:T(8,128)S(1)} %all-to-all-done.units, bf16[1536,1024]{1,0:T(8,128)(2,1)S(1)} %copy-done.1, f32[3,512]{1,0:T(4,128)S(1)} %pad_maximum_fusion.level.rows, ...), custom_call_target="tpu_custom_call" | custom-call | tf_op jit(solution)/shard_map/sent_flow/pallas_call | solution.py:220
  23.4 2.1 %collective-permute-start = (s16[392,512]{1,0:T(8,128)(2,1)}, s16[392,512]{1,0:T(8,128)(2,1)S(1)}, u32[]{:S(2)}, u32[]{:S(2)}) collective-permute-start(s16[392,512]{1,0:T(8,128)(2,1)} %get-tuple-element.26), channel_id=1, source_target_pairs={{0,64},{64,0},{128,192},{192,128},{256,320},{320,256},{384,448},{4... | collective-permute-start | bytes 1204232 | tf_op jit(solution)/shard_map/ppermute | solution.py:468
  25.5 3.9 %collective-permute-start.1 = (s16[392,512]{1,0:T(8,128)(2,1)}, s16[392,512]{1,0:T(8,128)(2,1)S(1)}, u32[]{:S(2)}, u32[]{:S(2)}) collective-permute-start(s16[392,512]{1,0:T(8,128)(2,1)} %get-tuple-element.27), channel_id=1, source_target_pairs={{0,448},{64,128},{128,64},{192,256},{256,192},{320,384},{384,320},... | collective-permute-start | bytes 1204232 | tf_op jit(solution)/shard_map/ppermute | solution.py:469
  29.4 0.0 copy-done.2
  29.5 3.2 %kept_flow.1 = (f32[768,512]{1,0:T(8,128)S(1)}, f32[4,8,192]{2,1,0:T(8,128)S(1)}) custom-call(s32[1]{0:T(128)} %bitcast.place, f32[16,1024]{1,0:T(8,128)S(1)} %get-tuple-element.22.capacity, bf16[1536,1024]{1,0:T(8,128)(2,1)S(1)} %copy-done.1, f32[768,512]{1,0:T(8,128)S(1)} %copy-done.2, f32[3,512]{1,0:T(4,128)S(1)} %pad_maximum_fusion.level.rows), custom_call_target="tpu_custom_call" | custom-call | tf_op jit(solution)/shard_map/kept_flow/pallas_call | solution.py:248
  32.7 0.2 collective-permute-done.code_a.power_a
  32.8 2.7 %collective-permute-done.1.code_b.power_b = s16[392,512]{1,0:T(8,128)(2,1)S(1)} collective-permute-done((s16[392,512]{1,0:T(8,128)(2,1)}, s16[392,512]{1,0:T(8,128)(2,1)S(1)}, u32[]{:S(2)}, u32[]{:S(2)}) %collective-permute-start.1) | collective-permute-done | bytes 401440 | tf_op jit(solution)/shard_map/ppermute | solution.py:469
  35.6 2.2 %pair_flow.1 = s16[4,200,512]{2,1,0:T(8,128)(2,1)} custom-call(f32[768,512]{1,0:T(8,128)S(1)} %get-tuple-element.24.part, f32[4,8,192]{2,1,0:T(8,128)S(1)} %get-tuple-element.25.top, s16[392,512]{1,0:T(8,128)(2,1)S(1)} %collective-permute-done.code_a.power_a, s16[392,512]{1,0:T(8,128)(2,1)S(1)} %collective-permute-done.1.code_b.power_b, ...), custom_call_target="tpu_custom_call" | custom-call | tf_op jit(solution)/shard_map/pair_flow/pallas_call | solution.py:291
  37.8 0.0 copy-start.5
  37.8 6.3 %all-to-all-start.1 = ((s16[4,200,512]{2,1,0:T(8,128)(2,1)}), s16[4,200,512]{2,1,0:T(8,128)(2,1)}, u32[]{:S(2)}, u32[]{:S(2)}) async-start(s16[4,200,512]{2,1,0:T(8,128)(2,1)} %pair_flow.1), calls=%async_computation.1 | async-start | bytes 1638400 | tf_op jit(solution)/shard_map/all_to_all | solution.py:472
  44.0 0.8 dynamic_slice.6
  44.8 0.1 copy.17.limit
  44.9 0.0 copy-done.5
  44.9 0.1 copy.18.target
  45.0 0.0 copy-done
  45.0 0.1 constant_dynamic-slice_fusion.current
  45.1 20.0 %all-to-all-done.1.coded = s16[4,200,512]{2,1,0:T(8,128)(2,1)} async-done(((s16[4,200,512]{2,1,0:T(8,128)(2,1)}), s16[4,200,512]{2,1,0:T(8,128)(2,1)}, u32[]{:S(2)}, u32[]{:S(2)}) %all-to-all-start.1) | async-done | bytes 819232 | tf_op jit(solution)/shard_map/all_to_all | solution.py:472
  65.0 3.2 %excess_sums.1 = s16[8,176,128]{2,1,0:T(8,128)(2,1)S(1)} custom-call(s16[4,200,512]{2,1,0:T(8,128)(2,1)} %all-to-all-done.1.coded, f32[192,1]{1,0:T(8,128)S(1)} %copy.17.limit, f32[3,512]{1,0:T(4,128)S(1)} %pad_maximum_fusion.level.rows, f32[8,192]{1,0:T(8,128)S(1)} %constant_dynamic-slice_fusion.current, f32[8,1]{1,0:T(8,128)S(1)} %copy.18.target), custom_call_target="tpu_custom_call" | custom-call | tf_op jit(solution)/shard_map/excess_sums/pallas_call | solution.py:356
  68.3 24.4 %all_to_all.25.sums = s16[8,176,128]{2,1,0:T(8,128)(2,1)S(1)} all-to-all(s16[8,176,128]{2,1,0:T(8,128)(2,1)S(1)} %excess_sums.1), channel_id=1, replica_groups=mesh['bus'=8,'line'=8,'scen'=8] {'scen'}, dimensions={0} | all-to-all | bytes 720896 | tf_op jit(solution)/shard_map/all_to_all | solution.py:431
  92.6 0.6 update.1
  93.2 13.5 %all_to_all.26.packed = s16[8,128,128]{2,1,0:T(8,128)(2,1)S(1)} all-to-all(s16[8,128,128]{2,1,0:T(8,128)(2,1)S(1)} %update.1), channel_id=1, replica_groups=mesh['bus'=8,'line'=8,'scen'=8] {'bus'}, dimensions={0} | all-to-all | bytes 524288 | tf_op jit(solution)/shard_map/all_to_all | solution.py:431
  106.8 1.5 %slopes.1 = (f32[64,1024]{1,0:T(8,128)}, f32[8,8,192]{2,1,0:T(8,128)S(1)}) custom-call(s16[8,128,128]{2,1,0:T(8,128)(2,1)S(1)} %all_to_all.26.packed, bf16[1536,1024]{1,0:T(8,128)(2,1)S(1)} %copy-done.1), custom_call_target="tpu_custom_call" | custom-call | tf_op jit(solution)/shard_map/slopes/pallas_call | solution.py:412
  108.3 8.0 %all-to-all-start.4 = ((f32[8,8,1024]{2,1,0:T(8,128)}), f32[8,8,1024]{2,1,0:T(8,128)S(1)}, u32[]{:S(2)}, u32[]{:S(2)}) async-start(f32[8,8,1024]{2,1,0:T(8,128)} %bitcast.9), calls=%async_computation.4 | async-start | bytes 524288 | tf_op jit(solution)/shard_map/all_to_all | solution.py:431
  116.3 0.7 reshape.40
  117.0 5.7 %all-to-all-done.4 = f32[8,8,1024]{2,1,0:T(8,128)S(1)} async-done(((f32[8,8,1024]{2,1,0:T(8,128)}), f32[8,8,1024]{2,1,0:T(8,128)S(1)}, u32[]{:S(2)}, u32[]{:S(2)}) %all-to-all-start.4) | async-done | bytes 262176 | tf_op jit(solution)/shard_map/all_to_all | solution.py:431
  122.7 0.6 reduce_sum.9
  (3 shorter events, 0.0 us)
Async XLA Ops:
  0.6 44.4 %copy-start = (f32[8,1536]{1,0:T(8,128)S(1)}, f32[8,1536]{1,0:T(8,128)}, u32[]{:S(2)}) copy-start(f32[8,1536]{1,0:T(8,128)} %param.20) | copy-start | bytes 147460
  2.1 16.0 %all-to-all-start = ((f32[8,40,128]{2,1,0:T(8,128)}), f32[8,40,128]{2,1,0:T(8,128)S(1)}, u32[]{:S(2)}, u32[]{:S(2)}) async-start(f32[8,40,128]{2,1,0:T(8,128)} %units.1), calls=%async_computation | async-start | bytes 327680 | tf_op jit(solution)/shard_map/all_to_all | solution.py:431
  9.7 6.2 %copy-start.6 = (s32[64,1]{0,1:T(1,128)S(1)}, s32[64,1]{0,1:T(1,128)}, u32[]{:S(2)}) copy-start(s32[64,1]{0,1:T(1,128)} %param.15) | copy-start | bytes 772
  9.7 6.3 %copy-start.4 = (f32[64]{0:T(128)S(1)}, f32[64]{0:T(128)}, u32[]{:S(2)}) copy-start(f32[64]{0:T(128)} %param.14) | copy-start | bytes 772
  9.7 6.5 %copy-start.3 = (f32[64,8]{0,1:T(8,128)S(1)}, f32[64,8]{0,1:T(8,128)}, u32[]{:S(2)}) copy-start(f32[64,8]{0,1:T(8,128)} %param.13) | copy-start | bytes 6148
  9.7 8.4 %copy-start.1 = (bf16[1536,1024]{1,0:T(8,128)(2,1)S(1)}, bf16[1536,1024]{1,0:T(8,128)(2,1)}, u32[]{:S(2)}) copy-start(bf16[1536,1024]{1,0:T(8,128)(2,1)} %factors.7) | copy-start | bytes 9437188
  18.1 11.4 %copy-start.2 = (f32[768,512]{1,0:T(8,128)S(1)}, f32[768,512]{1,0:T(8,128)}, u32[]{:S(2)}) copy-start(f32[768,512]{1,0:T(8,128)} %get-tuple-element.23.net) | copy-start | bytes 4718596
  23.4 9.4 %collective-permute-start = (s16[392,512]{1,0:T(8,128)(2,1)}, s16[392,512]{1,0:T(8,128)(2,1)S(1)}, u32[]{:S(2)}, u32[]{:S(2)}) collective-permute-start(s16[392,512]{1,0:T(8,128)(2,1)} %get-tuple-element.26), channel_id=1, source_target_pairs={{0,64},{64,0},{128,192},{192,128},{256,320},{320,256},{384,448},{4... | collective-permute-start | bytes 1204232 | tf_op jit(solution)/shard_map/ppermute | solution.py:468
  25.5 10.0 %collective-permute-start.1 = (s16[392,512]{1,0:T(8,128)(2,1)}, s16[392,512]{1,0:T(8,128)(2,1)S(1)}, u32[]{:S(2)}, u32[]{:S(2)}) collective-permute-start(s16[392,512]{1,0:T(8,128)(2,1)} %get-tuple-element.27), channel_id=1, source_target_pairs={{0,448},{64,128},{128,64},{192,256},{256,192},{320,384},{384,320},... | collective-permute-start | bytes 1204232 | tf_op jit(solution)/shard_map/ppermute | solution.py:469
  37.8 7.2 %copy-start.5 = (f32[8]{0:T(128)S(1)}, f32[8]{0:T(128)}, u32[]{:S(2)}) copy-start(f32[8]{0:T(128)} %param.21) | copy-start | bytes 100
  37.8 27.3 %all-to-all-start.1 = ((s16[4,200,512]{2,1,0:T(8,128)(2,1)}), s16[4,200,512]{2,1,0:T(8,128)(2,1)}, u32[]{:S(2)}, u32[]{:S(2)}) async-start(s16[4,200,512]{2,1,0:T(8,128)(2,1)} %pair_flow.1), calls=%async_computation.1 | async-start | bytes 1638400 | tf_op jit(solution)/shard_map/all_to_all | solution.py:472
  108.3 14.4 %all-to-all-start.4 = ((f32[8,8,1024]{2,1,0:T(8,128)}), f32[8,8,1024]{2,1,0:T(8,128)S(1)}, u32[]{:S(2)}, u32[]{:S(2)}) async-start(f32[8,8,1024]{2,1,0:T(8,128)} %bitcast.9), calls=%async_computation.4 | async-start | bytes 524288 | tf_op jit(solution)/shard_map/all_to_all | solution.py:431

commit v8 on v7

--- a/solution.py
+++ b/solution.py
@@ -27,6 +27,7 @@
 UPDATED = 128
 VMEM = 20 * 1024 * 1024
 WIDE = 56 * 1024 * 1024
+MIDDLE = 50 * 1024 * 1024
 
 F32 = jnp.float32
 BF16 = jnp.bfloat16
@@ -126,7 +127,7 @@
 
 
 def net_flow(parity, factors, load):
-    half = jax.ShapeDtypeStruct((PAIRS * SHARE, COLS), F32)
+    half = pltpu.HBM((PAIRS * SHARE, COLS), F32)
     return pl.pallas_call(
         net_flow_kernel,
         grid=(PAIRS,),
@@ -136,7 +137,7 @@
             pl.BlockSpec((COLS, BUSES), lambda j: (0, 0)),
         ],
         out_specs=[pl.BlockSpec((SHARE, COLS), lambda j: (j, 0))] * 2 + [pl.BlockSpec((1, 8, SHARE), lambda j: (j, 0, 0))],
-        out_shape=[half, half, jax.ShapeDtypeStruct((PAIRS, 8, SHARE), F32)],
+        out_shape=[half, half, pltpu.HBM((PAIRS, 8, SHARE), F32)],
         scratch_shapes=[pltpu.VMEM((2 * SHARE, COLS), F32)],
         compiler_params=pltpu.CompilerParams(vmem_limit_bytes=WIDE),
         name="net_flow",
@@ -215,7 +216,7 @@
 
 def sent_flow(place, units, factors, level, other, top):
     whole = pl.BlockSpec(memory_space=pltpu.VMEM)
-    anywhere = pl.BlockSpec(memory_space=pl.ANY)
+    anywhere = pl.BlockSpec(memory_space=pltpu.HBM)
     sent = jax.ShapeDtypeStruct((PAIRS * HALF + 8, COLS), jnp.int16)
     return pl.pallas_call(
         send_kernel,
@@ -228,9 +229,9 @@
             pltpu.VMEM((8, COLS), F32),
             pltpu.SemaphoreType.DMA((2,)),
         ],
-        compiler_params=pltpu.CompilerParams(vmem_limit_bytes=WIDE),
+        compiler_params=pltpu.CompilerParams(vmem_limit_bytes=VMEM),
         name="sent_flow",
-    )(place, near(units), factors, near(level), other, top)
+    )(place, near(units), factors, near(level), far(other), far(top))
 
 
 def kept_kernel(place, capacity, factors, net, level, out, top):
@@ -260,7 +261,7 @@
             pltpu.VMEM((PAIRS * SHARE, COLS), F32),
             pltpu.VMEM((PAIRS, 8, SHARE), F32),
         ],
-        compiler_params=pltpu.CompilerParams(vmem_limit_bytes=VMEM),
+        compiler_params=pltpu.CompilerParams(vmem_limit_bytes=MIDDLE),
         name="kept_flow",
     )(place, near(capacity), factors, net, near(level))
 
@@ -306,34 +307,44 @@
     )(part, top, code_a, code_b, code_a, code_b)
 
 
-def excess_kernel(coded, limit, rows, current, target, out):
+def excess_kernel(received, limit, rows, current, target, out, coded, pick, pushes, squares, pushed, semaphores):
+    loads = [pltpu.make_async_copy(received.at[src], coded.at[src], semaphores.at[src]) for src in range(PAIRS)]
+    for load in loads:
+        load.start()
     level = rows[0:1, :]
     weight = rows[1:2, :]
     cluster = rows[2:3, :]
     column = lax.broadcasted_iota(jnp.int32, (1, COLS), 1)
     hour = jnp.bitwise_and(column, HOURS - 1)
-    power = jnp.concatenate([from_code(coded[src, SHARE : SHARE + 8, 0:SHARE])[0:1] for src in range(PAIRS)] * 2, axis=0)
-    unit = unit_of(jnp.transpose(power))
-    flow = from_code(coded[0, 0:SHARE, :]) * unit[:, 0:1]
-    for src in range(1, PAIRS):
-        flow = flow + from_code(coded[src, 0:SHARE, :]) * unit[:, src : src + 1]
-    edge = limit[:, 0:1]
-    excess = flow - jnp.clip(flow, -edge, edge)
-    p0, p1 = split2(excess * (level * weight))
-    e0, e1 = split2(excess * excess * (0.5 * weight))
     key = cluster * float(HOURS) + hour.astype(F32)
-    row = lax.broadcasted_iota(jnp.int32, (COLS, COLS), 0)
-    inner = jnp.bitwise_and(row, ROWS - 1)
-    owner = jnp.right_shift(row, 6)
-    mine = (jnp.right_shift(inner, 3) * SCEN_AXIS + owner) * HOURS + jnp.bitwise_and(inner, HOURS - 1)
-    pick = jnp.where(mine.astype(F32) == key, 1.0, 0.0).astype(BF16)
-    pushed = dot_nt(pick, p0) + dot_nt(pick, p1)
+    for owner in range(SCEN_AXIS):
+        inner = lax.broadcasted_iota(jnp.int32, (ROWS, COLS), 0)
+        mine = (jnp.right_shift(inner, 3) * SCEN_AXIS + owner) * HOURS + jnp.bitwise_and(inner, HOURS - 1)
+        pick[owner * ROWS : owner * ROWS + ROWS, :] = jnp.where(mine.astype(F32) == key, 1.0, 0.0).astype(BF16)
     row = lax.broadcasted_iota(jnp.int32, (128, COLS), 0)
     inner = jnp.bitwise_and(row, 15)
     owner = jnp.right_shift(row, 4)
     mine = jnp.where(inner < 8, inner * SCEN_AXIS + owner, owner * OWNED + inner - 8)
-    pick = jnp.where(mine.astype(F32) == cluster, 1.0, 0.0).astype(BF16)
-    pooled = dot_nt(pick, e0) + dot_nt(pick, e1)
+    pick[COLS : COLS + 128, :] = jnp.where(mine.astype(F32) == cluster, 1.0, 0.0).astype(BF16)
+    scaled = level * weight
+    half = 0.5 * weight
+    for load in loads:
+        load.wait()
+    power = jnp.concatenate([from_code(coded[src, SHARE : SHARE + 8, 0:SHARE])[0:1] for src in range(PAIRS)] * 2, axis=0)
+    unit = unit_of(jnp.transpose(power))
+    for start in range(0, SHARE, 32):
+        some = slice(start, start + 32)
+        flow = from_code(coded[0, some, :]) * unit[some, 0:1]
+        for src in range(1, PAIRS):
+            flow = flow + from_code(coded[src, some, :]) * unit[some, src : src + 1]
+        edge = limit[some, 0:1]
+        excess = flow - jnp.clip(flow, -edge, edge)
+        for out_ref, value in ((pushes, excess * scaled), (squares, excess * excess * half)):
+            out_ref[some, 0:COLS], out_ref[some, COLS:] = split2(value)
+    twice = pick[0:COLS, :]
+    pushed[...] = dot_nt(jnp.concatenate([twice, twice], axis=1), pushes[...])
+    twice = pick[COLS:, :]
+    pooled = dot_nt(jnp.concatenate([twice, twice], axis=1), squares[...])
     lane = lax.broadcasted_iota(jnp.int32, (128, 128), 1)
     last = lax.broadcasted_iota(jnp.int32, (8, SHARE), 0)
     table = jnp.zeros((128, 128), F32)
@@ -341,7 +352,7 @@
     for dest in range(SCEN_AXIS):
         given = jnp.where(last == 0, current[dest : dest + 1, :], jnp.where(last == 1, target[dest : dest + 1, 0:1], 0.0))
         block, power = coded_rows(
-            pushed[dest * ROWS : dest * ROWS + ROWS],
+            pushed[dest * ROWS : dest * ROWS + ROWS, :],
             jnp.concatenate([pooled[dest * 16 : dest * 16 + 16], given], axis=0),
         )
         table = jnp.where(lane == dest, power, table)
@@ -352,15 +363,23 @@
         out[dest] = jnp.concatenate([blocks[dest], tail], axis=0).astype(jnp.int32).astype(jnp.int16)
 
 
-def excess_sums(coded, limit, rows, current, target):
+def excess_sums(received, limit, rows, current, target):
     return pl.pallas_call(
         excess_kernel,
-        in_specs=[pl.BlockSpec(memory_space=pltpu.VMEM)] * 5,
+        in_specs=[pl.BlockSpec(memory_space=pltpu.HBM)] + [pl.BlockSpec(memory_space=pltpu.VMEM)] * 4,
         out_specs=pl.BlockSpec(memory_space=pltpu.VMEM),
         out_shape=pltpu.VMEM((SCEN_AXIS, POOLED, 128), jnp.int16),
+        scratch_shapes=[
+            pltpu.VMEM((PAIRS, SHARE + 8, COLS), jnp.int16),
+            pltpu.VMEM((COLS + 128, COLS), BF16),
+            pltpu.VMEM((SHARE, 2 * COLS), BF16),
+            pltpu.VMEM((SHARE, 2 * COLS), BF16),
+            pltpu.VMEM((COLS, SHARE), F32),
+            pltpu.SemaphoreType.DMA((PAIRS,)),
+        ],
         compiler_params=pltpu.CompilerParams(vmem_limit_bytes=VMEM),
         name="excess_sums",
-    )(near(coded), near(limit), near(rows), near(current), near(target))
+    )(received, near(limit), near(rows), near(current), near(target))
 
 
 def update_kernel(sums, current, target, out):
@@ -429,6 +448,10 @@
 
 def exchange(tiles, axis):
     return lax.all_to_all(tiles, axis, 0, 0, tiled=True)
+
+
+def far(x):
+    return pltpu.with_memory_space_constraint(x, pltpu.HBM)
 
 
 def near(x):

time: 124 us -> 123 us (level)
  waiting for transfers between devices: 30.3 us -> 28.9 us
    ppermute x1, waiting for transfers between devices: 2.74 us -> 1.46 us  [per_device(): code_b = lax.ppermute(send_b, 'bus', NEAR_B)]
  transfers between devices with their start and end apart: 5 -> 5, of which waited for: 5 -> 4; matrix products, arithmetic and copies ran while one was open for 2% -> 2% of each run, Pallas kernels for 8% -> 9%
where the time goes in v8:
time: 123 us; the launch traced here: 122 us
  blocking collectives  37.9 us (31%)
  waiting for transfers between devices  28.9 us (23%)
  starting transfers between devices  27.9 us (23%)
  Pallas kernels  24.1 us (20%)
  local copies, waits for them, and re-layouts  2.31 us (2%)
    all_to_all x2, blocking collectives, exchange(): return lax.all_to_all(tiles, axis, 0, 0, tiled=True)  37.9 us
    all_to_all x1, waiting for transfers between devices, per_device(): lax.all_to_all(coded, 'bus', 0, 0, axis_index_groups=SAME_PARITY, tiled=T...  20 us
    all_to_all x2, starting transfers between devices, exchange(): return lax.all_to_all(tiles, axis, 0, 0, tiled=True)  15.6 us
    all_to_all x2, waiting for transfers between devices, exchange(): return lax.all_to_all(tiles, axis, 0, 0, tiled=True)  7.42 us
    all_to_all x1, starting transfers between devices, per_device(): lax.all_to_all(coded, 'bus', 0, 0, axis_index_groups=SAME_PARITY, tiled=T...  6.24 us
    pallas_call x1, Pallas kernels, net_flow(): pl.pallas_call(net_flow_kernel, grid=(PAIRS,), in_specs=[pl.BlockSpec(mem...  6.1 us
    pallas_call x1, Pallas kernels, kept_flow(): pl.pallas_call(kept_kernel, grid=(PAIRS,), in_specs=[pl.BlockSpec(memory_...  4.44 us
    pallas_call x1, Pallas kernels, sent_flow(): pl.pallas_call(send_kernel, in_specs=[pl.BlockSpec(memory_space=pltpu.SME...  4.43 us
  transfers between devices with their start and end apart: 5, of which 4 were waited for; matrix products, arithmetic and copies ran while one was open for 2% of the time, Pallas kernels for 9%

profile of v8, /device:TPU:1, one launch (start us, length us, event | category | flops | bytes accessed | tf_op | source)
XLA Modules:
  0.0 122.5 jit_solution(13609345499403787975)
XLA Ops:
  0.6 0.0 copy-start
  0.6 1.4 %units.1 = f32[8,40,128]{2,1,0:T(8,128)} custom-call(s32[8,512]{1,0:T(8,128)} %commitment.1, f32[1,512]{1,0:T(1,128)} %bitcast.16, s32[1,512]{1,0:T(1,128)} %bitcast.17), custom_call_target="tpu_custom_call" | custom-call | tf_op jit(solution)/shard_map/units/pallas_call | solution.py:113
  2.1 7.6 %all-to-all-start = ((f32[8,40,128]{2,1,0:T(8,128)}), f32[8,40,128]{2,1,0:T(8,128)S(1)}, u32[]{:S(2)}, u32[]{:S(2)}) async-start(f32[8,40,128]{2,1,0:T(8,128)} %units.1), calls=%async_computation | async-start | bytes 327680 | tf_op jit(solution)/shard_map/all_to_all | solution.py:450
  9.7 0.0 copy-start.5
  9.7 0.0 copy-start.3
  9.7 0.0 copy-start.2
  9.7 0.0 copy-start.1
  9.8 6.1 %net_flow.1 = (f32[768,512]{1,0:T(8,128)}, f32[768,512]{1,0:T(8,128)}, f32[4,8,192]{2,1,0:T(8,128)}) custom-call(s32[1]{0:T(128)} %bitcast.3.parity, bf16[1536,1024]{1,0:T(8,128)(2,1)} %factors.7, bf16[512,1024]{1,0:T(8,128)(2,1)} %bitcast.13), custom_call_target="tpu_custom_call" | custom-call | tf_op jit(solution)/shard_map/net_flow/pallas_call | solution.py:131
  15.9 0.0 copy-done.5
  15.9 0.1 broadcast_in_dim.10
  15.9 0.1 stack_reshape.11
  16.0 0.0 copy-done.3
  16.1 0.1 broadcast_in_dim.9
  16.1 0.1 stack_reshape.10
  16.2 0.0 copy-done.2
  16.2 0.1 copy.16
  16.3 0.1 stack_reshape.9
  16.4 1.7 %all-to-all-done.units = f32[8,40,128]{2,1,0:T(8,128)S(1)} async-done(((f32[8,40,128]{2,1,0:T(8,128)}), f32[8,40,128]{2,1,0:T(8,128)S(1)}, u32[]{:S(2)}, u32[]{:S(2)}) %all-to-all-start) | async-done | bytes 163872 | tf_op jit(solution)/shard_map/all_to_all | solution.py:450
  18.1 0.0 copy-done.1
  18.1 4.4 %sent_flow.1 = (f32[16,1024]{1,0:T(8,128)S(1)}, s16[392,512]{1,0:T(8,128)(2,1)S(1)}, s16[392,512]{1,0:T(8,128)(2,1)S(1)}) custom-call(s32[1]{0:T(128)} %bitcast.place, f32[8,40,128]{2,1,0:T(8,128)S(1)} %all-to-all-done.units, bf16[1536,1024]{1,0:T(8,128)(2,1)S(1)} %copy-done.1, f32[3,512]{1,0:T(4,128)S(1)} %pad_maximum_fusion.level.rows, ...), custom_call_target="tpu_custom_call" | custom-call | tf_op jit(solution)/shard_map/sent_flow/pallas_call | solution.py:221
  22.5 2.1 %collective-permute-start = (s16[392,512]{1,0:T(8,128)(2,1)S(1)}, s16[392,512]{1,0:T(8,128)(2,1)S(1)}, u32[]{:S(2)}, u32[]{:S(2)}) collective-permute-start(s16[392,512]{1,0:T(8,128)(2,1)S(1)} %get-tuple-element.26), channel_id=1, source_target_pairs={{0,64},{64,0},{128,192},{192,128},{256,320},{320,256},{384,448},{4... | collective-permute-start | bytes 1204232 | tf_op jit(solution)/shard_map/ppermute | solution.py:491
  24.6 3.9 %collective-permute-start.1 = (s16[392,512]{1,0:T(8,128)(2,1)S(1)}, s16[392,512]{1,0:T(8,128)(2,1)S(1)}, u32[]{:S(2)}, u32[]{:S(2)}) collective-permute-start(s16[392,512]{1,0:T(8,128)(2,1)S(1)} %get-tuple-element.27), channel_id=1, source_target_pairs={{0,448},{64,128},{128,64},{192,256},{256,192},{320,384},{384,320},... | collective-permute-start | bytes 1204232 | tf_op jit(solution)/shard_map/ppermute | solution.py:492
  28.5 4.4 %kept_flow.1 = (f32[768,512]{1,0:T(8,128)S(1)}, f32[4,8,192]{2,1,0:T(8,128)S(1)}) custom-call(s32[1]{0:T(128)} %bitcast.place, f32[16,1024]{1,0:T(8,128)S(1)} %get-tuple-element.22.capacity, bf16[1536,1024]{1,0:T(8,128)(2,1)S(1)} %copy-done.1, f32[768,512]{1,0:T(8,128)} %get-tuple-element.23.net, f32[3,512]{1,0:T(4,128)S(1)} %pad_maximum_fusion.level.rows), custom_call_target="tpu_custom_call" | custom-call | tf_op jit(solution)/shard_map/kept_flow/pallas_call | solution.py:249
  33.0 0.0 collective-permute-done.code_a.power_a
  33.0 1.5 %collective-permute-done.1.code_b.power_b = s16[392,512]{1,0:T(8,128)(2,1)S(1)} collective-permute-done((s16[392,512]{1,0:T(8,128)(2,1)S(1)}, s16[392,512]{1,0:T(8,128)(2,1)S(1)}, u32[]{:S(2)}, u32[]{:S(2)}) %collective-permute-start.1) | collective-permute-done | bytes 401440 | tf_op jit(solution)/shard_map/ppermute | solution.py:492
  34.5 2.2 %pair_flow.1 = s16[4,200,512]{2,1,0:T(8,128)(2,1)} custom-call(f32[768,512]{1,0:T(8,128)S(1)} %get-tuple-element.24.part, f32[4,8,192]{2,1,0:T(8,128)S(1)} %get-tuple-element.25.top, s16[392,512]{1,0:T(8,128)(2,1)S(1)} %collective-permute-done.code_a.power_a, s16[392,512]{1,0:T(8,128)(2,1)S(1)} %collective-permute-done.1.code_b.power_b, ...), custom_call_target="tpu_custom_call" | custom-call | tf_op jit(solution)/shard_map/pair_flow/pallas_call | solution.py:292
  36.7 0.0 copy-start.4
  36.7 6.2 %all-to-all-start.1 = ((s16[4,200,512]{2,1,0:T(8,128)(2,1)}), s16[4,200,512]{2,1,0:T(8,128)(2,1)}, u32[]{:S(2)}, u32[]{:S(2)}) async-start(s16[4,200,512]{2,1,0:T(8,128)(2,1)} %pair_flow.1), calls=%async_computation.1 | async-start | bytes 1638400 | tf_op jit(solution)/shard_map/all_to_all | solution.py:495
  42.9 0.8 dynamic_slice.6
  43.7 0.1 copy.17.limit
  43.8 0.0 copy-done.4
  43.8 0.1 copy.18.target
  43.9 0.0 copy-done
  43.9 0.1 constant_dynamic-slice_fusion.current
  44.0 20.0 %all-to-all-done.1.received = s16[4,200,512]{2,1,0:T(8,128)(2,1)} async-done(((s16[4,200,512]{2,1,0:T(8,128)(2,1)}), s16[4,200,512]{2,1,0:T(8,128)(2,1)}, u32[]{:S(2)}, u32[]{:S(2)}) %all-to-all-start.1) | async-done | bytes 819232 | tf_op jit(solution)/shard_map/all_to_all | solution.py:495
  64.0 3.3 %excess_sums.1 = s16[8,176,128]{2,1,0:T(8,128)(2,1)S(1)} custom-call(s16[4,200,512]{2,1,0:T(8,128)(2,1)} %all-to-all-done.1.received, f32[192,1]{1,0:T(8,128)S(1)} %copy.17.limit, f32[3,512]{1,0:T(4,128)S(1)} %pad_maximum_fusion.level.rows, f32[8,192]{1,0:T(8,128)S(1)} %constant_dynamic-slice_fusion.current, f32[8,1]{1,0:T(8,128)S(1)} %copy.18.target), custom_call_target="tpu_custom_call" | custom-call | tf_op jit(solution)/shard_map/excess_sums/pallas_call | solution.py:367
  67.3 24.3 %all_to_all.25.sums = s16[8,176,128]{2,1,0:T(8,128)(2,1)S(1)} all-to-all(s16[8,176,128]{2,1,0:T(8,128)(2,1)S(1)} %excess_sums.1), channel_id=1, replica_groups=mesh['bus'=8,'line'=8,'scen'=8] {'scen'}, dimensions={0} | all-to-all | bytes 720896 | tf_op jit(solution)/shard_map/all_to_all | solution.py:450
  91.7 0.6 update.1
  92.3 13.5 %all_to_all.26.packed = s16[8,128,128]{2,1,0:T(8,128)(2,1)S(1)} all-to-all(s16[8,128,128]{2,1,0:T(8,128)(2,1)S(1)} %update.1), channel_id=1, replica_groups=mesh['bus'=8,'line'=8,'scen'=8] {'bus'}, dimensions={0} | all-to-all | bytes 524288 | tf_op jit(solution)/shard_map/all_to_all | solution.py:450
  105.8 1.5 %slopes.1 = (f32[64,1024]{1,0:T(8,128)}, f32[8,8,192]{2,1,0:T(8,128)S(1)}) custom-call(s16[8,128,128]{2,1,0:T(8,128)(2,1)S(1)} %all_to_all.26.packed, bf16[1536,1024]{1,0:T(8,128)(2,1)S(1)} %copy-done.1), custom_call_target="tpu_custom_call" | custom-call | tf_op jit(solution)/shard_map/slopes/pallas_call | solution.py:431
  107.4 8.0 %all-to-all-start.4 = ((f32[8,8,1024]{2,1,0:T(8,128)}), f32[8,8,1024]{2,1,0:T(8,128)S(1)}, u32[]{:S(2)}, u32[]{:S(2)}) async-start(f32[8,8,1024]{2,1,0:T(8,128)} %bitcast.9), calls=%async_computation.4 | async-start | bytes 524288 | tf_op jit(solution)/shard_map/all_to_all | solution.py:450
  115.4 0.7 reshape.40
  116.1 5.7 %all-to-all-done.4 = f32[8,8,1024]{2,1,0:T(8,128)S(1)} async-done(((f32[8,8,1024]{2,1,0:T(8,128)}), f32[8,8,1024]{2,1,0:T(8,128)S(1)}, u32[]{:S(2)}, u32[]{:S(2)}) %all-to-all-start.4) | async-done | bytes 262176 | tf_op jit(solution)/shard_map/all_to_all | solution.py:450
  121.8 0.6 reduce_sum.9
  (3 shorter events, 0.0 us)
Async XLA Ops:
  0.6 43.3 %copy-start = (f32[8,1536]{1,0:T(8,128)S(1)}, f32[8,1536]{1,0:T(8,128)}, u32[]{:S(2)}) copy-start(f32[8,1536]{1,0:T(8,128)} %param.20) | copy-start | bytes 147460
  2.1 16.0 %all-to-all-start = ((f32[8,40,128]{2,1,0:T(8,128)}), f32[8,40,128]{2,1,0:T(8,128)S(1)}, u32[]{:S(2)}, u32[]{:S(2)}) async-start(f32[8,40,128]{2,1,0:T(8,128)} %units.1), calls=%async_computation | async-start | bytes 327680 | tf_op jit(solution)/shard_map/all_to_all | solution.py:450
  9.7 6.1 %copy-start.5 = (s32[64,1]{0,1:T(1,128)S(1)}, s32[64,1]{0,1:T(1,128)}, u32[]{:S(2)}) copy-start(s32[64,1]{0,1:T(1,128)} %param.15) | copy-start | bytes 772
  9.7 6.3 %copy-start.3 = (f32[64]{0:T(128)S(1)}, f32[64]{0:T(128)}, u32[]{:S(2)}) copy-start(f32[64]{0:T(128)} %param.14) | copy-start | bytes 772
  9.7 6.5 %copy-start.2 = (f32[64,8]{0,1:T(8,128)S(1)}, f32[64,8]{0,1:T(8,128)}, u32[]{:S(2)}) copy-start(f32[64,8]{0,1:T(8,128)} %param.13) | copy-start | bytes 6148
  9.7 8.4 %copy-start.1 = (bf16[1536,1024]{1,0:T(8,128)(2,1)S(1)}, bf16[1536,1024]{1,0:T(8,128)(2,1)}, u32[]{:S(2)}) copy-start(bf16[1536,1024]{1,0:T(8,128)(2,1)} %factors.7) | copy-start | bytes 9437188
  22.5 10.5 %collective-permute-start = (s16[392,512]{1,0:T(8,128)(2,1)S(1)}, s16[392,512]{1,0:T(8,128)(2,1)S(1)}, u32[]{:S(2)}, u32[]{:S(2)}) collective-permute-start(s16[392,512]{1,0:T(8,128)(2,1)S(1)} %get-tuple-element.26), channel_id=1, source_target_pairs={{0,64},{64,0},{128,192},{192,128},{256,320},{320,256},{384,448},{4... | collective-permute-start | bytes 1204232 | tf_op jit(solution)/shard_map/ppermute | solution.py:491
  24.6 9.8 %collective-permute-start.1 = (s16[392,512]{1,0:T(8,128)(2,1)S(1)}, s16[392,512]{1,0:T(8,128)(2,1)S(1)}, u32[]{:S(2)}, u32[]{:S(2)}) collective-permute-start(s16[392,512]{1,0:T(8,128)(2,1)S(1)} %get-tuple-element.27), channel_id=1, source_target_pairs={{0,448},{64,128},{128,64},{192,256},{256,192},{320,384},{384,320},... | collective-permute-start | bytes 1204232 | tf_op jit(solution)/shard_map/ppermute | solution.py:492
  36.7 7.1 %copy-start.4 = (f32[8]{0:T(128)S(1)}, f32[8]{0:T(128)}, u32[]{:S(2)}) copy-start(f32[8]{0:T(128)} %param.21) | copy-start | bytes 100
  36.7 27.3 %all-to-all-start.1 = ((s16[4,200,512]{2,1,0:T(8,128)(2,1)}), s16[4,200,512]{2,1,0:T(8,128)(2,1)}, u32[]{:S(2)}, u32[]{:S(2)}) async-start(s16[4,200,512]{2,1,0:T(8,128)(2,1)} %pair_flow.1), calls=%async_computation.1 | async-start | bytes 1638400 | tf_op jit(solution)/shard_map/all_to_all | solution.py:495
  107.4 14.5 %all-to-all-start.4 = ((f32[8,8,1024]{2,1,0:T(8,128)}), f32[8,8,1024]{2,1,0:T(8,128)S(1)}, u32[]{:S(2)}, u32[]{:S(2)}) async-start(f32[8,8,1024]{2,1,0:T(8,128)} %bitcast.9), calls=%async_computation.4 | async-start | bytes 524288 | tf_op jit(solution)/shard_map/all_to_all | solution.py:450

commit v9 on v8

--- a/solution.py
+++ b/solution.py
@@ -23,7 +23,7 @@
 CODE = 32000.0
 FINE = 60000.0
 OFFSET = 65536.5
-POOLED = 176
+POOLED = 144
 UPDATED = 128
 VMEM = 20 * 1024 * 1024
 WIDE = 56 * 1024 * 1024
@@ -81,6 +81,23 @@
     tail = jnp.concatenate([both[0:half, 128:SHARE], both[half:, 128:SHARE]], axis=1)
     blank = jnp.zeros((128 - rough_power.shape[0] - fine_power.shape[0], 1), F32)
     return jnp.concatenate([both[:, 0:128], tail], axis=0), jnp.concatenate([rough_power, fine_power, blank], axis=0)
+
+
+def coded_pool(rough, fine):
+    rough_power = powers_of(rough)
+    fine_power = powers_of(fine)
+    scaled = [part * (jnp.exp2(power * -0.125) * CODE) for part, power in ((rough, rough_power), (fine, fine_power))]
+    both = rounded(jnp.concatenate(scaled, axis=0))
+    right = jnp.concatenate([both[48:88, 128:SHARE], jnp.zeros((8, 64), F32)], axis=0)
+    tail = jnp.concatenate([both[0:48, 128:SHARE], right], axis=1)
+    power = jnp.concatenate([rough_power, fine_power, jnp.zeros((40, 1), F32)], axis=0)
+    return jnp.concatenate([both[:, 0:128], tail], axis=0), power
+
+
+def decoded_pool(block, unit):
+    tail = jnp.concatenate([block[88:136, 0:64], block[88:128, 64:128]], axis=0)
+    both = jnp.concatenate([block[0:88], tail], axis=1) * unit[0:88]
+    return both[0:ROWS], both[ROWS:88]
 
 
 def decoded_rows(block, unit, count):
@@ -351,16 +368,17 @@
     blocks = []
     for dest in range(SCEN_AXIS):
         given = jnp.where(last == 0, current[dest : dest + 1, :], jnp.where(last == 1, target[dest : dest + 1, 0:1], 0.0))
-        block, power = coded_rows(
+        block, power = coded_pool(
             pushed[dest * ROWS : dest * ROWS + ROWS, :],
             jnp.concatenate([pooled[dest * 16 : dest * 16 + 16], given], axis=0),
         )
         table = jnp.where(lane == dest, power, table)
-        blocks.append(block)
+        out[dest, 0:128, :] = block[0:128].astype(jnp.int32).astype(jnp.int16)
+        blocks.append(block[128:136])
     table = jnp.transpose(table)
     for dest in range(SCEN_AXIS):
         tail = jnp.broadcast_to(table[dest : dest + 1], (8, 128))
-        out[dest] = jnp.concatenate([blocks[dest], tail], axis=0).astype(jnp.int32).astype(jnp.int16)
+        out[dest, 128:144, :] = jnp.concatenate([blocks[dest], tail], axis=0).astype(jnp.int32).astype(jnp.int16)
 
 
 def excess_sums(received, limit, rows, current, target):
@@ -389,7 +407,7 @@
     pooled = jnp.zeros((16, SHARE), F32)
     given = []
     for src in range(SCEN_AXIS):
-        rough, fine = decoded_rows(from_code(sums[src]), units[:, src : src + 1], 24)
+        rough, fine = decoded_pool(from_code(sums[src]), units[:, src : src + 1])
         pushed = pushed + rough
         pooled = pooled + fine[0:16]
         given.append(fine[16:24])

time: 123 us -> 121 us (0.984)
  blocking collectives: 37.9 us -> 36.3 us
    all_to_all x2, blocking collectives: 37.9 us -> 36.3 us  [exchange(): return lax.all_to_all(tiles, axis, 0, 0, tiled=True)]
where the time goes in v9:
time: 121 us; the launch traced here: 120 us
  blocking collectives  36.3 us (30%)
  waiting for transfers between devices  28.9 us (24%)
  starting transfers between devices  27.7 us (23%)
  Pallas kernels  23.6 us (20%)
  local copies, waits for them, and re-layouts  2.31 us (2%)
    all_to_all x2, blocking collectives, exchange(): return lax.all_to_all(tiles, axis, 0, 0, tiled=True)  36.3 us
    all_to_all x1, waiting for transfers between devices, per_device(): lax.all_to_all(coded, 'bus', 0, 0, axis_index_groups=SAME_PARITY, tiled=T...  20 us
    all_to_all x2, starting transfers between devices, exchange(): return lax.all_to_all(tiles, axis, 0, 0, tiled=True)  15.5 us
    all_to_all x2, waiting for transfers between devices, exchange(): return lax.all_to_all(tiles, axis, 0, 0, tiled=True)  7.42 us
    all_to_all x1, starting transfers between devices, per_device(): lax.all_to_all(coded, 'bus', 0, 0, axis_index_groups=SAME_PARITY, tiled=T...  6.24 us
    pallas_call x1, Pallas kernels, net_flow(): pl.pallas_call(net_flow_kernel, grid=(PAIRS,), in_specs=[pl.BlockSpec(mem...  6.1 us
    pallas_call x1, Pallas kernels, kept_flow(): pl.pallas_call(kept_kernel, grid=(PAIRS,), in_specs=[pl.BlockSpec(memory_...  4.44 us
    pallas_call x1, Pallas kernels, sent_flow(): pl.pallas_call(send_kernel, in_specs=[pl.BlockSpec(memory_space=pltpu.SME...  4.43 us
  transfers between devices with their start and end apart: 5, of which 4 were waited for; matrix products, arithmetic and copies ran while one was open for 2% of the time, Pallas kernels for 9%

profile of v9, /device:TPU:1, one launch (start us, length us, event | category | flops | bytes accessed | tf_op | source)
XLA Modules:
  0.0 120.2 jit_solution(8999429180099588190)
XLA Ops:
  0.6 0.0 copy-start
  0.6 1.4 %units.1 = f32[8,40,128]{2,1,0:T(8,128)} custom-call(s32[8,512]{1,0:T(8,128)} %commitment.1, f32[1,512]{1,0:T(1,128)} %bitcast.16, s32[1,512]{1,0:T(1,128)} %bitcast.17), custom_call_target="tpu_custom_call" | custom-call | tf_op jit(solution)/shard_map/units/pallas_call | solution.py:130
  2.1 7.6 %all-to-all-start = ((f32[8,40,128]{2,1,0:T(8,128)}), f32[8,40,128]{2,1,0:T(8,128)S(1)}, u32[]{:S(2)}, u32[]{:S(2)}) async-start(f32[8,40,128]{2,1,0:T(8,128)} %units.1), calls=%async_computation | async-start | bytes 327680 | tf_op jit(solution)/shard_map/all_to_all | solution.py:468
  9.7 0.0 copy-start.5
  9.7 0.0 copy-start.3
  9.7 0.0 copy-start.2
  9.7 0.0 copy-start.1
  9.8 6.1 %net_flow.1 = (f32[768,512]{1,0:T(8,128)}, f32[768,512]{1,0:T(8,128)}, f32[4,8,192]{2,1,0:T(8,128)}) custom-call(s32[1]{0:T(128)} %bitcast.3.parity, bf16[1536,1024]{1,0:T(8,128)(2,1)} %factors.7, bf16[512,1024]{1,0:T(8,128)(2,1)} %bitcast.13), custom_call_target="tpu_custom_call" | custom-call | tf_op jit(solution)/shard_map/net_flow/pallas_call | solution.py:148
  15.9 0.0 copy-done.5
  15.9 0.1 broadcast_in_dim.10
  15.9 0.1 stack_reshape.11
  16.0 0.0 copy-done.3
  16.1 0.1 broadcast_in_dim.9
  16.1 0.1 stack_reshape.10
  16.2 0.0 copy-done.2
  16.2 0.1 copy.16
  16.3 0.1 stack_reshape.9
  16.4 1.7 %all-to-all-done.units = f32[8,40,128]{2,1,0:T(8,128)S(1)} async-done(((f32[8,40,128]{2,1,0:T(8,128)}), f32[8,40,128]{2,1,0:T(8,128)S(1)}, u32[]{:S(2)}, u32[]{:S(2)}) %all-to-all-start) | async-done | bytes 163872 | tf_op jit(solution)/shard_map/all_to_all | solution.py:468
  18.1 0.0 copy-done.1
  18.1 4.4 %sent_flow.1 = (f32[16,1024]{1,0:T(8,128)S(1)}, s16[392,512]{1,0:T(8,128)(2,1)S(1)}, s16[392,512]{1,0:T(8,128)(2,1)S(1)}) custom-call(s32[1]{0:T(128)} %bitcast.place, f32[8,40,128]{2,1,0:T(8,128)S(1)} %all-to-all-done.units, bf16[1536,1024]{1,0:T(8,128)(2,1)S(1)} %copy-done.1, f32[3,512]{1,0:T(4,128)S(1)} %pad_maximum_fusion.level.rows, ...), custom_call_target="tpu_custom_call" | custom-call | tf_op jit(solution)/shard_map/sent_flow/pallas_call | solution.py:238
  22.5 2.1 %collective-permute-start = (s16[392,512]{1,0:T(8,128)(2,1)S(1)}, s16[392,512]{1,0:T(8,128)(2,1)S(1)}, u32[]{:S(2)}, u32[]{:S(2)}) collective-permute-start(s16[392,512]{1,0:T(8,128)(2,1)S(1)} %get-tuple-element.26), channel_id=1, source_target_pairs={{0,64},{64,0},{128,192},{192,128},{256,320},{320,256},{384,448},{4... | collective-permute-start | bytes 1204232 | tf_op jit(solution)/shard_map/ppermute | solution.py:509
  24.6 3.9 %collective-permute-start.1 = (s16[392,512]{1,0:T(8,128)(2,1)S(1)}, s16[392,512]{1,0:T(8,128)(2,1)S(1)}, u32[]{:S(2)}, u32[]{:S(2)}) collective-permute-start(s16[392,512]{1,0:T(8,128)(2,1)S(1)} %get-tuple-element.27), channel_id=1, source_target_pairs={{0,448},{64,128},{128,64},{192,256},{256,192},{320,384},{384,320},... | collective-permute-start | bytes 1204232 | tf_op jit(solution)/shard_map/ppermute | solution.py:510
  28.5 4.4 %kept_flow.1 = (f32[768,512]{1,0:T(8,128)S(1)}, f32[4,8,192]{2,1,0:T(8,128)S(1)}) custom-call(s32[1]{0:T(128)} %bitcast.place, f32[16,1024]{1,0:T(8,128)S(1)} %get-tuple-element.22.capacity, bf16[1536,1024]{1,0:T(8,128)(2,1)S(1)} %copy-done.1, f32[768,512]{1,0:T(8,128)} %get-tuple-element.23.net, f32[3,512]{1,0:T(4,128)S(1)} %pad_maximum_fusion.level.rows), custom_call_target="tpu_custom_call" | custom-call | tf_op jit(solution)/shard_map/kept_flow/pallas_call | solution.py:266
  33.0 0.0 collective-permute-done.code_a.power_a
  33.0 1.5 %collective-permute-done.1.code_b.power_b = s16[392,512]{1,0:T(8,128)(2,1)S(1)} collective-permute-done((s16[392,512]{1,0:T(8,128)(2,1)S(1)}, s16[392,512]{1,0:T(8,128)(2,1)S(1)}, u32[]{:S(2)}, u32[]{:S(2)}) %collective-permute-start.1) | collective-permute-done | bytes 401440 | tf_op jit(solution)/shard_map/ppermute | solution.py:510
  34.5 2.2 %pair_flow.1 = s16[4,200,512]{2,1,0:T(8,128)(2,1)} custom-call(f32[768,512]{1,0:T(8,128)S(1)} %get-tuple-element.24.part, f32[4,8,192]{2,1,0:T(8,128)S(1)} %get-tuple-element.25.top, s16[392,512]{1,0:T(8,128)(2,1)S(1)} %collective-permute-done.code_a.power_a, s16[392,512]{1,0:T(8,128)(2,1)S(1)} %collective-permute-done.1.code_b.power_b, ...), custom_call_target="tpu_custom_call" | custom-call | tf_op jit(solution)/shard_map/pair_flow/pallas_call | solution.py:309
  36.7 0.0 copy-start.4
  36.7 6.2 %all-to-all-start.1 = ((s16[4,200,512]{2,1,0:T(8,128)(2,1)}), s16[4,200,512]{2,1,0:T(8,128)(2,1)}, u32[]{:S(2)}, u32[]{:S(2)}) async-start(s16[4,200,512]{2,1,0:T(8,128)(2,1)} %pair_flow.1), calls=%async_computation.1 | async-start | bytes 1638400 | tf_op jit(solution)/shard_map/all_to_all | solution.py:513
  42.9 0.8 dynamic_slice.6
  43.7 0.1 copy.17.limit
  43.8 0.0 copy-done.4
  43.8 0.1 copy.18.target
  43.9 0.0 copy-done
  43.9 0.1 constant_dynamic-slice_fusion.current
  44.0 20.0 %all-to-all-done.1.received = s16[4,200,512]{2,1,0:T(8,128)(2,1)} async-done(((s16[4,200,512]{2,1,0:T(8,128)(2,1)}), s16[4,200,512]{2,1,0:T(8,128)(2,1)}, u32[]{:S(2)}, u32[]{:S(2)}) %all-to-all-start.1) | async-done | bytes 819232 | tf_op jit(solution)/shard_map/all_to_all | solution.py:513
  64.0 2.9 %excess_sums.1 = s16[8,144,128]{2,1,0:T(8,128)(2,1)S(1)} custom-call(s16[4,200,512]{2,1,0:T(8,128)(2,1)} %all-to-all-done.1.received, f32[192,1]{1,0:T(8,128)S(1)} %copy.17.limit, f32[3,512]{1,0:T(4,128)S(1)} %pad_maximum_fusion.level.rows, f32[8,192]{1,0:T(8,128)S(1)} %constant_dynamic-slice_fusion.current, f32[8,1]{1,0:T(8,128)S(1)} %copy.18.target), custom_call_target="tpu_custom_call" | custom-call | tf_op jit(solution)/shard_map/excess_sums/pallas_call | solution.py:385
  66.9 22.2 %all_to_all.25.sums = s16[8,144,128]{2,1,0:T(8,128)(2,1)S(1)} all-to-all(s16[8,144,128]{2,1,0:T(8,128)(2,1)S(1)} %excess_sums.1), channel_id=1, replica_groups=mesh['bus'=8,'line'=8,'scen'=8] {'scen'}, dimensions={0} | all-to-all | bytes 589824 | tf_op jit(solution)/shard_map/all_to_all | solution.py:468
  89.1 0.6 update.1
  89.7 14.1 %all_to_all.26.packed = s16[8,128,128]{2,1,0:T(8,128)(2,1)S(1)} all-to-all(s16[8,128,128]{2,1,0:T(8,128)(2,1)S(1)} %update.1), channel_id=1, replica_groups=mesh['bus'=8,'line'=8,'scen'=8] {'bus'}, dimensions={0} | all-to-all | bytes 524288 | tf_op jit(solution)/shard_map/all_to_all | solution.py:468
  103.8 1.5 %slopes.1 = (f32[64,1024]{1,0:T(8,128)}, f32[8,8,192]{2,1,0:T(8,128)S(1)}) custom-call(s16[8,128,128]{2,1,0:T(8,128)(2,1)S(1)} %all_to_all.26.packed, bf16[1536,1024]{1,0:T(8,128)(2,1)S(1)} %copy-done.1), custom_call_target="tpu_custom_call" | custom-call | tf_op jit(solution)/shard_map/slopes/pallas_call | solution.py:449
  105.3 7.8 %all-to-all-start.4 = ((f32[8,8,1024]{2,1,0:T(8,128)}), f32[8,8,1024]{2,1,0:T(8,128)S(1)}, u32[]{:S(2)}, u32[]{:S(2)}) async-start(f32[8,8,1024]{2,1,0:T(8,128)} %bitcast.9), calls=%async_computation.4 | async-start | bytes 524288 | tf_op jit(solution)/shard_map/all_to_all | solution.py:468
  113.2 0.7 reshape.40
  113.9 5.7 %all-to-all-done.4 = f32[8,8,1024]{2,1,0:T(8,128)S(1)} async-done(((f32[8,8,1024]{2,1,0:T(8,128)}), f32[8,8,1024]{2,1,0:T(8,128)S(1)}, u32[]{:S(2)}, u32[]{:S(2)}) %all-to-all-start.4) | async-done | bytes 262176 | tf_op jit(solution)/shard_map/all_to_all | solution.py:468
  119.6 0.6 reduce_sum.9
  (3 shorter events, 0.0 us)
Async XLA Ops:
  0.6 43.3 %copy-start = (f32[8,1536]{1,0:T(8,128)S(1)}, f32[8,1536]{1,0:T(8,128)}, u32[]{:S(2)}) copy-start(f32[8,1536]{1,0:T(8,128)} %param.20) | copy-start | bytes 147460
  2.1 16.0 %all-to-all-start = ((f32[8,40,128]{2,1,0:T(8,128)}), f32[8,40,128]{2,1,0:T(8,128)S(1)}, u32[]{:S(2)}, u32[]{:S(2)}) async-start(f32[8,40,128]{2,1,0:T(8,128)} %units.1), calls=%async_computation | async-start | bytes 327680 | tf_op jit(solution)/shard_map/all_to_all | solution.py:468
  9.7 6.1 %copy-start.5 = (s32[64,1]{0,1:T(1,128)S(1)}, s32[64,1]{0,1:T(1,128)}, u32[]{:S(2)}) copy-start(s32[64,1]{0,1:T(1,128)} %param.15) | copy-start | bytes 772
  9.7 6.3 %copy-start.3 = (f32[64]{0:T(128)S(1)}, f32[64]{0:T(128)}, u32[]{:S(2)}) copy-start(f32[64]{0:T(128)} %param.14) | copy-start | bytes 772
  9.7 6.5 %copy-start.2 = (f32[64,8]{0,1:T(8,128)S(1)}, f32[64,8]{0,1:T(8,128)}, u32[]{:S(2)}) copy-start(f32[64,8]{0,1:T(8,128)} %param.13) | copy-start | bytes 6148
  9.7 8.4 %copy-start.1 = (bf16[1536,1024]{1,0:T(8,128)(2,1)S(1)}, bf16[1536,1024]{1,0:T(8,128)(2,1)}, u32[]{:S(2)}) copy-start(bf16[1536,1024]{1,0:T(8,128)(2,1)} %factors.7) | copy-start | bytes 9437188
  22.5 10.5 %collective-permute-start = (s16[392,512]{1,0:T(8,128)(2,1)S(1)}, s16[392,512]{1,0:T(8,128)(2,1)S(1)}, u32[]{:S(2)}, u32[]{:S(2)}) collective-permute-start(s16[392,512]{1,0:T(8,128)(2,1)S(1)} %get-tuple-element.26), channel_id=1, source_target_pairs={{0,64},{64,0},{128,192},{192,128},{256,320},{320,256},{384,448},{4... | collective-permute-start | bytes 1204232 | tf_op jit(solution)/shard_map/ppermute | solution.py:509
  24.6 9.8 %collective-permute-start.1 = (s16[392,512]{1,0:T(8,128)(2,1)S(1)}, s16[392,512]{1,0:T(8,128)(2,1)S(1)}, u32[]{:S(2)}, u32[]{:S(2)}) collective-permute-start(s16[392,512]{1,0:T(8,128)(2,1)S(1)} %get-tuple-element.27), channel_id=1, source_target_pairs={{0,448},{64,128},{128,64},{192,256},{256,192},{320,384},{384,320},... | collective-permute-start | bytes 1204232 | tf_op jit(solution)/shard_map/ppermute | solution.py:510
  36.7 7.1 %copy-start.4 = (f32[8]{0:T(128)S(1)}, f32[8]{0:T(128)}, u32[]{:S(2)}) copy-start(f32[8]{0:T(128)} %param.21) | copy-start | bytes 100
  36.7 27.3 %all-to-all-start.1 = ((s16[4,200,512]{2,1,0:T(8,128)(2,1)}), s16[4,200,512]{2,1,0:T(8,128)(2,1)}, u32[]{:S(2)}, u32[]{:S(2)}) async-start(s16[4,200,512]{2,1,0:T(8,128)(2,1)} %pair_flow.1), calls=%async_computation.1 | async-start | bytes 1638400 | tf_op jit(solution)/shard_map/all_to_all | solution.py:513
  105.3 14.3 %all-to-all-start.4 = ((f32[8,8,1024]{2,1,0:T(8,128)}), f32[8,8,1024]{2,1,0:T(8,128)S(1)}, u32[]{:S(2)}, u32[]{:S(2)}) async-start(f32[8,8,1024]{2,1,0:T(8,128)} %bitcast.9), calls=%async_computation.4 | async-start | bytes 524288 | tf_op jit(solution)/shard_map/all_to_all | solution.py:468

commit v10 on v9

--- a/solution.py
+++ b/solution.py
@@ -284,40 +284,43 @@
 
 
 def pair_kernel(part, top, code_a, code_b, power_a, power_b, coded):
-    here = lax.broadcasted_iota(jnp.int32, (8, 256), 0) == pl.program_id(0)
     lane = lax.broadcasted_iota(jnp.int32, (1, 256), 1)
-    rows = [
-        jnp.sum(jnp.where(here, from_code(power[:, 0:256]), 0.0), axis=0, keepdims=True) for power in (power_a, power_b)
-    ]
-    unit = unit_of(jnp.where(lane < HALF, rows[0], rows[1]))[:, 0:SHARE]
-    power = power_of(top[0, 0:1, :] + unit * CODE)
-    again = jnp.exp2(power * -0.125) * CODE
-    scales = [jnp.broadcast_to(scale, (8, SHARE)) for scale in (unit * again, again)]
-    scales = jnp.transpose(jnp.concatenate(scales, axis=0))
-    for index, code in enumerate((code_a, code_b)):
-        for start in range(0, HALF, 32):
-            some = slice(index * HALF + start, index * HALF + start + 32)
-            value = part[some, :] * scales[some, 8:9] + OFFSET
-            coded[0, some, :] = wrapped(value + from_code(code[start : start + 32, :]) * scales[some, 0:1])
-    across = jnp.concatenate([jnp.broadcast_to(power, (8, SHARE)), jnp.zeros((8, COLS - SHARE), F32)], axis=1)
-    coded[0, SHARE : SHARE + 8, :] = across.astype(jnp.int32).astype(jnp.int16)
+    for owner in range(2):
+        here = lax.broadcasted_iota(jnp.int32, (8, 256), 0) == 2 * pl.program_id(0) + owner
+        rows = [
+            jnp.sum(jnp.where(here, from_code(power[:, 0:256]), 0.0), axis=0, keepdims=True)
+            for power in (power_a, power_b)
+        ]
+        unit = unit_of(jnp.where(lane < HALF, rows[0], rows[1]))[:, 0:SHARE]
+        power = power_of(top[owner, 0:1, :] + unit * CODE)
+        again = jnp.exp2(power * -0.125) * CODE
+        scales = [jnp.broadcast_to(scale, (8, SHARE)) for scale in (unit * again, again)]
+        scales = jnp.transpose(jnp.concatenate(scales, axis=0))
+        for index, code in enumerate((code_a, code_b)):
+            for start in range(0, HALF, 32):
+                some = slice(index * HALF + start, index * HALF + start + 32)
+                value = part[owner * SHARE + some.start : owner * SHARE + some.stop, :] * scales[some, 8:9] + OFFSET
+                piece = from_code(code[owner * HALF + start : owner * HALF + start + 32, :])
+                coded[owner, some, :] = wrapped(value + piece * scales[some, 0:1])
+        across = jnp.concatenate([jnp.broadcast_to(power, (8, SHARE)), jnp.zeros((8, COLS - SHARE), F32)], axis=1)
+        coded[owner, SHARE : SHARE + 8, :] = across.astype(jnp.int32).astype(jnp.int16)
 
 
 def pair_flow(part, top, code_a, code_b):
-    lines = pl.BlockSpec((HALF, COLS), lambda j: (j, 0))
+    lines = pl.BlockSpec((2 * HALF, COLS), lambda j: (j, 0))
     tail = pl.BlockSpec((8, COLS), lambda j: (PAIRS * HALF // 8, 0))
     return pl.pallas_call(
         pair_kernel,
-        grid=(PAIRS,),
+        grid=(PAIRS // 2,),
         in_specs=[
-            pl.BlockSpec((SHARE, COLS), lambda j: (j, 0)),
-            pl.BlockSpec((1, 8, SHARE), lambda j: (j, 0, 0)),
+            pl.BlockSpec((2 * SHARE, COLS), lambda j: (j, 0)),
+            pl.BlockSpec((2, 8, SHARE), lambda j: (j, 0, 0)),
             lines,
             lines,
             tail,
             tail,
         ],
-        out_specs=pl.BlockSpec((1, SHARE + 8, COLS), lambda j: (j, 0, 0)),
+        out_specs=pl.BlockSpec((2, SHARE + 8, COLS), lambda j: (j, 0, 0)),
         out_shape=pltpu.HBM((PAIRS, SHARE + 8, COLS), jnp.int16),
         compiler_params=pltpu.CompilerParams(vmem_limit_bytes=VMEM),
         name="pair_flow",

time: 121 us -> 120 us (level)
  no operation moved by 1% of the time
where the time goes in v10:
time: 120 us
  blocking collectives  36.3 us (30%)
  waiting for transfers between devices  28.9 us (24%)
  starting transfers between devices  27.7 us (23%)
  Pallas kernels  23 us (19%)
  local copies, waits for them, and re-layouts  2.31 us (2%)
    all_to_all x2, blocking collectives, exchange(): return lax.all_to_all(tiles, axis, 0, 0, tiled=True)  36.3 us
    all_to_all x1, waiting for transfers between devices, per_device(): lax.all_to_all(coded, 'bus', 0, 0, axis_index_groups=SAME_PARITY, tiled=T...  20 us
    all_to_all x2, starting transfers between devices, exchange(): return lax.all_to_all(tiles, axis, 0, 0, tiled=True)  15.5 us
    all_to_all x2, waiting for transfers between devices, exchange(): return lax.all_to_all(tiles, axis, 0, 0, tiled=True)  7.42 us
    all_to_all x1, starting transfers between devices, per_device(): lax.all_to_all(coded, 'bus', 0, 0, axis_index_groups=SAME_PARITY, tiled=T...  6.24 us
    pallas_call x1, Pallas kernels, net_flow(): pl.pallas_call(net_flow_kernel, grid=(PAIRS,), in_specs=[pl.BlockSpec(mem...  6.1 us
    pallas_call x1, Pallas kernels, kept_flow(): pl.pallas_call(kept_kernel, grid=(PAIRS,), in_specs=[pl.BlockSpec(memory_...  4.44 us
    pallas_call x1, Pallas kernels, sent_flow(): pl.pallas_call(send_kernel, in_specs=[pl.BlockSpec(memory_space=pltpu.SME...  4.43 us
  transfers between devices with their start and end apart: 5, of which 4 were waited for; matrix products, arithmetic and copies ran while one was open for 2% of the time, Pallas kernels for 9%

profile of v10, /device:TPU:1, one launch (start us, length us, event | category | flops | bytes accessed | tf_op | source)
XLA Modules:
  0.0 119.6 jit_solution(1949073065348147244)
XLA Ops:
  0.6 0.0 copy-start
  0.6 1.4 %units.1 = f32[8,40,128]{2,1,0:T(8,128)} custom-call(s32[8,512]{1,0:T(8,128)} %commitment.1, f32[1,512]{1,0:T(1,128)} %bitcast.16, s32[1,512]{1,0:T(1,128)} %bitcast.17), custom_call_target="tpu_custom_call" | custom-call | tf_op jit(solution)/shard_map/units/pallas_call | solution.py:130
  2.1 7.6 %all-to-all-start = ((f32[8,40,128]{2,1,0:T(8,128)}), f32[8,40,128]{2,1,0:T(8,128)S(1)}, u32[]{:S(2)}, u32[]{:S(2)}) async-start(f32[8,40,128]{2,1,0:T(8,128)} %units.1), calls=%async_computation | async-start | bytes 327680 | tf_op jit(solution)/shard_map/all_to_all | solution.py:471
  9.7 0.0 copy-start.5
  9.7 0.0 copy-start.3
  9.7 0.0 copy-start.2
  9.7 0.0 copy-start.1
  9.8 6.1 %net_flow.1 = (f32[768,512]{1,0:T(8,128)}, f32[768,512]{1,0:T(8,128)}, f32[4,8,192]{2,1,0:T(8,128)}) custom-call(s32[1]{0:T(128)} %bitcast.3.parity, bf16[1536,1024]{1,0:T(8,128)(2,1)} %factors.7, bf16[512,1024]{1,0:T(8,128)(2,1)} %bitcast.13), custom_call_target="tpu_custom_call" | custom-call | tf_op jit(solution)/shard_map/net_flow/pallas_call | solution.py:148
  15.9 0.0 copy-done.5
  15.9 0.1 broadcast_in_dim.10
  15.9 0.1 stack_reshape.11
  16.0 0.0 copy-done.3
  16.1 0.1 broadcast_in_dim.9
  16.1 0.1 stack_reshape.10
  16.2 0.0 copy-done.2
  16.2 0.1 copy.16
  16.3 0.1 stack_reshape.9
  16.4 1.7 %all-to-all-done.units = f32[8,40,128]{2,1,0:T(8,128)S(1)} async-done(((f32[8,40,128]{2,1,0:T(8,128)}), f32[8,40,128]{2,1,0:T(8,128)S(1)}, u32[]{:S(2)}, u32[]{:S(2)}) %all-to-all-start) | async-done | bytes 163872 | tf_op jit(solution)/shard_map/all_to_all | solution.py:471
  18.1 0.0 copy-done.1
  18.1 4.4 %sent_flow.1 = (f32[16,1024]{1,0:T(8,128)S(1)}, s16[392,512]{1,0:T(8,128)(2,1)S(1)}, s16[392,512]{1,0:T(8,128)(2,1)S(1)}) custom-call(s32[1]{0:T(128)} %bitcast.place, f32[8,40,128]{2,1,0:T(8,128)S(1)} %all-to-all-done.units, bf16[1536,1024]{1,0:T(8,128)(2,1)S(1)} %copy-done.1, f32[3,512]{1,0:T(4,128)S(1)} %pad_maximum_fusion.level.rows, ...), custom_call_target="tpu_custom_call" | custom-call | tf_op jit(solution)/shard_map/sent_flow/pallas_call | solution.py:238
  22.5 2.1 %collective-permute-start = (s16[392,512]{1,0:T(8,128)(2,1)S(1)}, s16[392,512]{1,0:T(8,128)(2,1)S(1)}, u32[]{:S(2)}, u32[]{:S(2)}) collective-permute-start(s16[392,512]{1,0:T(8,128)(2,1)S(1)} %get-tuple-element.26), channel_id=1, source_target_pairs={{0,64},{64,0},{128,192},{192,128},{256,320},{320,256},{384,448},{4... | collective-permute-start | bytes 1204232 | tf_op jit(solution)/shard_map/ppermute | solution.py:512
  24.6 3.9 %collective-permute-start.1 = (s16[392,512]{1,0:T(8,128)(2,1)S(1)}, s16[392,512]{1,0:T(8,128)(2,1)S(1)}, u32[]{:S(2)}, u32[]{:S(2)}) collective-permute-start(s16[392,512]{1,0:T(8,128)(2,1)S(1)} %get-tuple-element.27), channel_id=1, source_target_pairs={{0,448},{64,128},{128,64},{192,256},{256,192},{320,384},{384,320},... | collective-permute-start | bytes 1204232 | tf_op jit(solution)/shard_map/ppermute | solution.py:513
  28.5 4.4 %kept_flow.1 = (f32[768,512]{1,0:T(8,128)S(1)}, f32[4,8,192]{2,1,0:T(8,128)S(1)}) custom-call(s32[1]{0:T(128)} %bitcast.place, f32[16,1024]{1,0:T(8,128)S(1)} %get-tuple-element.22.capacity, bf16[1536,1024]{1,0:T(8,128)(2,1)S(1)} %copy-done.1, f32[768,512]{1,0:T(8,128)} %get-tuple-element.23.net, f32[3,512]{1,0:T(4,128)S(1)} %pad_maximum_fusion.level.rows), custom_call_target="tpu_custom_call" | custom-call | tf_op jit(solution)/shard_map/kept_flow/pallas_call | solution.py:266
  33.0 0.0 collective-permute-done.code_a.power_a
  33.0 1.5 %collective-permute-done.1.code_b.power_b = s16[392,512]{1,0:T(8,128)(2,1)S(1)} collective-permute-done((s16[392,512]{1,0:T(8,128)(2,1)S(1)}, s16[392,512]{1,0:T(8,128)(2,1)S(1)}, u32[]{:S(2)}, u32[]{:S(2)}) %collective-permute-start.1) | collective-permute-done | bytes 401440 | tf_op jit(solution)/shard_map/ppermute | solution.py:513
  34.5 1.6 %pair_flow.1 = s16[4,200,512]{2,1,0:T(8,128)(2,1)} custom-call(f32[768,512]{1,0:T(8,128)S(1)} %get-tuple-element.24.part, f32[4,8,192]{2,1,0:T(8,128)S(1)} %get-tuple-element.25.top, s16[392,512]{1,0:T(8,128)(2,1)S(1)} %collective-permute-done.code_a.power_a, s16[392,512]{1,0:T(8,128)(2,1)S(1)} %collective-permute-done.1.code_b.power_b, ...), custom_call_target="tpu_custom_call" | custom-call | tf_op jit(solution)/shard_map/pair_flow/pallas_call | solution.py:312
  36.1 0.0 copy-start.4
  36.1 6.2 %all-to-all-start.1 = ((s16[4,200,512]{2,1,0:T(8,128)(2,1)}), s16[4,200,512]{2,1,0:T(8,128)(2,1)}, u32[]{:S(2)}, u32[]{:S(2)}) async-start(s16[4,200,512]{2,1,0:T(8,128)(2,1)} %pair_flow.1), calls=%async_computation.1 | async-start | bytes 1638400 | tf_op jit(solution)/shard_map/all_to_all | solution.py:516
  42.3 0.8 dynamic_slice.6
  43.1 0.1 copy.17.limit
  43.2 0.0 copy-done.4
  43.2 0.1 copy.18.target
  43.3 0.0 copy-done
  43.3 0.1 constant_dynamic-slice_fusion.current
  43.4 20.0 %all-to-all-done.1.received = s16[4,200,512]{2,1,0:T(8,128)(2,1)} async-done(((s16[4,200,512]{2,1,0:T(8,128)(2,1)}), s16[4,200,512]{2,1,0:T(8,128)(2,1)}, u32[]{:S(2)}, u32[]{:S(2)}) %all-to-all-start.1) | async-done | bytes 819232 | tf_op jit(solution)/shard_map/all_to_all | solution.py:516
  63.4 2.9 %excess_sums.1 = s16[8,144,128]{2,1,0:T(8,128)(2,1)S(1)} custom-call(s16[4,200,512]{2,1,0:T(8,128)(2,1)} %all-to-all-done.1.received, f32[192,1]{1,0:T(8,128)S(1)} %copy.17.limit, f32[3,512]{1,0:T(4,128)S(1)} %pad_maximum_fusion.level.rows, f32[8,192]{1,0:T(8,128)S(1)} %constant_dynamic-slice_fusion.current, f32[8,1]{1,0:T(8,128)S(1)} %copy.18.target), custom_call_target="tpu_custom_call" | custom-call | tf_op jit(solution)/shard_map/excess_sums/pallas_call | solution.py:388
  66.3 22.2 %all_to_all.25.sums = s16[8,144,128]{2,1,0:T(8,128)(2,1)S(1)} all-to-all(s16[8,144,128]{2,1,0:T(8,128)(2,1)S(1)} %excess_sums.1), channel_id=1, replica_groups=mesh['bus'=8,'line'=8,'scen'=8] {'scen'}, dimensions={0} | all-to-all | bytes 589824 | tf_op jit(solution)/shard_map/all_to_all | solution.py:471
  88.5 0.6 update.1
  89.1 14.1 %all_to_all.26.packed = s16[8,128,128]{2,1,0:T(8,128)(2,1)S(1)} all-to-all(s16[8,128,128]{2,1,0:T(8,128)(2,1)S(1)} %update.1), channel_id=1, replica_groups=mesh['bus'=8,'line'=8,'scen'=8] {'bus'}, dimensions={0} | all-to-all | bytes 524288 | tf_op jit(solution)/shard_map/all_to_all | solution.py:471
  103.2 1.5 %slopes.1 = (f32[64,1024]{1,0:T(8,128)}, f32[8,8,192]{2,1,0:T(8,128)S(1)}) custom-call(s16[8,128,128]{2,1,0:T(8,128)(2,1)S(1)} %all_to_all.26.packed, bf16[1536,1024]{1,0:T(8,128)(2,1)S(1)} %copy-done.1), custom_call_target="tpu_custom_call" | custom-call | tf_op jit(solution)/shard_map/slopes/pallas_call | solution.py:452
  104.7 7.8 %all-to-all-start.4 = ((f32[8,8,1024]{2,1,0:T(8,128)}), f32[8,8,1024]{2,1,0:T(8,128)S(1)}, u32[]{:S(2)}, u32[]{:S(2)}) async-start(f32[8,8,1024]{2,1,0:T(8,128)} %bitcast.9), calls=%async_computation.4 | async-start | bytes 524288 | tf_op jit(solution)/shard_map/all_to_all | solution.py:471
  112.6 0.7 reshape.40
  113.3 5.7 %all-to-all-done.4 = f32[8,8,1024]{2,1,0:T(8,128)S(1)} async-done(((f32[8,8,1024]{2,1,0:T(8,128)}), f32[8,8,1024]{2,1,0:T(8,128)S(1)}, u32[]{:S(2)}, u32[]{:S(2)}) %all-to-all-start.4) | async-done | bytes 262176 | tf_op jit(solution)/shard_map/all_to_all | solution.py:471
  119.0 0.6 reduce_sum.9
  (3 shorter events, 0.0 us)
Async XLA Ops:
  0.6 42.7 %copy-start = (f32[8,1536]{1,0:T(8,128)S(1)}, f32[8,1536]{1,0:T(8,128)}, u32[]{:S(2)}) copy-start(f32[8,1536]{1,0:T(8,128)} %param.20) | copy-start | bytes 147460
  2.1 16.0 %all-to-all-start = ((f32[8,40,128]{2,1,0:T(8,128)}), f32[8,40,128]{2,1,0:T(8,128)S(1)}, u32[]{:S(2)}, u32[]{:S(2)}) async-start(f32[8,40,128]{2,1,0:T(8,128)} %units.1), calls=%async_computation | async-start | bytes 327680 | tf_op jit(solution)/shard_map/all_to_all | solution.py:471
  9.7 6.1 %copy-start.5 = (s32[64,1]{0,1:T(1,128)S(1)}, s32[64,1]{0,1:T(1,128)}, u32[]{:S(2)}) copy-start(s32[64,1]{0,1:T(1,128)} %param.15) | copy-start | bytes 772
  9.7 6.3 %copy-start.3 = (f32[64]{0:T(128)S(1)}, f32[64]{0:T(128)}, u32[]{:S(2)}) copy-start(f32[64]{0:T(128)} %param.14) | copy-start | bytes 772
  9.7 6.5 %copy-start.2 = (f32[64,8]{0,1:T(8,128)S(1)}, f32[64,8]{0,1:T(8,128)}, u32[]{:S(2)}) copy-start(f32[64,8]{0,1:T(8,128)} %param.13) | copy-start | bytes 6148
  9.7 8.4 %copy-start.1 = (bf16[1536,1024]{1,0:T(8,128)(2,1)S(1)}, bf16[1536,1024]{1,0:T(8,128)(2,1)}, u32[]{:S(2)}) copy-start(bf16[1536,1024]{1,0:T(8,128)(2,1)} %factors.7) | copy-start | bytes 9437188
  22.5 10.5 %collective-permute-start = (s16[392,512]{1,0:T(8,128)(2,1)S(1)}, s16[392,512]{1,0:T(8,128)(2,1)S(1)}, u32[]{:S(2)}, u32[]{:S(2)}) collective-permute-start(s16[392,512]{1,0:T(8,128)(2,1)S(1)} %get-tuple-element.26), channel_id=1, source_target_pairs={{0,64},{64,0},{128,192},{192,128},{256,320},{320,256},{384,448},{4... | collective-permute-start | bytes 1204232 | tf_op jit(solution)/shard_map/ppermute | solution.py:512
  24.6 9.8 %collective-permute-start.1 = (s16[392,512]{1,0:T(8,128)(2,1)S(1)}, s16[392,512]{1,0:T(8,128)(2,1)S(1)}, u32[]{:S(2)}, u32[]{:S(2)}) collective-permute-start(s16[392,512]{1,0:T(8,128)(2,1)S(1)} %get-tuple-element.27), channel_id=1, source_target_pairs={{0,448},{64,128},{128,64},{192,256},{256,192},{320,384},{384,320},... | collective-permute-start | bytes 1204232 | tf_op jit(solution)/shard_map/ppermute | solution.py:513
  36.1 7.1 %copy-start.4 = (f32[8]{0:T(128)S(1)}, f32[8]{0:T(128)}, u32[]{:S(2)}) copy-start(f32[8]{0:T(128)} %param.21) | copy-start | bytes 100
  36.1 27.3 %all-to-all-start.1 = ((s16[4,200,512]{2,1,0:T(8,128)(2,1)}), s16[4,200,512]{2,1,0:T(8,128)(2,1)}, u32[]{:S(2)}, u32[]{:S(2)}) async-start(s16[4,200,512]{2,1,0:T(8,128)(2,1)} %pair_flow.1), calls=%async_computation.1 | async-start | bytes 1638400 | tf_op jit(solution)/shard_map/all_to_all | solution.py:516
  104.7 14.3 %all-to-all-start.4 = ((f32[8,8,1024]{2,1,0:T(8,128)}), f32[8,8,1024]{2,1,0:T(8,128)S(1)}, u32[]{:S(2)}, u32[]{:S(2)}) async-start(f32[8,8,1024]{2,1,0:T(8,128)} %bitcast.9), calls=%async_computation.4 | async-start | bytes 524288 | tf_op jit(solution)/shard_map/all_to_all | solution.py:471
